TPU v7x, 32 devices: a whole 2x2x4 slice. The times are simulated.
32 devices in a mesh: bx: 4 (over y, core), by: 8 (over z, x).
Axes of the slice: x: 2, y: 2, z: 4, core: 2. Of those that a mesh axis runs over, the one named last changes fastest.
Arguments:
- h_old: float32 [20, 256, 1024], P(None, 'bx', 'by'), may hold values from -3 to 0.5
- soil_type: int32 [20, 256, 1024], P(None, 'bx', 'by'), may hold values from 0 to 11
- ks_scale: float32 [20, 256, 1024], P(None, 'bx', 'by'), may hold values from 0.3 to 3
- soil_table: float32 [4, 12], replicated, may hold values from 0.2 to 1
- clump_brick: int32 [262144], P(('bx', 'by')), may hold values from -1 to 31, as said below
- clump_cell: int32 [262144], P(('bx', 'by')), may hold values from -1 to 8191, as said below
- root_fraction: float32 [14, 262144], P(None, ('bx', 'by')), may hold values from 0.05 to 0.3
- transpiration: float32 [262144], P(('bx', 'by')), may hold values from 0.2 to 2
- infiltration: float32 [262144], P(('bx', 'by')), may hold values from 0.2 to 2
Outputs:
- pressure: float32 [20, 256, 1024], P(None, 'bx', 'by')
- stress: float32 [262144], P(('bx', 'by'))
Inputs may be any that keep to these rules, and one draw needn't show every extreme that they name: `clump_brick`: A brick is the 64 x 128 columns with i // 64 and j // 128 fixed, numbered (i // 64) * 8 + j // 128. The slots of one device are the 8192 consecutive entries of its shard; its slots b * 256 to (b + 1) * 256 - 1 hold columns of brick b or are empty, and there the entry is b; -1 marks an empty slot (exactly where clump_cell is -1). `clump_cell`: A slot's entry is the position (i % 64) * 128 + j % 128 of its column within its brick, or -1 when empty; no column is held twice. In every draw one brick has all its columns held, all 256 of its slots filled on every device.
All inputs are finite; a program needn't handle non-finite values.
Results may differ from a plain program's by a relative error of at most 0.000068.
Values sent between devices are 32-bit elements; how exact they have to be, the bound alone decides.
No kernel may reach another device: no remote copies, remote signals or barrier semaphores. Data moves between devices by JAX's collectives and lax.ppermute only.
A program may use at most 64 MiB of HBM per device.

v0:
```python
import jax
import jax.numpy as jnp
from jax import lax
from jax.experimental import pallas as pl
from jax.experimental.pallas import tpu as pltpu
from jax.sharding import PartitionSpec as P

ITERS = 2
RESIDUAL_WATER = 0.05
STORAGE = 0.2
TIME_STEP = 0.5
LATERAL = 0.5
TINY = 1e-30
ROW_BLOCK = 32
PAD = 8
F32 = jnp.float32
BF16 = jnp.bfloat16
MIB = 1 << 20


def log2(x):
    return lax.log(x) * 1.4426950408889634


def lane_table(table, layers_like):
    t0, t1, t2, t3 = (table[i : i + 1, :] for i in range(4))
    alpha = 4.0 * t0
    n1 = 0.2 + 2.0 * t1
    half_m = 0.5 * n1 / (1.0 + n1)
    ks3 = 3.0 * t2
    room = (0.3 - RESIDUAL_WATER) + 0.3 * t3
    return [jnp.broadcast_to(r, layers_like) for r in (alpha, n1, half_m, ks3, room)]


def closure(head, alpha, n1, half_m, ksat, cap):
    suction = jnp.maximum(alpha * jnp.maximum(-head, 0.0), TINY)
    power = jnp.exp2(n1 * log2(suction))
    log_base = log2(1.0 + suction * power)
    root = jnp.exp2(-(half_m * log_base))
    saturation = root * root
    share = power * saturation
    inner = 1.0 - share
    conduct = ksat * root * (inner * inner)
    storage = STORAGE / TIME_STEP + cap * (share * jnp.exp2(-log_base))
    return saturation, conduct, storage


def lane_lookup(row, index):
    return jnp.take_along_axis(row, index, axis=1, mode="promise_in_bounds")


def edge_messages(head, conduct, k, lanes, packed):
    width = lanes.shape[1]
    for base, value in ((0, head), (width // 2, conduct)):
        moved = pltpu.roll(value, base + 2 * k + 1, 1)
        packed = jnp.where((lanes == base + 2 * k) | (lanes == base + 2 * k + 1), moved, packed)
    return packed


def first_kernel(
    h_ref, soil_ref, ks_ref, table_ref,
    alpha_ref, n1_ref, half_m_ref, ksat_ref, room_ref, sat_ref, cond_ref, stor_ref,
    row_even_ref, row_odd_ref, lane_ref,
):
    layers, rows, width = h_ref.shape
    tables = lane_table(table_ref[...], (rows, width))
    even = lax.rem(lax.axis_index("bx"), 2) == 0
    lanes = lax.broadcasted_iota(jnp.int32, (rows, width), 1)
    packed = jnp.zeros((rows, width), F32)
    for k in range(layers):
        head = h_ref[k]
        kind = soil_ref[k]
        alpha, n1, half_m, ks3, room = (lane_lookup(t, kind) for t in tables)
        ksat = ks3 * ks_ref[k]
        cap = (2.0 * room) * (n1 * alpha)
        saturation, conduct, storage = closure(head, alpha, n1, half_m, ksat, cap)
        alpha_ref[k] = alpha
        n1_ref[k] = n1
        half_m_ref[k] = half_m
        ksat_ref[k] = ksat
        room_ref[k] = room
        sat_ref[k] = saturation
        cond_ref[k] = conduct
        stor_ref[k] = storage
        packed = edge_messages(head, conduct, k, lanes, packed)
    lane_ref[...] = packed
    store_rows(h_ref, cond_ref, even, row_even_ref, row_odd_ref)


def store_rows(head_ref, cond_ref, even, row_even_ref, row_odd_ref):
    rows = head_ref.shape[1]
    for part, ref in enumerate((head_ref, cond_ref)):
        low = ref[:, 0, :]
        high = ref[:, rows - 1, :]
        row_even_ref[part] = jnp.where(even, high, low)
        row_odd_ref[part] = jnp.where(even, low, high)


def fill_pads(head_ref, cond_ref, row_even_ref, row_odd_ref, head_pad, cond_pad):
    rows = head_ref.shape[1]
    index = lax.axis_index("bx")
    even = lax.rem(index, 2) == 0
    first = index == 0
    last = index == lax.axis_size("bx") - 1
    for ref, pad, part, sign in ((head_ref, head_pad, 0, 1.0), (cond_ref, cond_pad, 1, -1.0)):
        pad[:, PAD : PAD + rows, :] = ref[...]
        low = jnp.where(even, row_odd_ref[part], row_even_ref[part])
        high = jnp.where(even, row_even_ref[part], row_odd_ref[part])
        pad[:, PAD - 1, :] = jnp.where(first, sign * ref[:, 0, :], low)
        pad[:, PAD + rows, :] = jnp.where(last, sign * ref[:, rows - 1, :], high)


def lane_halo(own, lane_even, lane_odd):
    index = lax.axis_index("by")
    even = lax.rem(index, 2) == 0
    width = own.shape[1]
    lanes = lax.broadcasted_iota(jnp.int32, own.shape, 1)
    sign = jnp.where(lanes < width // 2, 1.0, -1.0)
    low = jnp.where(even, lane_odd, lane_even)
    high = jnp.where(even, lane_even, lane_odd)
    low = jnp.where(index == 0, sign * pltpu.roll(own, width - 1, 1), low)
    high = jnp.where(
        index == lax.axis_size("by") - 1, sign * pltpu.roll(own, 1, 1), high
    )
    return jnp.where(lax.rem(lanes, 2) == 0, low, pltpu.roll(high, width - 2, 1))


def lateral_terms(k, head_pad, cond_pad, halo, lanes):
    rows = head_pad.shape[1] - 2 * PAD
    width = head_pad.shape[2]
    at = lambda pad, move: pad[k, PAD + move : PAD + move + rows, :]
    head, conduct = at(head_pad, 0), at(cond_pad, 0)
    halo_head = pltpu.roll(halo, (width - 2 * k) % width, 1)
    halo_cond = pltpu.roll(halo, (width // 2 - 2 * k) % width, 1)
    first = lanes == 0
    last = lanes == width - 1
    pairs = [
        (at(head_pad, -1), at(cond_pad, -1)),
        (at(head_pad, 1), at(cond_pad, 1)),
        (
            jnp.where(first, halo_head, pltpu.roll(head, 1, 1)),
            jnp.where(first, halo_cond, pltpu.roll(conduct, 1, 1)),
        ),
        (
            jnp.where(last, halo_head, pltpu.roll(head, width - 1, 1)),
            jnp.where(last, halo_cond, pltpu.roll(conduct, width - 1, 1)),
        ),
    ]
    flow = 0.0
    faces = 0.0
    for other_head, other_cond in pairs:
        both = conduct + other_cond
        flow = flow + both * (head - other_head)
        faces = faces + both
    return head, conduct, (0.5 * LATERAL) * flow, (0.5 * LATERAL) * faces


def factor_kernel(
    h_ref, cond_ref, stor_ref, row_even_ref, row_odd_ref, own_ref, lane_even_ref, lane_odd_ref,
    res_ref, inv_ref, vert_ref,
    head_pad, cond_pad,
):
    layers, rows, width = h_ref.shape
    fill_pads(h_ref, cond_ref, row_even_ref, row_odd_ref, head_pad, cond_pad)
    halo = lane_halo(own_ref[...], lane_even_ref[...], lane_odd_ref[...])
    lanes = lax.broadcasted_iota(jnp.int32, (rows, width), 1)
    vert_above = flux_above = ratio_above = None
    for k in range(layers):
        head, conduct, flow, faces = lateral_terms(k, head_pad, cond_pad, halo, lanes)
        diagonal = stor_ref[k] + faces
        if k < layers - 1:
            vert = 0.5 * (conduct + cond_ref[k + 1])
            flux = vert * (head - h_ref[k + 1] + 1.0)
            diagonal = diagonal + vert
        else:
            vert = None
            flux = conduct
        residual = flux + flow
        if k:
            residual = residual - flux_above
            diagonal = diagonal + vert_above
            diagonal = diagonal - vert_above * ratio_above
        inverse = 1.0 / diagonal
        res_ref[k] = residual
        inv_ref[k] = inverse
        if vert is not None:
            vert_ref[k] = vert
            ratio_above = vert * inverse
        vert_above, flux_above = vert, flux


def solve(residuals, inverses, verts):
    layers = len(residuals)
    values = []
    for k in range(layers):
        target = -residuals[k]
        if k:
            target = target + verts[k - 1]() * values[k - 1]
        values.append(target * inverses[k]())
    result = [values[layers - 1]]
    for k in range(layers - 2, -1, -1):
        result.insert(0, values[k] + (verts[k]() * inverses[k]()) * result[0])
    return result


def slot_places(ids, width):
    shift = width.bit_length() - 1
    row = ids >> shift
    return row & (ROW_BLOCK - 1), (row // ROW_BLOCK) * width + (ids & (width - 1))


def one_hot(ids, count, dtype):
    place = lax.broadcasted_iota(jnp.int32, (count, ids.shape[1]), 0)
    return (place == ids).astype(dtype)


def middle_kernel(
    slots_ref, h_ref, res_ref, inv_ref, vert_ref,
    alpha_ref, n1_ref, half_m_ref, ksat_ref, room_ref,
    head_ref, sat_ref, cond_ref, stor_ref, sink_ref, row_even_ref, row_odd_ref, lane_ref,
    total, left,
):
    layers, rows, width = h_ref.shape
    peers, fields, per_peer = slots_ref.shape
    roots = fields - 2
    values = fields - 1
    blocks = rows // ROW_BLOCK
    half = values * ROW_BLOCK
    total[...] = jnp.zeros_like(total)

    def place(peer, carry):
        block = slots_ref[peer]
        row, column = slot_places(block[values : values + 1, :].astype(jnp.int32), width)
        hot = one_hot(column, blocks * width, F32).astype(BF16)
        mask = lax.broadcasted_iota(jnp.int32, (ROW_BLOCK, per_peer), 0) == row
        high = block.astype(BF16).astype(F32)
        low = block - high
        for f in range(values):
            at = f * ROW_BLOCK
            left[at : at + ROW_BLOCK, :] = jnp.where(mask, high[f : f + 1, :], 0.0).astype(BF16)
            at = at + half
            left[at : at + ROW_BLOCK, :] = jnp.where(mask, low[f : f + 1, :], 0.0).astype(BF16)
        total[...] += lax.dot_general(
            left[...], hot, (((1,), (1,)), ((), ())), preferred_element_type=F32
        )
        return carry

    lax.fori_loop(0, peers, place, 0)

    def grid(f):
        at = f * ROW_BLOCK
        pieces = [
            total[at : at + ROW_BLOCK, b * width : (b + 1) * width]
            + total[half + at : half + at + ROW_BLOCK, b * width : (b + 1) * width]
            for b in range(blocks)
        ]
        return jnp.concatenate(pieces, 0)

    residuals = []
    for k in range(layers):
        residual = res_ref[k]
        if k < roots:
            sink = grid(k)
            sink_ref[k] = sink
            residual = residual + sink
        if k == 0:
            residual = residual - grid(roots)
        residuals.append(residual)
    sink_ref[roots] = grid(roots)
    inverses = [lambda k=k: inv_ref[k] for k in range(layers)]
    verts = [lambda k=k: vert_ref[k] for k in range(layers - 1)]
    delta = solve(residuals, inverses, verts)
    even = lax.rem(lax.axis_index("bx"), 2) == 0
    lanes = lax.broadcasted_iota(jnp.int32, (rows, width), 1)
    packed = jnp.zeros((rows, width), F32)
    for k in range(layers):
        head_ref[k] = h_ref[k] + delta[k]
    for k in range(layers):
        head = head_ref[k]
        alpha, n1 = alpha_ref[k], n1_ref[k]
        cap = (2.0 * room_ref[k]) * (n1 * alpha)
        saturation, conduct, storage = closure(
            head, alpha, n1, half_m_ref[k], ksat_ref[k], cap
        )
        sat_ref[k] = saturation
        cond_ref[k] = conduct
        stor_ref[k] = storage
        packed = edge_messages(head, conduct, k, lanes, packed)
    lane_ref[...] = packed
    store_rows(head_ref, cond_ref, even, row_even_ref, row_odd_ref)


def last_kernel(
    slots_ref, old_head_ref, old_sat_ref, sat_ref, cond_ref, stor_ref, sink_ref,
    alpha_ref, n1_ref, half_m_ref, room_ref,
    row_even_ref, row_odd_ref, own_ref, lane_even_ref, lane_odd_ref,
    head_ref, reply_ref,
    head_pad, cond_pad, inv_ref, vert_ref, value_ref,
):
    layers, rows, width = head_ref.shape
    peers, fields, per_peer = slots_ref.shape
    roots = fields - 2
    blocks = rows // ROW_BLOCK
    fill_pads(old_head_ref, cond_ref, row_even_ref, row_odd_ref, head_pad, cond_pad)
    halo = lane_halo(own_ref[...], lane_even_ref[...], lane_odd_ref[...])
    lanes = lax.broadcasted_iota(jnp.int32, (rows, width), 1)
    vert_above = flux_above = ratio_above = value = None
    for k in range(layers):
        head, conduct, flow, faces = lateral_terms(k, head_pad, cond_pad, halo, lanes)
        diagonal = stor_ref[k] + faces
        if k < layers - 1:
            vert = 0.5 * (conduct + cond_ref[k + 1])
            flux = vert * (head - old_head_ref[k + 1] + 1.0)
            diagonal = diagonal + vert
        else:
            vert = None
            flux = conduct
        residual = flux + flow + (room_ref[k] * (1.0 / TIME_STEP)) * (sat_ref[k] - old_sat_ref[k])
        if k < roots:
            residual = residual + sink_ref[k]
        if k:
            residual = residual - flux_above
            diagonal = diagonal + vert_above
            diagonal = diagonal - vert_above * ratio_above
        else:
            residual = residual - sink_ref[roots]
        inverse = 1.0 / diagonal
        target = -residual
        if k:
            target = target + vert_above * value
        value = target * inverse
        value_ref[k] = value
        if vert is not None:
            ratio_above = vert * inverse
            vert_ref[k] = ratio_above
        vert_above, flux_above = vert, flux
    change = value
    head_ref[layers - 1] = old_head_ref[layers - 1] + change
    numer = jnp.zeros((rows, width), F32)
    denom = jnp.zeros((rows, width), F32)
    for k in range(layers - 2, -1, -1):
        change = value_ref[k] + vert_ref[k] * change
        head = old_head_ref[k] + change
        head_ref[k] = head
        if k < roots:
            suction = jnp.maximum(alpha_ref[k] * jnp.maximum(-head, 0.0), TINY)
            power = jnp.exp2(n1_ref[k] * log2(suction))
            log_base = log2(1.0 + suction * power)
            saturation = jnp.exp2(-2.0 * half_m_ref[k] * log_base)
            sink = sink_ref[k]
            numer = numer + sink * saturation
            denom = denom + sink
    held = denom > 0.0
    stress = jnp.where(held, numer / jnp.where(held, denom, 1.0), 0.0)
    wide = jnp.concatenate(
        [stress[b * ROW_BLOCK : (b + 1) * ROW_BLOCK, :] for b in range(blocks)], 1
    )
    high = wide.astype(BF16)
    both = jnp.concatenate([high, (wide - high.astype(F32)).astype(BF16)], 0)

    def answer(peer, carry):
        ids = slots_ref[peer, fields - 1 : fields, :].astype(jnp.int32)
        row, column = slot_places(ids, width)
        hot = one_hot(column, blocks * width, F32).astype(BF16)
        found = jnp.dot(both, hot, preferred_element_type=F32)
        found = found[:ROW_BLOCK] + found[ROW_BLOCK:]
        mask = lax.broadcasted_iota(jnp.int32, (ROW_BLOCK, per_peer), 0) == row
        reply_ref[pl.ds(peer, 1), :] = jnp.sum(jnp.where(mask, found, 0.0), 0, keepdims=True)
        return carry

    lax.fori_loop(0, peers, answer, 0)


def swaps(size):
    even = [(i, i ^ 1) for i in range(size)]
    odd = [(i, (i + 1) % size if i % 2 else (i - 1) % size) for i in range(size)]
    return even, odd


def exchange(row_even, row_odd, packed):
    even_x, odd_x = swaps(lax.axis_size("bx"))
    even_y, odd_y = swaps(lax.axis_size("by"))
    return (
        lax.ppermute(row_even, "bx", even_x),
        lax.ppermute(row_odd, "bx", odd_x),
        packed,
        lax.ppermute(packed, "by", even_y),
        lax.ppermute(packed, "by", odd_y),
    )


def call(kernel, outs, scratch, name, limit=24):
    return pl.pallas_call(
        kernel,
        out_shape=[jax.ShapeDtypeStruct(s, F32) for s in outs],
        scratch_shapes=scratch,
        name=name,
        compiler_params=pltpu.CompilerParams(vmem_limit_bytes=limit * MIB),
    )


def on_device(
    h_old,
    soil_type,
    ks_scale,
    soil_table,
    clump_brick,
    clump_cell,
    root_fraction,
    transpiration,
    infiltration,
):
    layers, rows, width = h_old.shape
    peers = lax.axis_size("bx") * lax.axis_size("by")
    roots, slot_count = root_fraction.shape
    per_peer = slot_count // peers
    cells = (layers, rows, width)
    row_msg = (2, layers, width)
    lane_msg = (rows, width)
    axes = ("bx", "by")

    ids = jnp.where(clump_brick >= 0, clump_cell, -1).astype(F32)
    forcing = jnp.concatenate(
        [root_fraction * transpiration[None], infiltration[None], ids[None]], 0
    )
    fields = roots + 2
    slots = lax.all_to_all(
        forcing.reshape(fields, peers, per_peer).transpose(1, 0, 2),
        axes,
        split_axis=0,
        concat_axis=0,
        tiled=True,
    )
    table = jnp.pad(soil_table, ((0, 0), (0, width - soil_table.shape[1])))
    alpha, n1, half_m, ksat, room, old_sat, conduct, storage, row_even, row_odd, packed = call(
        first_kernel, [cells] * 8 + [row_msg, row_msg, lane_msg], [], "first"
    )(h_old, soil_type, ks_scale, table)
    pads = [pltpu.VMEM((layers, rows + 2 * PAD, width), F32)] * 2
    residual, inverse, vert = call(factor_kernel, [cells] * 3, pads, "factor")(
        h_old, conduct, storage, *exchange(row_even, row_odd, packed)
    )
    values = fields - 1
    blocks = rows // ROW_BLOCK
    head, sat, conduct, storage, sink, row_even, row_odd, packed = call(
        middle_kernel,
        [cells] * 4 + [(roots + 1, rows, width), row_msg, row_msg, lane_msg],
        [
            pltpu.VMEM((2 * values * ROW_BLOCK, blocks * width), F32),
            pltpu.VMEM((2 * values * ROW_BLOCK, per_peer), BF16),
        ],
        "middle",
    )(slots, h_old, residual, inverse, vert, alpha, n1, half_m, ksat, room)
    head, reply = call(
        last_kernel,
        [cells, (peers, per_peer)],
        pads + [pltpu.VMEM(cells, F32)] * 3,
        "last",
    )(
        slots, head, old_sat, sat, conduct, storage, sink, alpha, n1, half_m, room,
        *exchange(row_even, row_odd, packed),
    )
    stress = lax.all_to_all(reply, axes, split_axis=0, concat_axis=0, tiled=True)
    return head, stress.reshape(slot_count)


def solution(mesh):
    placed = (
        P(None, "bx", "by"),
        P(None, "bx", "by"),
        P(None, "bx", "by"),
        P(),
        P(("bx", "by")),
        P(("bx", "by")),
        P(None, ("bx", "by")),
        P(("bx", "by")),
        P(("bx", "by")),
    )
    return jax.shard_map(
        on_device,
        mesh=mesh,
        in_specs=placed,
        out_specs=(P(None, "bx", "by"), P(("bx", "by"))),
        check_vma=False,
    )
```

profile of v0, /device:TPU:0, one launch (start us, length us, event | category | flops | bytes accessed | tf_op | source)
XLA Modules:
  0.0 76.4 jit_solution(13525542396124114602)
XLA Ops:
  0.6 1.1 %broadcast_multiply_fusion = f32[14,8192]{1,0:T(8,128)S(1)} fusion(f32[14,8192]{1,0:T(8,128)} %param.15, f32[8192]{0:T(1024)} %param.16), kind=kLoop, calls=%fused_computation.1 | loop fusion | flops 114688 | bytes 950272 | tf_op jit(solution)/shard_map/mul | solution.py:424
  1.7 0.2 copy.14
  1.9 0.0 copy-start.16
  1.9 0.0 copy-start.17
  2.0 0.3 copy.12
  2.2 0.5 copy-done.16
  2.7 0.0 copy-done.17
  2.7 0.0 copy-start.18
  2.7 0.7 copy-done.18
  3.5 0.9 %maximum_bitcast_fusion = f32[32,16,256]{2,1,0:T(8,128)} fusion(f32[1,32,256]{2,0,1:T(1,128)S(1)} %bitcast.12, f32[1,32,256]{2,0,1:T(1,128)S(1)} %bitcast.14, f32[14,32,256]{2,0,1:T(8,128)S(1)} %copy.12), kind=kLoop, calls=%fused_computation | loop fusion | flops 262144 | bytes 1048576 | tf_op jit(solution)/shard_map/transpose | solution.py:428
  4.4 0.0 copy-start.19
  4.4 0.0 copy-start
  4.4 7.3 %all-to-all-start = ((f32[32,16,256]{2,1,0:T(8,128)}), f32[32,16,256]{2,1,0:T(8,128)S(1)}, u32[]{:S(2)}, u32[]{:S(2)}) async-start(f32[32,16,256]{2,1,0:T(8,128)} %maximum_bitcast_fusion), calls=%async_computation | async-start | bytes 1048576 | tf_op jit(solution)/shard_map/all_to_all | solution.py:427
  11.7 0.0 copy-done.19
  11.7 0.0 copy-done
  11.7 0.0 copy-start.14
  11.7 1.1 %copy-done.14 = s32[20,64,128]{2,1,0:T(8,128)S(1)} copy-done((s32[20,64,128]{2,1,0:T(8,128)S(1)}, s32[20,64,128]{2,1,0:T(8,128)}, u32[]{:S(2)}) %copy-start.14) | copy-done | bytes 655384
  12.8 0.0 copy-start.15
  12.8 1.1 %copy-done.15 = f32[20,64,128]{2,1,0:T(8,128)S(1)} copy-done((f32[20,64,128]{2,1,0:T(8,128)S(1)}, f32[20,64,128]{2,1,0:T(8,128)}, u32[]{:S(2)}) %copy-start.15) | copy-done | bytes 655384
  13.9 3.2 %first.1 = (f32[20,64,128]{2,1,0:T(8,128)S(1)}, f32[20,64,128]{2,1,0:T(8,128)S(1)}, f32[20,64,128]{2,1,0:T(8,128)S(1)}, f32[20,64,128]{2,1,0:T(8,128)S(1)}, f32[...) custom-call(f32[20,64,128]{2,1,0:T(8,128)S(1)} %copy-done, ...), custom_call_target="tpu_custom_call" | custom-call | tf_op jit(solution)/shard_map/first/pallas_call | solution.py:435
  17.1 0.0 copy-start.1
  17.1 0.8 %copy-done.1 = f32[20,64,128]{2,1,0:T(8,128)} copy-done((f32[20,64,128]{2,1,0:T(8,128)}, f32[20,64,128]{2,1,0:T(8,128)S(1)}, u32[]{:S(2)}) %copy-start.1) | copy-done | bytes 655384
  17.9 0.0 copy-start.4
  17.9 0.9 %copy-done.4 = f32[20,64,128]{2,1,0:T(8,128)} copy-done((f32[20,64,128]{2,1,0:T(8,128)}, f32[20,64,128]{2,1,0:T(8,128)S(1)}, u32[]{:S(2)}) %copy-start.4) | copy-done | bytes 655384
  18.8 0.0 copy-start.6
  18.8 0.8 %copy-done.6 = f32[20,64,128]{2,1,0:T(8,128)} copy-done((f32[20,64,128]{2,1,0:T(8,128)}, f32[20,64,128]{2,1,0:T(8,128)S(1)}, u32[]{:S(2)}) %copy-start.6) | copy-done | bytes 655384
  19.6 4.5 %collective-permute-start.3 = (f32[64,128]{1,0:T(8,128)S(1)}, f32[64,128]{1,0:T(8,128)S(1)}, u32[]{:S(2)}, u32[]{:S(2)}) collective-permute-start(f32[64,128]{1,0:T(8,128)S(1)} %get-tuple-element.30.own_ref), channel_id=1, source_target_pairs={{0,7},{1,2},{2,1},{3,4},{4,3},{5,6},{6,5},{7,0},{8,15},{9,10},{10,... | collective-permute-start | bytes 98312 | tf_op jit(solution)/shard_map/ppermute | solution.py:388
  24.2 0.0 collective-permute-start.2
  24.2 0.0 collective-permute-start
  24.2 1.6 %collective-permute-start.1 = (f32[2,20,128]{2,1,0:T(8,128)S(1)}, f32[2,20,128]{2,1,0:T(8,128)S(1)}, u32[]{:S(2)}, u32[]{:S(2)}) collective-permute-start(f32[2,20,128]{2,1,0:T(8,128)S(1)} %get-tuple-element.29), channel_id=1, source_target_pairs={{0,24},{8,16},{16,8},{24,0},{1,25},{9,17},{17,9},{25,1},{2,26},{10... | collective-permute-start | bytes 61448 | tf_op jit(solution)/shard_map/ppermute | solution.py:385
  25.8 0.0 collective-permute-done.row_even_ref
  25.8 1.6 %collective-permute-done.1.row_odd_ref = f32[2,20,128]{2,1,0:T(8,128)S(1)} collective-permute-done((f32[2,20,128]{2,1,0:T(8,128)S(1)}, f32[2,20,128]{2,1,0:T(8,128)S(1)}, u32[]{:S(2)}, u32[]{:S(2)}) %collective-permute-start.1) | collective-permute-done | bytes 20512 | tf_op jit(solution)/shard_map/ppermute | solution.py:385
  27.4 0.0 collective-permute-done.3.lane_odd_ref
  27.4 0.7 collective-permute-done.2.lane_even_ref
  28.1 1.3 %factor.1 = (f32[20,64,128]{2,1,0:T(8,128)S(1)}, f32[20,64,128]{2,1,0:T(8,128)S(1)}, f32[20,64,128]{2,1,0:T(8,128)S(1)}) custom-call(f32[20,64,128]{2,1,0:T(8,128)S(1)} %copy-done, f32[20,64,128]{2,1,0:T(8,128)S(1)} %get-tuple-element.26.cond_ref, f32[20,64,128]{2,1,0:T(8,128)S(1)} %get-tuple-element.27.stor_ref, ...), custom_call_target="tpu_custom_call" | custom-call | tf_op jit(solution)/shard_map/factor/pallas_call | solution.py:439
  29.4 0.0 copy-start.8
  29.4 0.8 %copy-done.8 = f32[20,64,128]{2,1,0:T(8,128)} copy-done((f32[20,64,128]{2,1,0:T(8,128)}, f32[20,64,128]{2,1,0:T(8,128)S(1)}, u32[]{:S(2)}) %copy-start.8) | copy-done | bytes 655384
  30.3 0.0 copy-start.10
  30.3 0.8 %copy-done.10 = f32[20,64,128]{2,1,0:T(8,128)} copy-done((f32[20,64,128]{2,1,0:T(8,128)}, f32[20,64,128]{2,1,0:T(8,128)S(1)}, u32[]{:S(2)}) %copy-start.10) | copy-done | bytes 655384
  31.1 0.0 copy-start.12
  31.1 0.8 %copy-done.12 = f32[20,64,128]{2,1,0:T(8,128)} copy-done((f32[20,64,128]{2,1,0:T(8,128)}, f32[20,64,128]{2,1,0:T(8,128)S(1)}, u32[]{:S(2)}) %copy-start.12) | copy-done | bytes 655384
  31.9 0.0 all-to-all-done.slots_ref
  31.9 0.0 copy-start.2
  32.0 1.1 %copy-done.2 = f32[20,64,128]{2,1,0:T(8,128)S(1)} copy-done((f32[20,64,128]{2,1,0:T(8,128)S(1)}, f32[20,64,128]{2,1,0:T(8,128)}, u32[]{:S(2)}) %copy-start.2) | copy-done | bytes 655384
  33.0 0.0 copy-start.7
  33.0 1.1 %copy-done.7 = f32[20,64,128]{2,1,0:T(8,128)S(1)} copy-done((f32[20,64,128]{2,1,0:T(8,128)S(1)}, f32[20,64,128]{2,1,0:T(8,128)}, u32[]{:S(2)}) %copy-start.7) | copy-done | bytes 655384
  34.1 0.0 copy-start.9
  34.1 1.1 %copy-done.9 = f32[20,64,128]{2,1,0:T(8,128)S(1)} copy-done((f32[20,64,128]{2,1,0:T(8,128)S(1)}, f32[20,64,128]{2,1,0:T(8,128)}, u32[]{:S(2)}) %copy-start.9) | copy-done | bytes 655384
  35.2 1.1 %copy-done.11 = f32[20,64,128]{2,1,0:T(8,128)S(1)} copy-done((f32[20,64,128]{2,1,0:T(8,128)S(1)}, f32[20,64,128]{2,1,0:T(8,128)}, u32[]{:S(2)}) %copy-start.11) | copy-done | bytes 655384
  36.3 1.1 %copy-done.13 = f32[20,64,128]{2,1,0:T(8,128)S(1)} copy-done((f32[20,64,128]{2,1,0:T(8,128)S(1)}, f32[20,64,128]{2,1,0:T(8,128)}, u32[]{:S(2)}) %copy-start.13) | copy-done | bytes 655384
  37.4 12.2 %middle.1 = (f32[20,64,128]{2,1,0:T(8,128)S(1)}, f32[20,64,128]{2,1,0:T(8,128)S(1)}, f32[20,64,128]{2,1,0:T(8,128)S(1)}, f32[20,64,128]{2,1,0:T(8,128)S(1)}, f32...) custom-call(f32[32,16,256]{2,1,0:T(8,128)S(1)} %all-to-all-done.slots_re, ...), custom_call_target="tpu_custom_call" | custom-call | tf_op jit(solution)/shard_map/middle/pallas_call | solution.py:444
  49.6 2.8 %collective-permute-start.7 = (f32[64,128]{1,0:T(8,128)S(1)}, f32[64,128]{1,0:T(8,128)S(1)}, u32[]{:S(2)}, u32[]{:S(2)}) collective-permute-start(f32[64,128]{1,0:T(8,128)S(1)} %get-tuple-element.47.own_ref), channel_id=1, source_target_pairs={{0,7},{1,2},{2,1},{3,4},{4,3},{5,6},{6,5},{7,0},{8,15},{9,10},{10,... | collective-permute-start | bytes 98312 | tf_op jit(solution)/shard_map/ppermute | solution.py:388
  52.4 0.0 collective-permute-start.6
  52.4 0.0 collective-permute-start.4
  52.4 1.6 %collective-permute-start.5 = (f32[2,20,128]{2,1,0:T(8,128)S(1)}, f32[2,20,128]{2,1,0:T(8,128)S(1)}, u32[]{:S(2)}, u32[]{:S(2)}) collective-permute-start(f32[2,20,128]{2,1,0:T(8,128)S(1)} %get-tuple-element.46), channel_id=1, source_target_pairs={{0,24},{8,16},{16,8},{24,0},{1,25},{9,17},{17,9},{25,1},{2,26},{10... | collective-permute-start | bytes 61448 | tf_op jit(solution)/shard_map/ppermute | solution.py:385
  54.0 0.0 collective-permute-done.4.row_even_ref
  54.0 1.6 %collective-permute-done.5.row_odd_ref = f32[2,20,128]{2,1,0:T(8,128)S(1)} collective-permute-done((f32[2,20,128]{2,1,0:T(8,128)S(1)}, f32[2,20,128]{2,1,0:T(8,128)S(1)}, u32[]{:S(2)}, u32[]{:S(2)}) %collective-permute-start.5) | collective-permute-done | bytes 20512 | tf_op jit(solution)/shard_map/ppermute | solution.py:385
  55.6 0.7 collective-permute-done.7.lane_odd_ref
  56.3 0.3 collective-permute-done.6.lane_even_ref
  56.7 0.0 copy-done.3
  56.7 0.0 copy-done.5
  56.7 8.5 %last.1 = (f32[20,64,128]{2,1,0:T(8,128)}, f32[32,256]{1,0:T(8,128)S(1)}) custom-call(f32[32,16,256]{2,1,0:T(8,128)S(1)} %all-to-all-done.slots_ref, f32[20,64,128]{2,1,0:T(8,128)S(1)} %get-tuple-element.39.old_head_ref, f32[20,64,128]{2,1,0:T(8,128)S(1)} %copy-done.5, f32[20,64,128]{2,1,0:T(8,128)S(1)} %get-tuple-element.41.sat_ref, ...), custom_call_target="tpu_custom_call" | custom-call | tf_op jit(solution)/shard_map/last/pallas_call | solution.py:453
  65.2 10.7 %all_to_all.14 = f32[32,1,256]{2,1,0:T(1,128)S(1)} all-to-all(f32[32,1,256]{2,1,0:T(1,128)S(1)} %copy.13), channel_id=1, replica_groups=mesh['bx'=4,'by'=8] {'bx','by'}, dimensions={0} | all-to-all | bytes 65536 | tf_op jit(solution)/shard_map/all_to_all | solution.py:462
  75.8 0.6 copy.16
  (8 shorter events, 0.1 us)
Async XLA Ops:
  1.9 0.8 copy-start.16
  1.9 0.8 %copy-start.17 = (s32[8192]{0:T(1024)S(1)}, s32[8192]{0:T(1024)}, u32[]{:S(2)}) copy-start(s32[8192]{0:T(1024)} %param.13) | copy-start | bytes 98308
  2.7 0.8 copy-start.18
  4.4 7.3 %copy-start.19 = (f32[4,12]{1,0:T(4,128)S(1)}, f32[4,12]{1,0:T(4,128)}, u32[]{:S(2)}) copy-start(f32[4,12]{1,0:T(4,128)} %param.12) | copy-start | bytes 580
  4.4 7.4 %copy-start = (f32[20,64,128]{2,1,0:T(8,128)S(1)}, f32[20,64,128]{2,1,0:T(8,128)}, u32[]{:S(2)}) copy-start(f32[20,64,128]{2,1,0:T(8,128)} %h_ref.5) | copy-start | bytes 1966084
  4.4 27.6 %all-to-all-start = ((f32[32,16,256]{2,1,0:T(8,128)}), f32[32,16,256]{2,1,0:T(8,128)S(1)}, u32[]{:S(2)}, u32[]{:S(2)}) async-start(f32[32,16,256]{2,1,0:T(8,128)} %maximum_bitcast_fusion), calls=%async_computation | async-start | bytes 1048576 | tf_op jit(solution)/shard_map/all_to_all | solution.py:427
  11.7 1.1 %copy-start.14 = (s32[20,64,128]{2,1,0:T(8,128)S(1)}, s32[20,64,128]{2,1,0:T(8,128)}, u32[]{:S(2)}) copy-start(s32[20,64,128]{2,1,0:T(8,128)} %soil_ref.1) | copy-start | bytes 1966084
  12.8 1.1 %copy-start.15 = (f32[20,64,128]{2,1,0:T(8,128)S(1)}, f32[20,64,128]{2,1,0:T(8,128)}, u32[]{:S(2)}) copy-start(f32[20,64,128]{2,1,0:T(8,128)} %ks_ref.1) | copy-start | bytes 1966084
  17.1 0.8 %copy-start.1 = (f32[20,64,128]{2,1,0:T(8,128)}, f32[20,64,128]{2,1,0:T(8,128)S(1)}, u32[]{:S(2)}) copy-start(f32[20,64,128]{2,1,0:T(8,128)S(1)} %get-tuple-element.38.room_ref) | copy-start | bytes 1966084
  17.9 0.9 %copy-start.4 = (f32[20,64,128]{2,1,0:T(8,128)}, f32[20,64,128]{2,1,0:T(8,128)S(1)}, u32[]{:S(2)}) copy-start(f32[20,64,128]{2,1,0:T(8,128)S(1)} %get-tuple-element.40.old_sat_ref) | copy-start | bytes 1966084
  18.8 0.8 %copy-start.6 = (f32[20,64,128]{2,1,0:T(8,128)}, f32[20,64,128]{2,1,0:T(8,128)S(1)}, u32[]{:S(2)}) copy-start(f32[20,64,128]{2,1,0:T(8,128)S(1)} %get-tuple-element.37.ksat_ref) | copy-start | bytes 1966084
  19.6 7.8 %collective-permute-start.3 = (f32[64,128]{1,0:T(8,128)S(1)}, f32[64,128]{1,0:T(8,128)S(1)}, u32[]{:S(2)}, u32[]{:S(2)}) collective-permute-start(f32[64,128]{1,0:T(8,128)S(1)} %get-tuple-element.30.own_ref), channel_id=1, source_target_pairs={{0,7},{1,2},{2,1},{3,4},{4,3},{5,6},{6,5},{7,0},{8,15},{9,10},{10,... | collective-permute-start | bytes 98312 | tf_op jit(solution)/shard_map/ppermute | solution.py:388
  24.2 3.9 %collective-permute-start.2 = (f32[64,128]{1,0:T(8,128)S(1)}, f32[64,128]{1,0:T(8,128)S(1)}, u32[]{:S(2)}, u32[]{:S(2)}) collective-permute-start(f32[64,128]{1,0:T(8,128)S(1)} %get-tuple-element.30.own_ref), channel_id=1, source_target_pairs={{0,1},{1,0},{2,3},{3,2},{4,5},{5,4},{6,7},{7,6},{8,9},{9,8},{10,11... | collective-permute-start | bytes 98312 | tf_op jit(solution)/shard_map/ppermute | solution.py:387
  24.2 1.6 %collective-permute-start = (f32[2,20,128]{2,1,0:T(8,128)S(1)}, f32[2,20,128]{2,1,0:T(8,128)S(1)}, u32[]{:S(2)}, u32[]{:S(2)}) collective-permute-start(f32[2,20,128]{2,1,0:T(8,128)S(1)} %get-tuple-element.28), channel_id=1, source_target_pairs={{0,8},{8,0},{16,24},{24,16},{1,9},{9,1},{17,25},{25,17},{2,10},{10... | collective-permute-start | bytes 61448 | tf_op jit(solution)/shard_map/ppermute | solution.py:384
  24.2 3.3 %collective-permute-start.1 = (f32[2,20,128]{2,1,0:T(8,128)S(1)}, f32[2,20,128]{2,1,0:T(8,128)S(1)}, u32[]{:S(2)}, u32[]{:S(2)}) collective-permute-start(f32[2,20,128]{2,1,0:T(8,128)S(1)} %get-tuple-element.29), channel_id=1, source_target_pairs={{0,24},{8,16},{16,8},{24,0},{1,25},{9,17},{17,9},{25,1},{2,26},{10... | collective-permute-start | bytes 61448 | tf_op jit(solution)/shard_map/ppermute | solution.py:385
  29.4 0.8 %copy-start.8 = (f32[20,64,128]{2,1,0:T(8,128)}, f32[20,64,128]{2,1,0:T(8,128)S(1)}, u32[]{:S(2)}) copy-start(f32[20,64,128]{2,1,0:T(8,128)S(1)} %get-tuple-element.31.res_ref) | copy-start | bytes 1966084
  30.3 0.8 %copy-start.10 = (f32[20,64,128]{2,1,0:T(8,128)}, f32[20,64,128]{2,1,0:T(8,128)S(1)}, u32[]{:S(2)}) copy-start(f32[20,64,128]{2,1,0:T(8,128)S(1)} %get-tuple-element.32.inv_ref) | copy-start | bytes 1966084
  31.1 0.8 %copy-start.12 = (f32[20,64,128]{2,1,0:T(8,128)}, f32[20,64,128]{2,1,0:T(8,128)S(1)}, u32[]{:S(2)}) copy-start(f32[20,64,128]{2,1,0:T(8,128)S(1)} %get-tuple-element.33.vert_ref) | copy-start | bytes 1966084
  31.9 1.1 %copy-start.2 = (f32[20,64,128]{2,1,0:T(8,128)S(1)}, f32[20,64,128]{2,1,0:T(8,128)}, u32[]{:S(2)}) copy-start(f32[20,64,128]{2,1,0:T(8,128)} %copy-done.1) | copy-start | bytes 1966084
  33.0 1.1 %copy-start.7 = (f32[20,64,128]{2,1,0:T(8,128)S(1)}, f32[20,64,128]{2,1,0:T(8,128)}, u32[]{:S(2)}) copy-start(f32[20,64,128]{2,1,0:T(8,128)} %copy-done.6) | copy-start | bytes 1966084
  34.1 1.1 %copy-start.9 = (f32[20,64,128]{2,1,0:T(8,128)S(1)}, f32[20,64,128]{2,1,0:T(8,128)}, u32[]{:S(2)}) copy-start(f32[20,64,128]{2,1,0:T(8,128)} %copy-done.8) | copy-start | bytes 1966084
  35.2 1.1 %copy-start.11 = (f32[20,64,128]{2,1,0:T(8,128)S(1)}, f32[20,64,128]{2,1,0:T(8,128)}, u32[]{:S(2)}) copy-start(f32[20,64,128]{2,1,0:T(8,128)} %copy-done.10) | copy-start | bytes 1966084
  36.3 1.1 %copy-start.13 = (f32[20,64,128]{2,1,0:T(8,128)S(1)}, f32[20,64,128]{2,1,0:T(8,128)}, u32[]{:S(2)}) copy-start(f32[20,64,128]{2,1,0:T(8,128)} %copy-done.12) | copy-start | bytes 1966084
  37.4 19.3 %copy-start.3 = (f32[20,64,128]{2,1,0:T(8,128)S(1)}, f32[20,64,128]{2,1,0:T(8,128)}, u32[]{:S(2)}) copy-start(f32[20,64,128]{2,1,0:T(8,128)} %copy-done.1) | copy-start | bytes 1966084
  37.4 19.3 %copy-start.5 = (f32[20,64,128]{2,1,0:T(8,128)S(1)}, f32[20,64,128]{2,1,0:T(8,128)}, u32[]{:S(2)}) copy-start(f32[20,64,128]{2,1,0:T(8,128)} %copy-done.4) | copy-start | bytes 1966084
  49.6 6.7 %collective-permute-start.7 = (f32[64,128]{1,0:T(8,128)S(1)}, f32[64,128]{1,0:T(8,128)S(1)}, u32[]{:S(2)}, u32[]{:S(2)}) collective-permute-start(f32[64,128]{1,0:T(8,128)S(1)} %get-tuple-element.47.own_ref), channel_id=1, source_target_pairs={{0,7},{1,2},{2,1},{3,4},{4,3},{5,6},{6,5},{7,0},{8,15},{9,10},{10,... | collective-permute-start | bytes 98312 | tf_op jit(solution)/shard_map/ppermute | solution.py:388
  52.4 4.3 %collective-permute-start.6 = (f32[64,128]{1,0:T(8,128)S(1)}, f32[64,128]{1,0:T(8,128)S(1)}, u32[]{:S(2)}, u32[]{:S(2)}) collective-permute-start(f32[64,128]{1,0:T(8,128)S(1)} %get-tuple-element.47.own_ref), channel_id=1, source_target_pairs={{0,1},{1,0},{2,3},{3,2},{4,5},{5,4},{6,7},{7,6},{8,9},{9,8},{10,11... | collective-permute-start | bytes 98312 | tf_op jit(solution)/shard_map/ppermute | solution.py:387
  52.4 1.6 %collective-permute-start.4 = (f32[2,20,128]{2,1,0:T(8,128)S(1)}, f32[2,20,128]{2,1,0:T(8,128)S(1)}, u32[]{:S(2)}, u32[]{:S(2)}) collective-permute-start(f32[2,20,128]{2,1,0:T(8,128)S(1)} %get-tuple-element.45), channel_id=1, source_target_pairs={{0,8},{8,0},{16,24},{24,16},{1,9},{9,1},{17,25},{25,17},{2,10},{10... | collective-permute-start | bytes 61448 | tf_op jit(solution)/shard_map/ppermute | solution.py:384
  52.4 3.3 %collective-permute-start.5 = (f32[2,20,128]{2,1,0:T(8,128)S(1)}, f32[2,20,128]{2,1,0:T(8,128)S(1)}, u32[]{:S(2)}, u32[]{:S(2)}) collective-permute-start(f32[2,20,128]{2,1,0:T(8,128)S(1)} %get-tuple-element.46), channel_id=1, source_target_pairs={{0,24},{8,16},{16,8},{24,0},{1,25},{9,17},{17,9},{25,1},{2,26},{10... | collective-permute-start | bytes 61448 | tf_op jit(solution)/shard_map/ppermute | solution.py:385
where the time goes:
time: 77.1 us; the launch traced here: 76.4 us
  Pallas kernels  25.2 us (33%)
  starting transfers between devices  17.8 us (23%)
  local copies, waits for them, and re-layouts  15 us (19%)
  blocking collectives  10.7 us (14%)
  waiting for transfers between devices  4.95 us (6%)
  other arithmetic  1.98 us (3%)
  between operations  0.78 us (1%)
    unnamed x42, local copies, waits for them, and re-layouts  14.7 us
    pallas_call x1, Pallas kernels, on_device(): call(middle_kernel, [cells] * 4 + [(roots + 1, rows, width), row_msg, row...  12.2 us
    all_to_all x1, blocking collectives, on_device(): lax.all_to_all(reply, axes, split_axis=0, concat_axis=0, tiled=True)  10.7 us
    pallas_call x1, Pallas kernels, on_device(): call(last_kernel, [cells, (peers, per_peer)], pads + [pltpu.VMEM(cells, F...  8.47 us
    all_to_all x1, starting transfers between devices, on_device(): lax.all_to_all(forcing.reshape(fields, peers, per_peer).transpose(1, 0, 2...  7.33 us
    ppermute x2, starting transfers between devices, exchange(): lax.ppermute(packed, 'by', odd_y)  7.29 us
    ppermute x2, waiting for transfers between devices, exchange(): lax.ppermute(row_odd, 'bx', odd_x)  3.28 us
    ppermute x2, starting transfers between devices, exchange(): lax.ppermute(row_odd, 'bx', odd_x)  3.22 us
  transfers between devices with their start and end apart: 9, of which 5 were waited for; matrix products, arithmetic and copies ran while one was open for 0% of the time, Pallas kernels for 6%

commit v1 on v0

v1 whole, which is shorter than its diff:
```python
import jax
import jax.numpy as jnp
from jax import lax
from jax.experimental import pallas as pl
from jax.experimental.pallas import tpu as pltpu
from jax.sharding import PartitionSpec as P

ITERS = 2
RESIDUAL_WATER = 0.05
STORAGE = 0.2
TIME_STEP = 0.5
LATERAL = 0.5
TINY = 1e-30
ROW_BLOCK = 32
HALF = 32
UNROLL = 8
GROUP = 2
LOG2E = 1.4426950408889634
PAD = 8
F32 = jnp.float32
BF16 = jnp.bfloat16
MIB = 1 << 20


def lane_tables(table, shape):
    t0, t1, t2, t3 = (table[i : i + 1, :] for i in range(4))
    alpha = 4.0 * t0
    n1 = 0.2 + 2.0 * t1
    half_m = 0.5 * n1 / (1.0 + n1)
    ks3 = (0.5 * LATERAL * 3.0) * t2
    room = ((0.3 - RESIDUAL_WATER) + 0.3 * t3) * (1.0 / TIME_STEP)
    rows = (alpha, LOG2E * n1, -LOG2E * half_m, ks3, room)
    return [jnp.broadcast_to(r, shape) for r in rows]


def powers(head, alpha, n1, half_m):
    suction = jnp.maximum(alpha * jnp.maximum(-head, 0.0), TINY)
    power = jnp.exp2(n1 * lax.log(suction))
    log_base = lax.log(1.0 + suction * power)
    return power, log_base, half_m * log_base


def closure(head, alpha, n1, half_m, ksat, room):
    power, log_base, half = powers(head, alpha, n1, half_m)
    root = jnp.exp2(half)
    saturation = root * root
    share = power * saturation
    inner = 1.0 - share
    conduct = (ksat * root) * (inner * inner)
    cap = (room * (1.0 / LOG2E)) * (n1 * alpha)
    storage = STORAGE / TIME_STEP + cap * (share * jnp.exp2(-LOG2E * log_base))
    return saturation, conduct, storage


def lane_lookup(row, index):
    return jnp.take_along_axis(row, index, axis=1, mode="promise_in_bounds")


def edge_messages(values, k, lanes, packed):
    width = lanes.shape[1]
    for part, value in enumerate(values):
        at = part * (width // 2) + 2 * k
        moved = pltpu.roll(value, at + 1, 1)
        packed = jnp.where((lanes == at) | (lanes == at + 1), moved, packed)
    return packed


def prepare_kernel(root_ref, transp_ref, infil_ref, cell_ref, out_ref):
    peers, fields, per_peer = out_ref.shape
    roots = fields - 2
    for peer in range(peers):
        at = slice(peer * per_peer, (peer + 1) * per_peer)
        out_ref[peer, :roots, :] = root_ref[:, at] * transp_ref[:, at]
        out_ref[peer, roots : roots + 1, :] = infil_ref[:, at]
        out_ref[peer, roots + 1 :, :] = cell_ref[:, at].astype(F32)


def layer_chunks(layers):
    size = 5 if layers % 5 == 0 else layers
    return [(at, size) for at in range(0, layers, size)]


def copies(pairs, sems, layers):
    chunks = layer_chunks(layers)
    return [
        [
            pltpu.make_async_copy(
                a.at[pl.ds(at, size)], b.at[pl.ds(at, size)], sems.at[c * len(pairs) + i]
            )
            for i, (a, b) in enumerate(pairs)
        ]
        for c, (at, size) in enumerate(chunks)
    ]


def first_kernel(
    h_hbm, soil_hbm, ks_hbm, table_ref,
    alpha_hbm, n1_hbm, half_m_hbm, ksat_hbm, room_hbm, sat_hbm,
    h_ref, cond_ref, stor_ref, row_even_ref, row_odd_ref, lane_ref,
    soil_ref, ks_ref, alpha_ref, n1_ref, half_m_ref, ksat_ref, room_ref, sat_ref,
    in_sems, out_sems,
):
    layers, rows, width = h_ref.shape
    ins = copies([(h_hbm, h_ref), (soil_hbm, soil_ref), (ks_hbm, ks_ref)], in_sems, layers)
    outs = copies(
        [
            (alpha_ref, alpha_hbm), (n1_ref, n1_hbm), (half_m_ref, half_m_hbm),
            (ksat_ref, ksat_hbm), (room_ref, room_hbm), (sat_ref, sat_hbm),
        ],
        out_sems,
        layers,
    )
    for chunk in ins:
        for copy in chunk:
            copy.start()
    tables = lane_tables(table_ref[...], (rows, width))
    even = lax.rem(lax.axis_index("bx"), 2) == 0
    lanes = lax.broadcasted_iota(jnp.int32, (rows, width), 1)
    packed = jnp.zeros((rows, width), F32)
    for (at, size), arrive, leave in zip(layer_chunks(layers), ins, outs):
        for copy in arrive:
            copy.wait()
        for k in range(at, at + size):
            head = h_ref[k]
            kind = soil_ref[k]
            alpha, n1, half_m, ks3, room = (lane_lookup(t, kind) for t in tables)
            ksat = ks3 * ks_ref[k]
            saturation, conduct, storage = closure(head, alpha, n1, half_m, ksat, room)
            alpha_ref[k] = alpha
            n1_ref[k] = n1
            half_m_ref[k] = half_m
            ksat_ref[k] = ksat
            room_ref[k] = room
            sat_ref[k] = saturation
            cond_ref[k] = conduct
            stor_ref[k] = storage
            packed = edge_messages((head, conduct), k, lanes, packed)
        for copy in leave:
            copy.start()
    lane_ref[...] = packed
    store_rows(h_ref, cond_ref, even, row_even_ref, row_odd_ref)
    for chunk in outs:
        for copy in chunk:
            copy.wait()


def store_rows(head_ref, cond_ref, even, row_even_ref, row_odd_ref):
    rows = head_ref.shape[1]
    for part, ref in enumerate((head_ref, cond_ref)):
        low = ref[:, 0, :]
        high = ref[:, rows - 1, :]
        row_even_ref[part] = jnp.where(even, high, low)
        row_odd_ref[part] = jnp.where(even, low, high)


def fill_pads(head_ref, cond_ref, row_even_ref, row_odd_ref, head_pad, cond_pad):
    rows = head_ref.shape[1]
    index = lax.axis_index("bx")
    even = lax.rem(index, 2) == 0
    first = index == 0
    last = index == lax.axis_size("bx") - 1
    for ref, pad, part, sign in ((head_ref, head_pad, 0, 1.0), (cond_ref, cond_pad, 1, -1.0)):
        pad[:, PAD : PAD + rows, :] = ref[...]
        low = jnp.where(even, row_odd_ref[part], row_even_ref[part])
        high = jnp.where(even, row_even_ref[part], row_odd_ref[part])
        pad[:, PAD - 1, :] = jnp.where(first, sign * ref[:, 0, :], low)
        pad[:, PAD + rows, :] = jnp.where(last, sign * ref[:, rows - 1, :], high)


def lane_halo(own, lane_even, lane_odd):
    index = lax.axis_index("by")
    even = lax.rem(index, 2) == 0
    width = own.shape[1]
    lanes = lax.broadcasted_iota(jnp.int32, own.shape, 1)
    sign = jnp.where(lanes < width // 2, 1.0, -1.0)
    low = jnp.where(even, lane_odd, lane_even)
    high = jnp.where(even, lane_even, lane_odd)
    low = jnp.where(index == 0, sign * pltpu.roll(own, width - 1, 1), low)
    high = jnp.where(
        index == lax.axis_size("by") - 1, sign * pltpu.roll(own, 1, 1), high
    )
    return jnp.where(lax.rem(lanes, 2) == 0, low, pltpu.roll(high, width - 2, 1))


def lateral_terms(k, top, size, head_pad, cond_pad, halo, lanes):
    width = head_pad.shape[2]
    at = lambda pad, move: pad[k, PAD + top + move : PAD + top + move + size, :]
    head, conduct = at(head_pad, 0), at(cond_pad, 0)
    halo_head = pltpu.roll(halo, (width - 2 * k) % width, 1)
    halo_cond = pltpu.roll(halo, (width // 2 - 2 * k) % width, 1)
    first = lanes == 0
    last = lanes == width - 1
    pairs = [
        (at(head_pad, -1), at(cond_pad, -1)),
        (at(head_pad, 1), at(cond_pad, 1)),
        (
            jnp.where(first, halo_head, pltpu.roll(head, 1, 1)),
            jnp.where(first, halo_cond, pltpu.roll(conduct, 1, 1)),
        ),
        (
            jnp.where(last, halo_head, pltpu.roll(head, width - 1, 1)),
            jnp.where(last, halo_cond, pltpu.roll(conduct, width - 1, 1)),
        ),
    ]
    flow = faces = None
    for other_head, other_cond in pairs:
        both = conduct + other_cond
        term = both * (head - other_head)
        flow = term if flow is None else flow + term
        faces = both if faces is None else faces + both
    return head, conduct, flow, faces


VERTICAL = 0.5 / (0.5 * LATERAL)


def factor_kernel(
    h_ref, cond_ref, stor_ref, row_even_ref, row_odd_ref, own_ref, lane_even_ref, lane_odd_ref,
    res_hbm, inv_hbm, vert_hbm,
    head_pad, cond_pad, res_ref, inv_ref, vert_ref, halo_ref, sems,
):
    layers, rows, width = h_ref.shape
    outs = copies([(res_ref, res_hbm), (inv_ref, inv_hbm), (vert_ref, vert_hbm)], sems, layers)
    fill_pads(h_ref, cond_ref, row_even_ref, row_odd_ref, head_pad, cond_pad)
    halo_ref[...] = lane_halo(own_ref[...], lane_even_ref[...], lane_odd_ref[...])
    size = HALF if rows % HALF == 0 else rows
    lanes = lax.broadcasted_iota(jnp.int32, (size, width), 1)
    for top in range(0, rows, size):
        span = slice(top, top + size)
        halo = halo_ref[span, :]
        vert_above = flux_above = ratio_above = None
        for k in range(layers):
            head, conduct, flow, faces = lateral_terms(
                k, top, size, head_pad, cond_pad, halo, lanes
            )
            diagonal = stor_ref[k, span, :] + faces
            if k < layers - 1:
                vert = VERTICAL * (conduct + cond_ref[k + 1, span, :])
                flux = vert * (head - h_ref[k + 1, span, :] + 1.0)
                diagonal = diagonal + vert
            else:
                vert = None
                flux = conduct * (2.0 * VERTICAL)
            residual = flux + flow
            if k:
                residual = residual - flux_above
                diagonal = diagonal + vert_above
                diagonal = diagonal - vert_above * ratio_above
            inverse = 1.0 / diagonal
            res_ref[k, span, :] = residual
            inv_ref[k, span, :] = inverse
            if vert is not None:
                vert_ref[k, span, :] = vert
                ratio_above = vert * inverse
            else:
                vert_ref[k, span, :] = jnp.zeros_like(inverse)
            vert_above, flux_above = vert, flux
    for chunk in outs:
        for copy in chunk:
            copy.start()
    for chunk in outs:
        for copy in chunk:
            copy.wait()


def slot_places(ids, width):
    shift = width.bit_length() - 1
    row = ids >> shift
    low = ROW_BLOCK.bit_length() - 1
    return row & (ROW_BLOCK - 1), (row >> low) * width + (ids & (width - 1))


def one_hot(ids, count):
    place = lax.broadcasted_iota(jnp.int32, (count, ids.shape[1]), 0)
    return (place == ids).astype(F32).astype(BF16)


def middle_kernel(
    slots_ref, h_hbm, res_hbm, inv_hbm, vert_hbm,
    alpha_hbm, n1_hbm, half_m_hbm, ksat_hbm, room_hbm, sat_hbm,
    head_ref, cond_ref, stor_ref, source_ref, sink_ref, row_even_ref, row_odd_ref, lane_ref,
    total, left_a, left_b, hot_a, hot_b,
    h_ref, res_ref, inv_ref, vert_ref,
    alpha_ref, n1_ref, half_m_ref, ksat_ref, room_ref, sat_ref, sems,
):
    layers, rows, width = h_ref.shape
    peers, fields, per_peer = slots_ref.shape
    roots = fields - 2
    values = fields - 1
    blocks = rows // ROW_BLOCK
    half = values * ROW_BLOCK
    group = left_a.shape[1] // per_peer
    steps = peers // group
    loads = [
        pltpu.make_async_copy(a, b, sems.at[i])
        for i, (a, b) in enumerate(
            [
                (res_hbm, res_ref), (inv_hbm, inv_ref), (vert_hbm, vert_ref), (h_hbm, h_ref),
                (alpha_hbm, alpha_ref), (n1_hbm, n1_ref), (half_m_hbm, half_m_ref),
                (ksat_hbm, ksat_ref), (room_hbm, room_ref), (sat_hbm, sat_ref),
            ]
        )
    ]
    for copy in loads:
        copy.start()
    total[...] = jnp.zeros_like(total)

    def build(step, left, hot):
        for g in range(group):
            block = slots_ref[step * group + g]
            at = slice(g * per_peer, (g + 1) * per_peer)
            row, column = slot_places(block[values : values + 1, :].astype(jnp.int32), width)
            hot[:, at] = one_hot(column, blocks * width)
            mask = lax.broadcasted_iota(jnp.int32, (ROW_BLOCK, per_peer), 0) == row
            high = block.astype(BF16).astype(F32)
            low = block - high
            for f in range(values):
                for base, part in ((0, high), (half, low)):
                    first = base + f * ROW_BLOCK
                    left[first : first + ROW_BLOCK, at] = jnp.where(
                        mask, part[f : f + 1, :], 0.0
                    ).astype(BF16)

    def add(left, hot):
        total[...] += lax.dot_general(
            left[...], hot[...], (((1,), (1,)), ((), ())), preferred_element_type=F32
        )

    build(0, left_a, hot_a)

    def place(pair, carry):
        build(2 * pair + 1, left_b, hot_b)
        add(left_a, hot_a)
        build(jnp.minimum(2 * pair + 2, steps - 1), left_a, hot_a)
        add(left_b, hot_b)
        return carry

    lax.fori_loop(0, steps // 2, place, 0)
    for copy in loads:
        copy.wait()

    def grid(f, b):
        at = f * ROW_BLOCK
        cols = slice(b * width, (b + 1) * width)
        return total[at : at + ROW_BLOCK, cols] + total[half + at : half + at + ROW_BLOCK, cols]

    even = lax.rem(lax.axis_index("bx"), 2) == 0
    lanes = lax.broadcasted_iota(jnp.int32, (ROW_BLOCK, width), 1)
    for b in range(blocks):
        span = slice(b * ROW_BLOCK, (b + 1) * ROW_BLOCK)
        value = None
        for k in range(layers):
            residual = res_ref[k, span, :]
            if k < roots:
                sink = grid(k, b)
                sink_ref[k, span, :] = sink
                if k == 0:
                    sink = sink - grid(roots, b)
                source_ref[k, span, :] = sink
                residual = residual + sink
            target = -residual
            if k:
                target = target + vert_ref[k - 1, span, :] * value
            value = target * inv_ref[k, span, :]
            head_ref[k, span, :] = value
        change = value
        head_ref[layers - 1, span, :] = h_ref[layers - 1, span, :] + change
        for k in range(layers - 2, -1, -1):
            ratio = vert_ref[k, span, :] * inv_ref[k, span, :]
            change = head_ref[k, span, :] + ratio * change
            head_ref[k, span, :] = h_ref[k, span, :] + change
    for b in range(blocks):
        span = slice(b * ROW_BLOCK, (b + 1) * ROW_BLOCK)
        packed = jnp.zeros((ROW_BLOCK, width), F32)
        for k in range(layers):
            head = head_ref[k, span, :]
            room = room_ref[k, span, :]
            saturation, conduct, storage = closure(
                head, alpha_ref[k, span, :], n1_ref[k, span, :], half_m_ref[k, span, :],
                ksat_ref[k, span, :], room,
            )
            cond_ref[k, span, :] = conduct
            stor_ref[k, span, :] = storage
            source = room * (saturation - sat_ref[k, span, :])
            if k < roots:
                source = source + source_ref[k, span, :]
            source_ref[k, span, :] = source
            packed = edge_messages((head, conduct), k, lanes, packed)
        lane_ref[span, :] = packed
    store_rows(head_ref, cond_ref, even, row_even_ref, row_odd_ref)


def last_kernel(
    slots_ref, old_head_ref, cond_ref, stor_ref, source_ref, sink_ref,
    alpha_hbm, n1_hbm, half_m_hbm,
    row_even_ref, row_odd_ref, own_ref, lane_even_ref, lane_odd_ref,
    head_hbm, reply_ref,
    head_pad, cond_pad, head_ref, ratio_ref, value_ref, alpha_ref, n1_ref, half_m_ref,
    halo_ref, stress_ref, sems,
):
    layers, rows, width = head_ref.shape
    peers, fields, per_peer = slots_ref.shape
    roots = fields - 2
    blocks = rows // ROW_BLOCK
    loads = [
        pltpu.make_async_copy(a, b, sems.at[i])
        for i, (a, b) in enumerate(
            [(alpha_hbm, alpha_ref), (n1_hbm, n1_ref), (half_m_hbm, half_m_ref)]
        )
    ]
    for copy in loads:
        copy.start()
    fill_pads(old_head_ref, cond_ref, row_even_ref, row_odd_ref, head_pad, cond_pad)
    halo_ref[...] = lane_halo(own_ref[...], lane_even_ref[...], lane_odd_ref[...])
    size = HALF if rows % HALF == 0 else rows
    lanes = lax.broadcasted_iota(jnp.int32, (size, width), 1)
    for top in range(0, rows, size):
        span = slice(top, top + size)
        halo = halo_ref[span, :]
        vert_above = flux_above = ratio_above = value = None
        for k in range(layers):
            head, conduct, flow, faces = lateral_terms(
                k, top, size, head_pad, cond_pad, halo, lanes
            )
            diagonal = stor_ref[k, span, :] + faces
            if k < layers - 1:
                vert = VERTICAL * (conduct + cond_ref[k + 1, span, :])
                flux = vert * (head - old_head_ref[k + 1, span, :] + 1.0)
                diagonal = diagonal + vert
            else:
                vert = None
                flux = conduct * (2.0 * VERTICAL)
            residual = flux + flow + source_ref[k, span, :]
            if k:
                residual = residual - flux_above
                diagonal = diagonal + vert_above
                diagonal = diagonal - vert_above * ratio_above
                value = (vert_above * value - residual) * (inverse := 1.0 / diagonal)
            else:
                value = -residual * (inverse := 1.0 / diagonal)
            value_ref[k, span, :] = value
            if vert is not None:
                ratio_above = vert * inverse
                ratio_ref[k, span, :] = ratio_above
            vert_above, flux_above = vert, flux
        if top == 0:
            for copy in loads:
                copy.wait()
        change = value
        head_ref[layers - 1, span, :] = old_head_ref[layers - 1, span, :] + change
        numer = denom = None
        for k in range(layers - 2, -1, -1):
            change = value_ref[k, span, :] + ratio_ref[k, span, :] * change
            head = old_head_ref[k, span, :] + change
            head_ref[k, span, :] = head
            if k < roots:
                half = powers(
                    head, alpha_ref[k, span, :], n1_ref[k, span, :], half_m_ref[k, span, :]
                )[2]
                sink = sink_ref[k, span, :]
                term = sink * jnp.exp2(half + half)
                numer = term if numer is None else numer + term
                denom = sink if denom is None else denom + sink
        held = denom > 0.0
        stress_ref[span, :] = jnp.where(held, numer / jnp.where(held, denom, 1.0), 0.0)
    leave = pltpu.make_async_copy(head_ref, head_hbm, sems.at[3])
    leave.start()
    wide = jnp.concatenate(
        [stress_ref[b * ROW_BLOCK : (b + 1) * ROW_BLOCK, :] for b in range(blocks)], 1
    )
    high = wide.astype(BF16)
    both = jnp.concatenate([high, (wide - high.astype(F32)).astype(BF16)], 0)

    def answer(block, carry):
        for g in range(UNROLL):
            peer = block * UNROLL + g
            ids = slots_ref[peer, fields - 1 : fields, :].astype(jnp.int32)
            row, column = slot_places(ids, width)
            hot = one_hot(column, blocks * width)
            found = jnp.dot(both, hot, preferred_element_type=F32)
            found = found[:ROW_BLOCK] + found[ROW_BLOCK:]
            mask = lax.broadcasted_iota(jnp.int32, (ROW_BLOCK, per_peer), 0) == row
            reply_ref[pl.ds(peer, 1), :] = jnp.sum(
                jnp.where(mask, found, 0.0), 0, keepdims=True
            )
        return carry

    lax.fori_loop(0, peers // UNROLL, answer, 0)
    leave.wait()


def swaps(size):
    even = [(i, i ^ 1) for i in range(size)]
    odd = [(i, (i + 1) % size if i % 2 else (i - 1) % size) for i in range(size)]
    return even, odd


def exchange(row_even, row_odd, packed):
    even_x, odd_x = swaps(lax.axis_size("bx"))
    even_y, odd_y = swaps(lax.axis_size("by"))
    return (
        lax.ppermute(row_even, "bx", even_x),
        lax.ppermute(row_odd, "bx", odd_x),
        packed,
        lax.ppermute(packed, "by", even_y),
        lax.ppermute(packed, "by", odd_y),
    )


VMEM = pltpu.VMEM
HBM = pltpu.HBM


def call(kernel, ins, outs, scratch, name):
    return pl.pallas_call(
        kernel,
        in_specs=[pl.BlockSpec(memory_space=m) for m in ins],
        out_specs=[pl.BlockSpec(memory_space=m) for _, m in outs],
        out_shape=[
            HBM(s, F32) if m is HBM else jax.ShapeDtypeStruct(s, F32) for s, m in outs
        ],
        scratch_shapes=scratch,
        name=name,
        compiler_params=pltpu.CompilerParams(vmem_limit_bytes=20 * MIB),
    )


def in_hbm(*arrays):
    return [pltpu.with_memory_space_constraint(a, HBM) for a in arrays]


def prepare(root_fraction, transpiration, infiltration, clump_cell, peers, per_peer):
    roots, slot_count = root_fraction.shape
    steps = 4 if peers % 4 == 0 else 1
    span = slot_count // steps
    line = pl.BlockSpec((1, span), lambda i: (0, i))
    return pl.pallas_call(
        prepare_kernel,
        grid=(steps,),
        in_specs=[pl.BlockSpec((roots, span), lambda i: (0, i)), line, line, line],
        out_specs=pl.BlockSpec((peers // steps, roots + 2, per_peer), lambda i: (i, 0, 0)),
        out_shape=jax.ShapeDtypeStruct((peers, roots + 2, per_peer), F32),
        name="prepare",
        compiler_params=pltpu.CompilerParams(vmem_limit_bytes=4 * MIB),
    )(*in_hbm(root_fraction, transpiration[None], infiltration[None], clump_cell[None]))


def on_device(
    h_old,
    soil_type,
    ks_scale,
    soil_table,
    clump_brick,
    clump_cell,
    root_fraction,
    transpiration,
    infiltration,
):
    layers, rows, width = h_old.shape
    peers = lax.axis_size("bx") * lax.axis_size("by")
    roots, slot_count = root_fraction.shape
    per_peer = slot_count // peers
    cells = (layers, rows, width)
    row_msg = (2, layers, width)
    lane_msg = (rows, width)
    axes = ("bx", "by")
    on_chip = lambda *shapes: [(s, VMEM) for s in shapes]
    buffers = lambda n: [VMEM(cells, F32)] * n
    semaphores = pltpu.SemaphoreType.DMA
    chunks = len(layer_chunks(layers))

    slots = lax.all_to_all(
        prepare(root_fraction, transpiration, infiltration, clump_cell, peers, per_peer),
        axes,
        split_axis=0,
        concat_axis=0,
        tiled=True,
    )
    table = jnp.pad(soil_table, ((0, 0), (0, width - soil_table.shape[1])))
    alpha, n1, half_m, ksat, room, sat, head, conduct, storage, row_even, row_odd, packed = call(
        first_kernel,
        [HBM] * 3 + [VMEM],
        [(cells, HBM)] * 6 + on_chip(cells, cells, cells, row_msg, row_msg, lane_msg),
        [VMEM(cells, jnp.int32)] + buffers(7) + [semaphores((3 * chunks,)), semaphores((6 * chunks,))],
        "first",
    )(*in_hbm(h_old, soil_type, ks_scale), table)
    pads = [VMEM((layers, rows + 2 * PAD, width), F32)] * 2
    residual, inverse, vert = call(
        factor_kernel,
        [VMEM] * 8,
        [(cells, HBM)] * 3,
        pads + buffers(3) + [VMEM(lane_msg, F32), semaphores((3 * chunks,))],
        "factor",
    )(head, conduct, storage, *exchange(row_even, row_odd, packed))
    values = roots + 1
    columns = rows // ROW_BLOCK * width
    group = GROUP if peers % (2 * GROUP) == 0 else 1
    lefts = [VMEM((2 * values * ROW_BLOCK, group * per_peer), BF16)] * 2
    hots = [VMEM((columns, group * per_peer), BF16)] * 2
    head, conduct, storage, source, sink, row_even, row_odd, packed = call(
        middle_kernel,
        [VMEM] + [HBM] * 10,
        on_chip(*[cells] * 4, (roots, rows, width), row_msg, row_msg, lane_msg),
        [VMEM((2 * values * ROW_BLOCK, columns), F32)] + lefts + hots
        + buffers(10) + [semaphores((10,))],
        "middle",
    )(slots, *in_hbm(h_old, residual, inverse, vert, alpha, n1, half_m, ksat, room, sat))
    head, reply = call(
        last_kernel,
        [VMEM] * 6 + [HBM] * 3 + [VMEM] * 5,
        [(cells, HBM), ((peers, per_peer), VMEM)],
        pads + buffers(6) + [VMEM(lane_msg, F32)] * 2 + [semaphores((4,))],
        "last",
    )(
        slots, head, conduct, storage, source, sink, *in_hbm(alpha, n1, half_m),
        *exchange(row_even, row_odd, packed),
    )
    stress = lax.all_to_all(reply, axes, split_axis=0, concat_axis=0, tiled=True)
    return head, stress.reshape(slot_count)


def solution(mesh):
    placed = (
        P(None, "bx", "by"),
        P(None, "bx", "by"),
        P(None, "bx", "by"),
        P(),
        P(("bx", "by")),
        P(("bx", "by")),
        P(None, ("bx", "by")),
        P(("bx", "by")),
        P(("bx", "by")),
    )
    return jax.shard_map(
        on_device,
        mesh=mesh,
        in_specs=placed,
        out_specs=(P(None, "bx", "by"), P(("bx", "by"))),
        check_vma=False,
    )
```

time: 77.1 us -> 58.7 us (0.76)
  local copies, waits for them, and re-layouts: 15 us -> 0.66 us
  Pallas kernels: 25.2 us -> 23.1 us
  other arithmetic: 1.98 us -> 0 us
  waiting for transfers between devices: 4.95 us -> 6.04 us
    unnamed x42 -> x3, local copies, waits for them, and re-layouts: 14.7 us -> 0.62 us
    pallas_call x4 -> x5, Pallas kernels: 25.2 us -> 23.1 us  [the longest x1 7.32 us: on_device(): call(middle_kernel, [VMEM] + [HBM] * 10, on_chip(*[cells] * 4, (roots, ro...]
    ppermute x2, waiting for transfers between devices: 0.69 us -> 2.74 us  [exchange(): lax.ppermute(packed, 'by', odd_y)]
    mul x1 -> x0, other arithmetic: 1.09 us -> none  [on_device(): root_fraction * transpiration[None]]
    ppermute x2, waiting for transfers between devices: 0.97 us -> 0.01 us  [exchange(): lax.ppermute(packed, 'by', even_y)]
    transpose x1 -> x0, other arithmetic: 0.88 us -> none  [on_device(): forcing.reshape(fields, peers, per_peer).transpose(1, 0, 2)]
  transfers between devices with their start and end apart: 9 -> 9, of which waited for: 5 -> 4; matrix products, arithmetic and copies ran while one was open for 0% -> 0% of each run, Pallas kernels for 6% -> 14%
where the time goes in v1:
time: 58.7 us; the launch traced here: 58.4 us
  Pallas kernels  23.1 us (39%)
  starting transfers between devices  17.2 us (29%)
  blocking collectives  10.6 us (18%)
  waiting for transfers between devices  6.04 us (10%)
  between operations  0.71 us (1%)
  local copies, waits for them, and re-layouts  0.66 us (1%)
    all_to_all x1, blocking collectives, on_device(): lax.all_to_all(reply, axes, split_axis=0, concat_axis=0, tiled=True)  10.6 us
    all_to_all x1, starting transfers between devices, on_device(): lax.all_to_all(prepare(root_fraction, transpiration, infiltration, clump_...  7.33 us
    pallas_call x1, Pallas kernels, on_device(): call(middle_kernel, [VMEM] + [HBM] * 10, on_chip(*[cells] * 4, (roots, ro...  7.32 us
    ppermute x2, starting transfers between devices, exchange(): lax.ppermute(packed, 'by', odd_y)  6.65 us
    pallas_call x1, Pallas kernels, on_device(): call(first_kernel, [HBM] * 3 + [VMEM], [(cells, HBM)] * 6 + on_chip(cells...  5.47 us
    pallas_call x1, Pallas kernels, on_device(): call(last_kernel, [VMEM] * 6 + [HBM] * 3 + [VMEM] * 5, [(cells, HBM), ((p...  4.44 us
    ppermute x2, waiting for transfers between devices, exchange(): lax.ppermute(row_odd, 'bx', odd_x)  3.29 us
    pallas_call x1, Pallas kernels, prepare(): pl.pallas_call(prepare_kernel, grid=(steps,), in_specs=[pl.BlockSpec((roo...  3.26 us
  transfers between devices with their start and end apart: 9, of which 4 were waited for; matrix products, arithmetic and copies ran while one was open for 0% of the time, Pallas kernels for 14%

profile of v1, /device:TPU:0, one launch (start us, length us, event | category | flops | bytes accessed | tf_op | source)
XLA Modules:
  0.0 58.4 jit_solution(14859094432455715510)
XLA Ops:
  0.6 3.3 %prepare.1 = f32[32,16,256]{2,1,0:T(8,128)} custom-call(f32[14,8192]{1,0:T(8,128)} %root_ref.1, f32[1,8192]{1,0:T(1,128)} %bitcast.7, f32[1,8192]{1,0:T(1,128)} %bitcast.8, s32[1,8192]{1,0:T(1,128)} %bitcast.9), custom_call_target="tpu_custom_call" | custom-call | tf_op jit(solution)/shard_map/prepare/pallas_call | solution.py:537
  3.9 0.0 copy-start
  3.9 7.3 %all-to-all-start = ((f32[32,16,256]{2,1,0:T(8,128)}), f32[32,16,256]{2,1,0:T(8,128)S(1)}, u32[]{:S(2)}, u32[]{:S(2)}) async-start(f32[32,16,256]{2,1,0:T(8,128)} %prepare.1), calls=%async_computation | async-start | bytes 1048576 | tf_op jit(solution)/shard_map/all_to_all | solution.py:572
  11.2 0.0 copy-done
  11.2 5.5 %first.1 = (f32[20,64,128]{2,1,0:T(8,128)}, f32[20,64,128]{2,1,0:T(8,128)}, f32[20,64,128]{2,1,0:T(8,128)}, f32[20,64,128]{2,1,0:T(8,128)}, f32[20,64,128]{2,1,0...) custom-call(f32[20,64,128]{2,1,0:T(8,128)} %h_hbm.3, ...), custom_call_target="tpu_custom_call" | custom-call | tf_op jit(solution)/shard_map/first/pallas_call | solution.py:580
  16.7 4.6 %collective-permute-start.3 = (f32[64,128]{1,0:T(8,128)S(1)}, f32[64,128]{1,0:T(8,128)S(1)}, u32[]{:S(2)}, u32[]{:S(2)}) collective-permute-start(f32[64,128]{1,0:T(8,128)S(1)} %get-tuple-element.32.own_ref), channel_id=1, source_target_pairs={{0,7},{1,2},{2,1},{3,4},{4,3},{5,6},{6,5},{7,0},{8,15},{9,10},{10,... | collective-permute-start | bytes 98312 | tf_op jit(solution)/shard_map/ppermute | solution.py:506
  21.3 0.0 collective-permute-start.2
  21.3 0.0 collective-permute-start
  21.3 1.6 %collective-permute-start.1 = (f32[2,20,128]{2,1,0:T(8,128)S(1)}, f32[2,20,128]{2,1,0:T(8,128)S(1)}, u32[]{:S(2)}, u32[]{:S(2)}) collective-permute-start(f32[2,20,128]{2,1,0:T(8,128)S(1)} %get-tuple-element.31), channel_id=1, source_target_pairs={{0,24},{8,16},{16,8},{24,0},{1,25},{9,17},{17,9},{25,1},{2,26},{10... | collective-permute-start | bytes 61448 | tf_op jit(solution)/shard_map/ppermute | solution.py:503
  22.9 0.0 collective-permute-done.row_even_ref
  22.9 1.6 %collective-permute-done.1.row_odd_ref = f32[2,20,128]{2,1,0:T(8,128)S(1)} collective-permute-done((f32[2,20,128]{2,1,0:T(8,128)S(1)}, f32[2,20,128]{2,1,0:T(8,128)S(1)}, u32[]{:S(2)}, u32[]{:S(2)}) %collective-permute-start.1) | collective-permute-done | bytes 20512 | tf_op jit(solution)/shard_map/ppermute | solution.py:503
  24.6 1.4 %collective-permute-done.3.lane_odd_ref = f32[64,128]{1,0:T(8,128)S(1)} collective-permute-done((f32[64,128]{1,0:T(8,128)S(1)}, f32[64,128]{1,0:T(8,128)S(1)}, u32[]{:S(2)}, u32[]{:S(2)}) %collective-permute-start.3) | collective-permute-done | bytes 32800 | tf_op jit(solution)/shard_map/ppermute | solution.py:506
  26.0 0.0 collective-permute-done.2.lane_even_ref
  26.0 2.7 %factor.1 = (f32[20,64,128]{2,1,0:T(8,128)}, f32[20,64,128]{2,1,0:T(8,128)}, f32[20,64,128]{2,1,0:T(8,128)}) custom-call(f32[20,64,128]{2,1,0:T(8,128)S(1)} %get-tuple-element.27.h_ref, f32[20,64,128]{2,1,0:T(8,128)S(1)} %get-tuple-element.28.cond_ref, f32[20,64,128]{2,1,0:T(8,128)S(1)} %get-tuple-element.29.stor_ref, ...), custom_call_target="tpu_custom_call" | custom-call | tf_op jit(solution)/shard_map/factor/pallas_call | solution.py:588
  28.6 0.0 all-to-all-done.slots_ref
  28.6 7.3 %middle.1 = (f32[20,64,128]{2,1,0:T(8,128)S(1)}, f32[20,64,128]{2,1,0:T(8,128)S(1)}, f32[20,64,128]{2,1,0:T(8,128)S(1)}, f32[20,64,128]{2,1,0:T(8,128)S(1)}, f32...) custom-call(f32[32,16,256]{2,1,0:T(8,128)S(1)} %all-to-all-done.slots_re, ...), custom_call_target="tpu_custom_call" | custom-call | tf_op jit(solution)/shard_map/middle/pallas_call | solution.py:600
  36.0 2.0 %collective-permute-start.7 = (f32[64,128]{1,0:T(8,128)S(1)}, f32[64,128]{1,0:T(8,128)S(1)}, u32[]{:S(2)}, u32[]{:S(2)}) collective-permute-start(f32[64,128]{1,0:T(8,128)S(1)} %get-tuple-element.49.own_ref), channel_id=1, source_target_pairs={{0,7},{1,2},{2,1},{3,4},{4,3},{5,6},{6,5},{7,0},{8,15},{9,10},{10,... | collective-permute-start | bytes 98312 | tf_op jit(solution)/shard_map/ppermute | solution.py:506
  38.0 0.0 collective-permute-start.6
  38.0 0.0 collective-permute-start.4
  38.0 1.6 %collective-permute-start.5 = (f32[2,20,128]{2,1,0:T(8,128)S(1)}, f32[2,20,128]{2,1,0:T(8,128)S(1)}, u32[]{:S(2)}, u32[]{:S(2)}) collective-permute-start(f32[2,20,128]{2,1,0:T(8,128)S(1)} %get-tuple-element.48), channel_id=1, source_target_pairs={{0,24},{8,16},{16,8},{24,0},{1,25},{9,17},{17,9},{25,1},{2,26},{10... | collective-permute-start | bytes 61448 | tf_op jit(solution)/shard_map/ppermute | solution.py:503
  39.6 0.0 collective-permute-done.4.row_even_ref
  39.6 1.6 %collective-permute-done.5.row_odd_ref = f32[2,20,128]{2,1,0:T(8,128)S(1)} collective-permute-done((f32[2,20,128]{2,1,0:T(8,128)S(1)}, f32[2,20,128]{2,1,0:T(8,128)S(1)}, u32[]{:S(2)}, u32[]{:S(2)}) %collective-permute-start.5) | collective-permute-done | bytes 20512 | tf_op jit(solution)/shard_map/ppermute | solution.py:503
  41.3 1.4 %collective-permute-done.7.lane_odd_ref = f32[64,128]{1,0:T(8,128)S(1)} collective-permute-done((f32[64,128]{1,0:T(8,128)S(1)}, f32[64,128]{1,0:T(8,128)S(1)}, u32[]{:S(2)}, u32[]{:S(2)}) %collective-permute-start.7) | collective-permute-done | bytes 32800 | tf_op jit(solution)/shard_map/ppermute | solution.py:506
  42.6 0.0 collective-permute-done.6.lane_even_ref
  42.6 4.4 %last.1 = (f32[20,64,128]{2,1,0:T(8,128)}, f32[32,256]{1,0:T(8,128)S(1)}) custom-call(f32[32,16,256]{2,1,0:T(8,128)S(1)} %all-to-all-done.slots_ref, f32[20,64,128]{2,1,0:T(8,128)S(1)} %get-tuple-element.42.old_head_ref, f32[20,64,128]{2,1,0:T(8,128)S(1)} %get-tuple-element.43.cond_ref, f32[20,64,128]{2,1,0:T(8,128)S(1)} %get-tuple-element.44.stor_ref, ...), custom_call_target="tpu_custom_call" | custom-call | tf_op jit(solution)/shard_map/last/pallas_call | solution.py:608
  47.1 10.6 %all_to_all.14 = f32[32,1,256]{2,1,0:T(1,128)S(1)} all-to-all(f32[32,1,256]{2,1,0:T(1,128)S(1)} %copy.10), channel_id=1, replica_groups=mesh['bx'=4,'by'=8] {'bx','by'}, dimensions={0} | all-to-all | bytes 65536 | tf_op jit(solution)/shard_map/all_to_all | solution.py:618
  57.8 0.6 %copy.12 = f32[8192]{0:T(1024)} copy(f32[8192]{0:T(1024)S(1)} %bitcast.6) | data formatting | bytes 65536
  (2 shorter events, 0.0 us)
Async XLA Ops:
  3.9 7.3 %copy-start = (f32[4,12]{1,0:T(4,128)S(1)}, f32[4,12]{1,0:T(4,128)}, u32[]{:S(2)}) copy-start(f32[4,12]{1,0:T(4,128)} %param.12) | copy-start | bytes 580
  3.9 24.7 %all-to-all-start = ((f32[32,16,256]{2,1,0:T(8,128)}), f32[32,16,256]{2,1,0:T(8,128)S(1)}, u32[]{:S(2)}, u32[]{:S(2)}) async-start(f32[32,16,256]{2,1,0:T(8,128)} %prepare.1), calls=%async_computation | async-start | bytes 1048576 | tf_op jit(solution)/shard_map/all_to_all | solution.py:572
  16.7 9.2 %collective-permute-start.3 = (f32[64,128]{1,0:T(8,128)S(1)}, f32[64,128]{1,0:T(8,128)S(1)}, u32[]{:S(2)}, u32[]{:S(2)}) collective-permute-start(f32[64,128]{1,0:T(8,128)S(1)} %get-tuple-element.32.own_ref), channel_id=1, source_target_pairs={{0,7},{1,2},{2,1},{3,4},{4,3},{5,6},{6,5},{7,0},{8,15},{9,10},{10,... | collective-permute-start | bytes 98312 | tf_op jit(solution)/shard_map/ppermute | solution.py:506
  21.3 4.6 %collective-permute-start.2 = (f32[64,128]{1,0:T(8,128)S(1)}, f32[64,128]{1,0:T(8,128)S(1)}, u32[]{:S(2)}, u32[]{:S(2)}) collective-permute-start(f32[64,128]{1,0:T(8,128)S(1)} %get-tuple-element.32.own_ref), channel_id=1, source_target_pairs={{0,1},{1,0},{2,3},{3,2},{4,5},{5,4},{6,7},{7,6},{8,9},{9,8},{10,11... | collective-permute-start | bytes 98312 | tf_op jit(solution)/shard_map/ppermute | solution.py:505
  21.3 1.6 %collective-permute-start = (f32[2,20,128]{2,1,0:T(8,128)S(1)}, f32[2,20,128]{2,1,0:T(8,128)S(1)}, u32[]{:S(2)}, u32[]{:S(2)}) collective-permute-start(f32[2,20,128]{2,1,0:T(8,128)S(1)} %get-tuple-element.30), channel_id=1, source_target_pairs={{0,8},{8,0},{16,24},{24,16},{1,9},{9,1},{17,25},{25,17},{2,10},{10... | collective-permute-start | bytes 61448 | tf_op jit(solution)/shard_map/ppermute | solution.py:502
  21.3 3.3 %collective-permute-start.1 = (f32[2,20,128]{2,1,0:T(8,128)S(1)}, f32[2,20,128]{2,1,0:T(8,128)S(1)}, u32[]{:S(2)}, u32[]{:S(2)}) collective-permute-start(f32[2,20,128]{2,1,0:T(8,128)S(1)} %get-tuple-element.31), channel_id=1, source_target_pairs={{0,24},{8,16},{16,8},{24,0},{1,25},{9,17},{17,9},{25,1},{2,26},{10... | collective-permute-start | bytes 61448 | tf_op jit(solution)/shard_map/ppermute | solution.py:503
  36.0 6.7 %collective-permute-start.7 = (f32[64,128]{1,0:T(8,128)S(1)}, f32[64,128]{1,0:T(8,128)S(1)}, u32[]{:S(2)}, u32[]{:S(2)}) collective-permute-start(f32[64,128]{1,0:T(8,128)S(1)} %get-tuple-element.49.own_ref), channel_id=1, source_target_pairs={{0,7},{1,2},{2,1},{3,4},{4,3},{5,6},{6,5},{7,0},{8,15},{9,10},{10,... | collective-permute-start | bytes 98312 | tf_op jit(solution)/shard_map/ppermute | solution.py:506
  38.0 4.6 %collective-permute-start.6 = (f32[64,128]{1,0:T(8,128)S(1)}, f32[64,128]{1,0:T(8,128)S(1)}, u32[]{:S(2)}, u32[]{:S(2)}) collective-permute-start(f32[64,128]{1,0:T(8,128)S(1)} %get-tuple-element.49.own_ref), channel_id=1, source_target_pairs={{0,1},{1,0},{2,3},{3,2},{4,5},{5,4},{6,7},{7,6},{8,9},{9,8},{10,11... | collective-permute-start | bytes 98312 | tf_op jit(solution)/shard_map/ppermute | solution.py:505
  38.0 1.6 %collective-permute-start.4 = (f32[2,20,128]{2,1,0:T(8,128)S(1)}, f32[2,20,128]{2,1,0:T(8,128)S(1)}, u32[]{:S(2)}, u32[]{:S(2)}) collective-permute-start(f32[2,20,128]{2,1,0:T(8,128)S(1)} %get-tuple-element.47), channel_id=1, source_target_pairs={{0,8},{8,0},{16,24},{24,16},{1,9},{9,1},{17,25},{25,17},{2,10},{10... | collective-permute-start | bytes 61448 | tf_op jit(solution)/shard_map/ppermute | solution.py:502
  38.0 3.3 %collective-permute-start.5 = (f32[2,20,128]{2,1,0:T(8,128)S(1)}, f32[2,20,128]{2,1,0:T(8,128)S(1)}, u32[]{:S(2)}, u32[]{:S(2)}) collective-permute-start(f32[2,20,128]{2,1,0:T(8,128)S(1)} %get-tuple-element.48), channel_id=1, source_target_pairs={{0,24},{8,16},{16,8},{24,0},{1,25},{9,17},{17,9},{25,1},{2,26},{10... | collective-permute-start | bytes 61448 | tf_op jit(solution)/shard_map/ppermute | solution.py:503

commit v2 on v1

v2 whole, which is shorter than its diff:
```python
import jax
import jax.numpy as jnp
from jax import lax
from jax.experimental import pallas as pl
from jax.experimental.pallas import tpu as pltpu
from jax.sharding import PartitionSpec as P

ITERS = 2
RESIDUAL_WATER = 0.05
STORAGE = 0.2
TIME_STEP = 0.5
LATERAL = 0.5
TINY = 1e-30
ROW_BLOCK = 32
HALF = 32
UNROLL = 8
GROUP = 4
LOG2E = 1.4426950408889634
PAD = 8
F32 = jnp.float32
BF16 = jnp.bfloat16
MIB = 1 << 20
VMEM = pltpu.VMEM
HBM = pltpu.HBM


def lane_tables(table, shape):
    t0, t1, t2, t3 = (table[i : i + 1, :] for i in range(4))
    alpha = 4.0 * t0
    n1 = 0.2 + 2.0 * t1
    half_m = 0.5 * n1 / (1.0 + n1)
    ks3 = (0.5 * LATERAL * 3.0) * t2
    room = ((0.3 - RESIDUAL_WATER) + 0.3 * t3) * (1.0 / TIME_STEP)
    rows = (alpha, LOG2E * n1, -LOG2E * half_m, ks3, room)
    return [jnp.broadcast_to(r, shape) for r in rows]


def powers(head, alpha, n1, half_m):
    suction = jnp.maximum(alpha * jnp.maximum(-head, 0.0), TINY)
    power = jnp.exp2(n1 * lax.log(suction))
    log_base = lax.log(1.0 + suction * power)
    return power, log_base, half_m * log_base


def closure(head, alpha, n1, half_m, ksat, room):
    power, log_base, half = powers(head, alpha, n1, half_m)
    root = jnp.exp2(half)
    saturation = root * root
    share = power * saturation
    inner = 1.0 - share
    conduct = (ksat * root) * (inner * inner)
    cap = (room * (1.0 / LOG2E)) * (n1 * alpha)
    storage = STORAGE / TIME_STEP + cap * (share * jnp.exp2(-LOG2E * log_base))
    return saturation, conduct, storage


def lane_lookup(row, index):
    return jnp.take_along_axis(row, index, axis=1, mode="promise_in_bounds")


def conductivity(head, alpha, n1, half_m, ksat):
    power, _, half = powers(head, alpha, n1, half_m)
    root = jnp.exp2(half)
    inner = 1.0 - power * (root * root)
    return (ksat * root) * (inner * inner)


def edge_lanes(values, k, layers, lanes, packed):
    for part, value in enumerate(values):
        at = 2 * (part * layers + k)
        moved = pltpu.roll(value, at + 1, 1)
        packed = jnp.where((lanes == at) | (lanes == at + 1), moved, packed)
    return packed


def edge_rows(refs, row_even_ref, row_odd_ref):
    even = lax.rem(lax.axis_index("bx"), 2) == 0
    for part, ref in enumerate(refs):
        rows = ref.shape[1]
        low = ref[:, 0, :].astype(F32)
        high = ref[:, rows - 1, :].astype(F32)
        row_even_ref[part] = jnp.where(even, high, low)
        row_odd_ref[part] = jnp.where(even, low, high)


def row_halo(own_even, own_odd, row_even, row_odd):
    index = lax.axis_index("bx")
    even = lax.rem(index, 2) == 0
    low = jnp.where(even, row_odd, row_even)
    high = jnp.where(even, row_even, row_odd)
    own_low = jnp.where(even, own_odd, own_even)
    own_high = jnp.where(even, own_even, own_odd)
    low = jnp.where(index == 0, own_low, low)
    high = jnp.where(index == lax.axis_size("bx") - 1, own_high, high)
    return low, high


def lane_halo(own, lane_even, lane_odd):
    index = lax.axis_index("by")
    even = lax.rem(index, 2) == 0
    width = own.shape[1]
    lanes = lax.broadcasted_iota(jnp.int32, own.shape, 1)
    low = jnp.where(even, lane_odd, lane_even)
    high = jnp.where(even, lane_even, lane_odd)
    low = jnp.where(index == 0, pltpu.roll(own, width - 1, 1), low)
    high = jnp.where(index == lax.axis_size("by") - 1, pltpu.roll(own, 1, 1), high)
    return jnp.where(lax.rem(lanes, 2) == 0, low, pltpu.roll(high, width - 2, 1))


def edge_signs(shape):
    x, y = lax.axis_index("bx"), lax.axis_index("by")
    minus = lambda at_edge: jnp.where(at_edge, -1.0, 1.0)
    lanes = lax.broadcasted_iota(jnp.int32, shape, 1)
    return (
        minus(x == 0),
        minus(x == lax.axis_size("bx") - 1),
        jnp.where(
            lax.rem(lanes, 2) == 0, minus(y == 0), minus(y == lax.axis_size("by") - 1)
        ),
    )


def prepare_kernel(
    root_hbm, transp_hbm, infil_hbm, cell_hbm, out_ref,
    root_ref, transp_ref, infil_ref, cell_ref, sems,
):
    peers, fields, per_peer = out_ref.shape
    roots = fields - 2
    steps = 4 if peers % 4 == 0 else 1
    span = peers // steps * per_peer
    lines = [
        pltpu.make_async_copy(a, b, sems.at[steps + i])
        for i, (a, b) in enumerate(
            [(transp_hbm, transp_ref), (infil_hbm, infil_ref), (cell_hbm, cell_ref)]
        )
    ]
    parts = [
        pltpu.make_async_copy(
            root_hbm.at[:, pl.ds(i * span, span)],
            root_ref.at[:, pl.ds(i * span, span)],
            sems.at[i],
        )
        for i in range(steps)
    ]
    for copy in lines + parts:
        copy.start()
    for copy in lines:
        copy.wait()
    for i, copy in enumerate(parts):
        copy.wait()
        for peer in range(i * peers // steps, (i + 1) * peers // steps):
            at = slice(peer * per_peer, (peer + 1) * per_peer)
            out_ref[peer, :roots, :] = root_ref[:, at] * transp_ref[:, at]
            out_ref[peer, roots : roots + 1, :] = infil_ref[:, at]
            out_ref[peer, roots + 1 :, :] = cell_ref[:, at].astype(F32)


def layer_chunks(layers):
    size = 5 if layers % 5 == 0 else layers
    return [(at, size) for at in range(0, layers, size)]


def copies(pairs, sems, layers):
    chunks = layer_chunks(layers)
    return [
        [
            pltpu.make_async_copy(
                a.at[pl.ds(at, size)], b.at[pl.ds(at, size)], sems.at[c * len(pairs) + i]
            )
            for i, (a, b) in enumerate(pairs)
        ]
        for c, (at, size) in enumerate(chunks)
    ]


def edges_kernel(
    h_hbm, soil_hbm, ks_hbm,
    h_ref, soil_ref, ks_ref, row_even_ref, row_odd_ref, lane_ref,
    sems,
):
    layers, rows, width = h_ref.shape
    ins = copies([(h_hbm, h_ref), (soil_hbm, soil_ref), (ks_hbm, ks_ref)], sems, layers)
    for chunk in ins:
        for copy in chunk:
            copy.start()
    lanes = lax.broadcasted_iota(jnp.int32, (rows, width), 1)
    packed = jnp.zeros((rows, width), F32)
    for (at, size), arrive in zip(layer_chunks(layers), ins):
        for copy in arrive:
            copy.wait()
        for k in range(at, at + size):
            packed = edge_lanes(
                (h_ref[k], soil_ref[k].astype(F32), ks_ref[k]), k, layers, lanes, packed
            )
    lane_ref[...] = packed
    edge_rows((h_ref, soil_ref, ks_ref), row_even_ref, row_odd_ref)


def lateral_terms(k, top, size, head_pad, cond_pad, halo_head, halo_cond, lanes):
    width = head_pad.shape[2]
    at = lambda pad, move: pad[k, PAD + top + move : PAD + top + move + size, :]
    head, conduct = at(head_pad, 0), at(cond_pad, 0)
    halo_head = pltpu.roll(halo_head, (width - 2 * k) % width, 1)
    halo_cond = pltpu.roll(halo_cond, (width - 2 * k) % width, 1)
    first = lanes == 0
    last = lanes == width - 1
    pairs = [
        (at(head_pad, -1), at(cond_pad, -1)),
        (at(head_pad, 1), at(cond_pad, 1)),
        (
            jnp.where(first, halo_head, pltpu.roll(head, 1, 1)),
            jnp.where(first, halo_cond, pltpu.roll(conduct, 1, 1)),
        ),
        (
            jnp.where(last, halo_head, pltpu.roll(head, width - 1, 1)),
            jnp.where(last, halo_cond, pltpu.roll(conduct, width - 1, 1)),
        ),
    ]
    flow = faces = None
    for other_head, other_cond in pairs:
        both = conduct + other_cond
        term = both * (head - other_head)
        flow = term if flow is None else flow + term
        faces = both if faces is None else faces + both
    return head, conduct, flow, faces


VERTICAL = 0.5 / (0.5 * LATERAL)


def first_kernel(
    h_ref, soil_ref, ks_ref, table_ref,
    alpha_hbm, n1_hbm, half_m_hbm, ksat_hbm, room_hbm, sat_ref, cond_ref, stor_ref,
    alpha_ref, n1_ref, half_m_ref, ksat_ref, room_ref, sems,
):
    layers, rows, width = h_ref.shape
    outs = copies(
        [
            (alpha_ref, alpha_hbm), (n1_ref, n1_hbm), (half_m_ref, half_m_hbm),
            (ksat_ref, ksat_hbm), (room_ref, room_hbm),
        ],
        sems,
        layers,
    )
    tables = lane_tables(table_ref[...], (8, width))
    for (at, size), leave in zip(layer_chunks(layers), outs):
        for k in range(at, at + size):
            for row in range(0, rows, 8):
                span = slice(row, row + 8)
                kind = soil_ref[k, span, :]
                alpha, n1, half_m, ks3, room = (lane_lookup(t, kind) for t in tables)
                ksat = ks3 * ks_ref[k, span, :]
                alpha_ref[k, span, :] = alpha
                n1_ref[k, span, :] = n1
                half_m_ref[k, span, :] = half_m
                ksat_ref[k, span, :] = ksat
                room_ref[k, span, :] = room
                saturation, conduct, storage = closure(
                    h_ref[k, span, :], alpha, n1, half_m, ksat, room
                )
                sat_ref[k, span, :] = saturation
                cond_ref[k, span, :] = conduct
                stor_ref[k, span, :] = storage
        for copy in leave:
            copy.start()
    for chunk in outs:
        for copy in chunk:
            copy.wait()


def factor_kernel(
    h_ref, cond_ref, stor_ref, table_ref,
    own_even_ref, own_odd_ref, row_even_ref, row_odd_ref, own_ref, lane_even_ref, lane_odd_ref,
    res_ref, inv_ref, vert_ref, row_par_ref, lane_par_ref,
    head_pad, cond_pad, halo_ref,
):
    layers, rows, width = h_ref.shape
    head_pad[:, PAD : PAD + rows, :] = h_ref[...]
    cond_pad[:, PAD : PAD + rows, :] = cond_ref[...]
    sign_low, sign_high, sign_lane = edge_signs((rows, width))
    kinds = lambda x: jnp.clip(x.astype(jnp.int32), 0, width - 1)
    for side, sign in ((0, sign_low), (1, sign_high)):
        head, kind, ks = (
            row_halo(own_even_ref[i], own_odd_ref[i], row_even_ref[i], row_odd_ref[i])[side]
            for i in range(3)
        )
        wide = lane_tables(table_ref[...], head.shape)[:4]
        pars = [lane_lookup(t, kinds(kind)) for t in wide]
        pars[3] = sign * (pars[3] * ks)
        for i in range(4):
            row_par_ref[side, i] = pars[i]
        row = PAD - 1 if side == 0 else PAD + rows
        head_pad[:, row, :] = head
        cond_pad[:, row, :] = conductivity(head, *pars)
    halo = lane_halo(own_ref[...], lane_even_ref[...], lane_odd_ref[...])
    wide = lane_tables(table_ref[...], halo.shape)[:4]
    kind = kinds(pltpu.roll(halo, width - 2 * layers, 1))
    pars = [lane_lookup(t, kind) for t in wide]
    pars[3] = sign_lane * (pars[3] * pltpu.roll(halo, width - 4 * layers, 1))
    for i in range(4):
        lane_par_ref[i] = pars[i]
    halo_ref[0] = halo
    halo_ref[1] = conductivity(halo, *pars)
    size = HALF if rows % HALF == 0 else rows
    lanes = lax.broadcasted_iota(jnp.int32, (size, width), 1)
    for top in range(0, rows, size):
        span = slice(top, top + size)
        inner = slice(PAD + top, PAD + top + size)
        vert_above = flux_above = ratio_above = None
        for k in range(layers):
            head, conduct, flow, faces = lateral_terms(
                k, top, size, head_pad, cond_pad, halo_ref[0, span], halo_ref[1, span], lanes
            )
            diagonal = stor_ref[k, span, :] + faces
            if k < layers - 1:
                vert = VERTICAL * (conduct + cond_pad[k + 1, inner, :])
                flux = vert * (head - head_pad[k + 1, inner, :] + 1.0)
                diagonal = diagonal + vert
            else:
                vert = None
                flux = conduct * (2.0 * VERTICAL)
            residual = flux + flow
            if k:
                residual = residual - flux_above
                diagonal = diagonal + vert_above
                diagonal = diagonal - vert_above * ratio_above
            inverse = 1.0 / diagonal
            res_ref[k, span, :] = residual
            inv_ref[k, span, :] = inverse
            if vert is not None:
                vert_ref[k, span, :] = vert
                ratio_above = vert * inverse
            vert_above, flux_above = vert, flux


def slot_places(ids, width):
    shift = width.bit_length() - 1
    row = ids >> shift
    low = ROW_BLOCK.bit_length() - 1
    return row & (ROW_BLOCK - 1), (row >> low) * width + (ids & (width - 1))


def one_hot(ids, count):
    place = lax.broadcasted_iota(jnp.int32, (count, ids.shape[1]), 0)
    return (place == ids).astype(F32).astype(BF16)


def middle_kernel(
    slots_ref, h_hbm, alpha_hbm, n1_hbm, half_m_hbm, ksat_hbm, room_hbm,
    res_ref, inv_ref, vert_ref,
    head_ref, sink_ref, infil_ref, row_even_ref, row_odd_ref, lane_ref,
    alpha_ref, n1_ref, half_m_ref, ksat_ref, room_ref,
    total, left_a, left_b, hot_a, hot_b, h_ref, sems,
):
    layers, rows, width = h_ref.shape
    peers, fields, per_peer = slots_ref.shape
    roots = fields - 2
    values = fields - 1
    blocks = rows // ROW_BLOCK
    half = values * ROW_BLOCK
    group = left_a.shape[1] // per_peer
    steps = peers // group
    loads = [
        pltpu.make_async_copy(a, b, sems.at[i])
        for i, (a, b) in enumerate(
            [
                (h_hbm, h_ref),
                (alpha_hbm, alpha_ref), (n1_hbm, n1_ref), (half_m_hbm, half_m_ref),
                (ksat_hbm, ksat_ref), (room_hbm, room_ref),
            ]
        )
    ]
    for copy in loads:
        copy.start()
    total[...] = jnp.zeros_like(total)

    def build(step, left, hot):
        for g in range(group):
            block = slots_ref[step * group + g]
            at = slice(g * per_peer, (g + 1) * per_peer)
            row, column = slot_places(block[values : values + 1, :].astype(jnp.int32), width)
            hot[:, at] = one_hot(column, blocks * width)
            mask = lax.broadcasted_iota(jnp.int32, (ROW_BLOCK, per_peer), 0) == row
            high = block.astype(BF16).astype(F32)
            low = block - high
            for f in range(values):
                for base, part in ((0, high), (half, low)):
                    first = base + f * ROW_BLOCK
                    left[first : first + ROW_BLOCK, at] = jnp.where(
                        mask, part[f : f + 1, :], 0.0
                    ).astype(BF16)

    def add(left, hot):
        total[...] += lax.dot_general(
            left[...], hot[...], (((1,), (1,)), ((), ())), preferred_element_type=F32
        )

    build(0, left_a, hot_a)

    def place(pair, carry):
        build(2 * pair + 1, left_b, hot_b)
        add(left_a, hot_a)
        build(jnp.minimum(2 * pair + 2, steps - 1), left_a, hot_a)
        add(left_b, hot_b)
        return carry

    lax.fori_loop(0, steps // 2, place, 0)
    for copy in loads:
        copy.wait()

    def grid(f, b):
        at = f * ROW_BLOCK
        cols = slice(b * width, (b + 1) * width)
        return total[at : at + ROW_BLOCK, cols] + total[half + at : half + at + ROW_BLOCK, cols]

    lanes = lax.broadcasted_iota(jnp.int32, (ROW_BLOCK, width), 1)
    for b in range(blocks):
        span = slice(b * ROW_BLOCK, (b + 1) * ROW_BLOCK)
        packed = jnp.zeros((ROW_BLOCK, width), F32)
        infil = grid(roots, b)
        infil_ref[span, :] = infil
        value = None
        for k in range(layers):
            target = -res_ref[k, span, :]
            if k < roots:
                sink = grid(k, b)
                sink_ref[k, span, :] = sink
                target = target - sink
            if k == 0:
                target = target + infil
            else:
                target = target + vert_ref[k - 1, span, :] * value
            value = target * inv_ref[k, span, :]
            head_ref[k, span, :] = value
        change = value
        for k in range(layers - 1, -1, -1):
            if k < layers - 1:
                ratio = vert_ref[k, span, :] * inv_ref[k, span, :]
                change = head_ref[k, span, :] + ratio * change
            head = h_ref[k, span, :] + change
            head_ref[k, span, :] = head
            packed = edge_lanes((head,), k, layers, lanes, packed)
        lane_ref[span, :] = packed
    edge_rows((head_ref,), row_even_ref, row_odd_ref)


def close_kernel(
    head_ref, sink_ref, infil_ref,
    alpha_ref, n1_ref, half_m_ref, ksat_ref, room_ref, sat_ref,
    cond_ref, stor_ref, source_ref,
):
    layers, rows, width = head_ref.shape
    roots = sink_ref.shape[0]
    for k in range(layers):
        room = room_ref[k]
        saturation, conduct, storage = closure(
            head_ref[k], alpha_ref[k], n1_ref[k], half_m_ref[k], ksat_ref[k], room
        )
        cond_ref[k] = conduct
        stor_ref[k] = storage
        source = room * (saturation - sat_ref[k])
        if k < roots:
            source = source + sink_ref[k]
        if k == 0:
            source = source - infil_ref[...]
        source_ref[k] = source


def last_kernel(
    slots_ref, old_head_ref, cond_ref, stor_ref, source_ref, sink_ref,
    alpha_ref, n1_ref, half_m_ref, row_par_ref, lane_par_ref,
    own_even_ref, own_odd_ref, row_even_ref, row_odd_ref, own_ref, lane_even_ref, lane_odd_ref,
    head_hbm, reply_ref,
    head_pad, cond_pad, head_ref, ratio_ref, value_ref, halo_ref, stress_ref, sems,
):
    layers, rows, width = head_ref.shape
    peers, fields, per_peer = slots_ref.shape
    roots = fields - 2
    blocks = rows // ROW_BLOCK
    head_pad[:, PAD : PAD + rows, :] = old_head_ref[...]
    cond_pad[:, PAD : PAD + rows, :] = cond_ref[...]
    sides = row_halo(own_even_ref[0], own_odd_ref[0], row_even_ref[0], row_odd_ref[0])
    for side, row in ((0, PAD - 1), (1, PAD + rows)):
        head_pad[:, row, :] = sides[side]
        pars = [row_par_ref[side, i] for i in range(4)]
        cond_pad[:, row, :] = conductivity(sides[side], *pars)
    halo = lane_halo(own_ref[...], lane_even_ref[...], lane_odd_ref[...])
    halo_ref[0] = halo
    halo_ref[1] = conductivity(halo, *(lane_par_ref[i] for i in range(4)))
    size = HALF if rows % HALF == 0 else rows
    lanes = lax.broadcasted_iota(jnp.int32, (size, width), 1)
    for top in range(0, rows, size):
        span = slice(top, top + size)
        vert_above = flux_above = ratio_above = value = None
        for k in range(layers):
            head, conduct, flow, faces = lateral_terms(
                k, top, size, head_pad, cond_pad, halo_ref[0, span], halo_ref[1, span], lanes
            )
            diagonal = stor_ref[k, span, :] + faces
            if k < layers - 1:
                vert = VERTICAL * (conduct + cond_ref[k + 1, span, :])
                flux = vert * (head - old_head_ref[k + 1, span, :] + 1.0)
                diagonal = diagonal + vert
            else:
                vert = None
                flux = conduct * (2.0 * VERTICAL)
            residual = flux + flow + source_ref[k, span, :]
            if k:
                residual = residual - flux_above
                diagonal = diagonal + vert_above
                diagonal = diagonal - vert_above * ratio_above
                inverse = 1.0 / diagonal
                value = (vert_above * value - residual) * inverse
            else:
                inverse = 1.0 / diagonal
                value = -residual * inverse
            value_ref[k, span, :] = value
            if vert is not None:
                ratio_above = vert * inverse
                ratio_ref[k, span, :] = ratio_above
            vert_above, flux_above = vert, flux
        change = value
        head_ref[layers - 1, span, :] = old_head_ref[layers - 1, span, :] + change
        numer = denom = None
        for k in range(layers - 2, -1, -1):
            change = value_ref[k, span, :] + ratio_ref[k, span, :] * change
            head = old_head_ref[k, span, :] + change
            head_ref[k, span, :] = head
            if k < roots:
                half = powers(
                    head, alpha_ref[k, span, :], n1_ref[k, span, :], half_m_ref[k, span, :]
                )[2]
                sink = sink_ref[k, span, :]
                term = sink * jnp.exp2(half + half)
                numer = term if numer is None else numer + term
                denom = sink if denom is None else denom + sink
        held = denom > 0.0
        stress_ref[span, :] = jnp.where(held, numer / jnp.where(held, denom, 1.0), 0.0)
    leave = pltpu.make_async_copy(head_ref, head_hbm, sems.at[0])
    leave.start()
    wide = jnp.concatenate(
        [stress_ref[b * ROW_BLOCK : (b + 1) * ROW_BLOCK, :] for b in range(blocks)], 1
    )
    high = wide.astype(BF16)
    both = jnp.concatenate([high, (wide - high.astype(F32)).astype(BF16)], 0)

    def answer(block, carry):
        for g in range(UNROLL):
            peer = block * UNROLL + g
            ids = slots_ref[peer, fields - 1 : fields, :].astype(jnp.int32)
            row, column = slot_places(ids, width)
            hot = one_hot(column, blocks * width)
            found = jnp.dot(both, hot, preferred_element_type=F32)
            found = found[:ROW_BLOCK] + found[ROW_BLOCK:]
            mask = lax.broadcasted_iota(jnp.int32, (ROW_BLOCK, per_peer), 0) == row
            reply_ref[pl.ds(peer, 1), :] = jnp.sum(
                jnp.where(mask, found, 0.0), 0, keepdims=True
            )
        return carry

    lax.fori_loop(0, peers // UNROLL, answer, 0)
    leave.wait()


def swaps():
    count_x, count_y = lax.axis_size("bx"), lax.axis_size("by")

    def pairs(partner):
        return [
            (x * count_y + y, px * count_y + py)
            for x in range(count_x)
            for y in range(count_y)
            for px, py in [partner(x, y)]
        ]

    odd = lambda i: i + 1 if i % 2 else i - 1
    return (
        pairs(lambda x, y: (x ^ 1, y)),
        pairs(lambda x, y: (odd(x) % count_x, y)),
        pairs(lambda x, y: (x, y ^ 1)),
        pairs(lambda x, y: (x, odd(y)) if 0 < y < count_y - 1 else (x ^ 1, y)),
    )


def exchange(row_even, row_odd, packed):
    even_x, odd_x, even_y, odd_y = swaps()
    axes = ("bx", "by")
    return (
        row_even,
        row_odd,
        lax.ppermute(row_even, axes, even_x),
        lax.ppermute(row_odd, axes, odd_x),
        packed,
        lax.ppermute(packed, axes, even_y),
        lax.ppermute(packed, axes, odd_y),
    )


def call(kernel, ins, outs, scratch, name, limit=20, flops=0):
    return pl.pallas_call(
        kernel,
        in_specs=[pl.BlockSpec(memory_space=m) for m in ins],
        out_specs=[pl.BlockSpec(memory_space=m) for _, _, m in outs],
        out_shape=[HBM(s, t) if m is HBM else jax.ShapeDtypeStruct(s, t) for s, t, m in outs],
        scratch_shapes=scratch,
        name=name,
        cost_estimate=pl.CostEstimate(flops=flops, bytes_accessed=flops, transcendentals=0),
        compiler_params=pltpu.CompilerParams(vmem_limit_bytes=limit * MIB),
    )


def in_hbm(*arrays):
    return [pltpu.with_memory_space_constraint(a, HBM) for a in arrays]


def prepare(root_fraction, transpiration, infiltration, clump_cell, peers, per_peer):
    roots, slot_count = root_fraction.shape
    line = (1, slot_count)
    return pl.pallas_call(
        prepare_kernel,
        in_specs=[pl.BlockSpec(memory_space=HBM)] * 4,
        out_specs=pl.BlockSpec(memory_space=VMEM),
        out_shape=VMEM((peers, roots + 2, per_peer), F32),
        scratch_shapes=[
            VMEM(root_fraction.shape, F32), VMEM(line, F32), VMEM(line, F32),
            VMEM(line, jnp.int32), pltpu.SemaphoreType.DMA((8,)),
        ],
        name="prepare",
        compiler_params=pltpu.CompilerParams(vmem_limit_bytes=6 * MIB),
    )(*in_hbm(root_fraction, transpiration[None], infiltration[None], clump_cell[None]))


def on_device(
    h_old,
    soil_type,
    ks_scale,
    soil_table,
    clump_brick,
    clump_cell,
    root_fraction,
    transpiration,
    infiltration,
):
    layers, rows, width = h_old.shape
    peers = lax.axis_size("bx") * lax.axis_size("by")
    roots, slot_count = root_fraction.shape
    per_peer = slot_count // peers
    cells = (layers, rows, width)
    lane_msg = (rows, width)
    axes = ("bx", "by")
    on_chip = lambda *shapes: [(s, F32, VMEM) for s in shapes]
    in_main = lambda *shapes: [(s, F32, HBM) for s in shapes]
    buffers = lambda n: [VMEM(cells, F32)] * n
    semaphores = pltpu.SemaphoreType.DMA
    chunks = len(layer_chunks(layers))

    slots = lax.all_to_all(
        prepare(root_fraction, transpiration, infiltration, clump_cell, peers, per_peer),
        axes,
        split_axis=0,
        concat_axis=0,
        tiled=True,
    )
    table = jnp.pad(soil_table, ((0, 0), (0, width - soil_table.shape[1])))
    raw_msg = (3, layers, width)
    head, soil, scale, row_even, row_odd, packed = call(
        edges_kernel,
        [HBM] * 3,
        on_chip(cells) + [(cells, jnp.int32, VMEM)] + on_chip(cells, raw_msg, raw_msg, lane_msg),
        [semaphores((3 * chunks,))],
        "edges",
    )(*in_hbm(h_old, soil_type, ks_scale))
    pads = [VMEM((layers, rows + 2 * PAD, width), F32)] * 2
    halo = [VMEM((2,) + lane_msg, F32)]
    arrived = exchange(row_even, row_odd, packed)
    alpha, n1, half_m, ksat, room, old_sat, conduct, storage = call(
        first_kernel,
        [VMEM] * 4,
        in_main(*[cells] * 5) + on_chip(*[cells] * 3),
        buffers(5) + [semaphores((5 * chunks,))],
        "first",
        flops=8_000_000,
    )(head, soil, scale, table)
    residual, inverse, vert, row_par, lane_par = call(
        factor_kernel,
        [VMEM] * 11,
        on_chip(*[cells] * 3, (2, 4, layers, width), (4,) + lane_msg),
        pads + halo,
        "factor",
        flops=4_000_000,
    )(head, conduct, storage, table, *arrived)
    values = roots + 1
    columns = rows // ROW_BLOCK * width
    group = GROUP if peers % (2 * GROUP) == 0 else 1
    lefts = [VMEM((2 * values * ROW_BLOCK, group * per_peer), BF16)] * 2
    hots = [VMEM((columns, group * per_peer), BF16)] * 2
    row_msg = (1, layers, width)
    head, sink, infil, row_even, row_odd, packed, alpha, n1, half_m, ksat, room = call(
        middle_kernel,
        [VMEM] + [HBM] * 6 + [VMEM] * 3,
        on_chip(cells, (roots, rows, width), lane_msg, row_msg, row_msg, lane_msg)
        + on_chip(*[cells] * 5),
        [VMEM((2 * values * ROW_BLOCK, columns), F32)] + lefts + hots
        + buffers(1) + [semaphores((6,))],
        "middle",
    )(
        slots, *in_hbm(h_old, alpha, n1, half_m, ksat, room), residual, inverse, vert
    )
    arrived = exchange(row_even, row_odd, packed)
    conduct, storage, source = call(
        close_kernel, [VMEM] * 9, on_chip(*[cells] * 3), [], "close", limit=4, flops=4_000_000
    )(head, sink, infil, alpha, n1, half_m, ksat, room, old_sat)
    head, reply = call(
        last_kernel,
        [VMEM] * 18,
        in_main(cells) + on_chip((peers, per_peer)),
        pads + buffers(3) + halo + [VMEM(lane_msg, F32), semaphores((1,))],
        "last",
    )(
        slots, head, conduct, storage, source, sink, alpha, n1, half_m, row_par, lane_par,
        *arrived,
    )
    stress = lax.all_to_all(reply, axes, split_axis=0, concat_axis=0, tiled=True)
    return head, stress.reshape(slot_count)


def solution(mesh):
    placed = (
        P(None, "bx", "by"),
        P(None, "bx", "by"),
        P(None, "bx", "by"),
        P(),
        P(("bx", "by")),
        P(("bx", "by")),
        P(None, ("bx", "by")),
        P(("bx", "by")),
        P(("bx", "by")),
    )
    return jax.shard_map(
        on_device,
        mesh=mesh,
        in_specs=placed,
        out_specs=(P(None, "bx", "by"), P(("bx", "by"))),
        check_vma=False,
    )
```

time: 58.7 us -> 53.2 us (0.906)
  Pallas kernels: 23.1 us -> 17.8 us
  starting transfers between devices: 17.2 us -> 15.2 us
  waiting for transfers between devices: 6.04 us -> 7.07 us
  blocking collectives: 10.6 us -> 11.4 us
    pallas_call x5 -> x7, Pallas kernels: 23.1 us -> 17.8 us  [the longest x1 5.97 us: on_device(): call(middle_kernel, [VMEM] + [HBM] * 6 + [VMEM] * 3, on_chip(cells, (root...]
    all_to_all x1, waiting for transfers between devices: 0.01 us -> 5.31 us  [on_device(): lax.all_to_all(prepare(root_fraction, transpiration, infiltration, clump_...]
    ppermute x8, waiting for transfers between devices: 6.04 us -> 1.76 us  [the longest x2 1.75 us: exchange(): lax.ppermute(row_odd, axes, odd_x)]
    ppermute x8, starting transfers between devices: 9.87 us -> 7.83 us  [the longest x2 5.22 us: exchange(): lax.ppermute(packed, axes, even_y)]
    all_to_all x1, blocking collectives: 10.6 us -> 11.4 us  [on_device(): lax.all_to_all(reply, axes, split_axis=0, concat_axis=0, tiled=True)]
  transfers between devices with their start and end apart: 9 -> 9, of which waited for: 4 -> 2; matrix products, arithmetic and copies ran while one was open for 0% -> 0% of each run, Pallas kernels for 14% -> 13%
where the time goes in v2:
time: 53.2 us; the launch traced here: 52.9 us
  Pallas kernels  17.8 us (33%)
  starting transfers between devices  15.2 us (29%)
  blocking collectives  11.4 us (21%)
  waiting for transfers between devices  7.07 us (13%)
  between operations  0.75 us (1%)
  local copies, waits for them, and re-layouts  0.66 us (1%)
    all_to_all x1, blocking collectives, on_device(): lax.all_to_all(reply, axes, split_axis=0, concat_axis=0, tiled=True)  11.4 us
    all_to_all x1, starting transfers between devices, on_device(): lax.all_to_all(prepare(root_fraction, transpiration, infiltration, clump_...  7.33 us
    pallas_call x1, Pallas kernels, on_device(): call(middle_kernel, [VMEM] + [HBM] * 6 + [VMEM] * 3, on_chip(cells, (root...  5.97 us
    all_to_all x1, waiting for transfers between devices, on_device(): lax.all_to_all(prepare(root_fraction, transpiration, infiltration, clump_...  5.31 us
    ppermute x2, starting transfers between devices, exchange(): lax.ppermute(packed, axes, even_y)  5.22 us
    pallas_call x1, Pallas kernels, on_device(): call(last_kernel, [VMEM] * 18, in_main(cells) + on_chip((peers, per_peer)...  3.1 us
    pallas_call x1, Pallas kernels, on_device(): call(first_kernel, [VMEM] * 4, in_main(*[cells] * 5) + on_chip(*[cells] *...  2.46 us
    ppermute x2, starting transfers between devices, exchange(): lax.ppermute(row_odd, axes, odd_x)  2.21 us
  transfers between devices with their start and end apart: 9, of which 2 were waited for; matrix products, arithmetic and copies ran while one was open for 0% of the time, Pallas kernels for 13%

profile of v2, /device:TPU:0, one launch (start us, length us, event | category | flops | bytes accessed | tf_op | source)
XLA Modules:
  0.0 52.9 jit_solution(7945422418893425205)
XLA Ops:
  0.6 2.0 %prepare.1 = f32[32,16,256]{2,1,0:T(8,128)} custom-call(f32[14,8192]{1,0:T(8,128)} %root_hbm.1, f32[1,8192]{1,0:T(1,128)} %bitcast.7, f32[1,8192]{1,0:T(1,128)} %bitcast.8, s32[1,8192]{1,0:T(1,128)} %bitcast.9), custom_call_target="tpu_custom_call" | custom-call | tf_op jit(solution)/shard_map/prepare/pallas_call | solution.py:619
  2.7 7.3 %all-to-all-start = ((f32[32,16,256]{2,1,0:T(8,128)}), f32[32,16,256]{2,1,0:T(8,128)S(1)}, u32[]{:S(2)}, u32[]{:S(2)}) async-start(f32[32,16,256]{2,1,0:T(8,128)} %prepare.1), calls=%async_computation | async-start | bytes 1048576 | tf_op jit(solution)/shard_map/all_to_all | solution.py:657
  10.0 2.1 %edges.1 = (f32[20,64,128]{2,1,0:T(8,128)S(1)}, s32[20,64,128]{2,1,0:T(8,128)S(1)}, f32[20,64,128]{2,1,0:T(8,128)S(1)}, f32[3,20,128]{2,1,0:T(8,128)S(1)}, f32[3...) custom-call(f32[20,64,128]{2,1,0:T(8,128)} %h_hbm.3, s32[20,64,128]{2,1,0:T(8,128)} %soil_hbm.1, f32[20,64,128]{2,1,0:T(8,128)} %ks_hbm.1), custom_call_target="tpu_custom_call" | custom-call | tf_op jit(solution)/shard_map/edges/pallas_call | solution.py:666
  12.1 0.0 copy-start
  12.1 0.3 collective-permute-start.3
  12.4 3.0 %collective-permute-start.2 = (f32[64,128]{1,0:T(8,128)S(1)}, f32[64,128]{1,0:T(8,128)S(1)}, u32[]{:S(2)}, u32[]{:S(2)}) collective-permute-start(f32[64,128]{1,0:T(8,128)S(1)} %get-tuple-element.49.own_ref), channel_id=1, source_target_pairs={{0,1},{1,0},{2,3},{3,2},{4,5},{5,4},{6,7},{7,6},{8,9},{9,8},{10,11... | collective-permute-start | bytes 98312 | tf_op jit(solution)/shard_map/ppermute | solution.py:594
  15.4 0.0 collective-permute-start
  15.4 1.6 %collective-permute-start.1 = (f32[3,20,128]{2,1,0:T(8,128)S(1)}, f32[3,20,128]{2,1,0:T(8,128)S(1)}, u32[]{:S(2)}, u32[]{:S(2)}) collective-permute-start(f32[3,20,128]{2,1,0:T(8,128)S(1)} %get-tuple-element.48.own_odd_ref), channel_id=1, source_target_pairs={{0,24},{1,25},{2,26},{3,27},{4,28},{5,29},{6,30},{7,31},{8,16},{9,... | collective-permute-start | bytes 92168 | tf_op jit(solution)/shard_map/ppermute | solution.py:592
  17.0 0.0 copy-done
  17.0 2.5 %first.1 = (f32[20,64,128]{2,1,0:T(8,128)}, f32[20,64,128]{2,1,0:T(8,128)}, f32[20,64,128]{2,1,0:T(8,128)}, f32[20,64,128]{2,1,0:T(8,128)}, f32[20,64,128]{2,1,0...) custom-call(f32[20,64,128]{2,1,0:T(8,128)S(1)} %get-tuple-element.37.h_ref, ...), custom_call_target="tpu_custom_call" | custom-call | flops 8000000 | bytes 8000000 | tf_op jit(solution)/shard_map/first/pallas_call | solution.py:676
  19.5 0.0 collective-permute-done.row_even_ref
  19.5 0.0 collective-permute-done.1.row_odd_ref
  19.5 0.0 collective-permute-done.3.lane_odd_ref
  19.5 0.0 collective-permute-done.2.lane_even_ref
  19.5 1.4 %factor.1 = (f32[20,64,128]{2,1,0:T(8,128)S(1)}, f32[20,64,128]{2,1,0:T(8,128)S(1)}, f32[20,64,128]{2,1,0:T(8,128)S(1)}, f32[2,4,20,128]{3,2,1,0:T(8,128)S(1)}, f32[4,64,128]{2,1,0:T(8,128)S(1)}) custom-call(f32[20,64,128]{2,1,0:T(8,128)S(1)} %get-tuple-element.37.h_ref, f32[20,64,128]{2,1,0:T(8,128)S(1)} %get-tuple-element.45.cond_ref, ...), custom_call_target="tpu_custom_call" | custom-call | flops 4000000 | bytes 4000000 | tf_op jit(solution)/shard_map/factor/pallas_call | solution.py:684
  21.0 5.3 %all-to-all-done.slots_ref = f32[32,16,256]{2,1,0:T(8,128)S(1)} async-done(((f32[32,16,256]{2,1,0:T(8,128)}), f32[32,16,256]{2,1,0:T(8,128)S(1)}, u32[]{:S(2)}, u32[]{:S(2)}) %all-to-all-start) | async-done | bytes 524320 | tf_op jit(solution)/shard_map/all_to_all | solution.py:657
  26.3 6.0 %middle.1 = (f32[20,64,128]{2,1,0:T(8,128)S(1)}, f32[14,64,128]{2,1,0:T(8,128)S(1)}, f32[64,128]{1,0:T(8,128)S(1)}, f32[1,20,128]{2,1,0:T(8,128)S(1)}, f32[1,20,...) custom-call(f32[32,16,256]{2,1,0:T(8,128)S(1)} %all-to-all-done.slot, ...), custom_call_target="tpu_custom_call" | custom-call | tf_op jit(solution)/shard_map/middle/pallas_call | solution.py:698
  32.2 0.1 collective-permute-start.7
  32.3 2.2 %collective-permute-start.6 = (f32[64,128]{1,0:T(8,128)S(1)}, f32[64,128]{1,0:T(8,128)S(1)}, u32[]{:S(2)}, u32[]{:S(2)}) collective-permute-start(f32[64,128]{1,0:T(8,128)S(1)} %get-tuple-element.69.own_ref), channel_id=1, source_target_pairs={{0,1},{1,0},{2,3},{3,2},{4,5},{5,4},{6,7},{7,6},{8,9},{9,8},{10,11... | collective-permute-start | bytes 98312 | tf_op jit(solution)/shard_map/ppermute | solution.py:594
  34.6 0.0 collective-permute-start.4
  34.6 0.6 %collective-permute-start.5 = (f32[1,20,128]{2,1,0:T(8,128)S(1)}, f32[1,20,128]{2,1,0:T(8,128)S(1)}, u32[]{:S(2)}, u32[]{:S(2)}) collective-permute-start(f32[1,20,128]{2,1,0:T(8,128)S(1)} %get-tuple-element.68.own_odd_ref), channel_id=1, source_target_pairs={{0,24},{1,25},{2,26},{3,27},{4,28},{5,29},{6,30},{7,31},{8,16},{9,... | collective-permute-start | bytes 30728 | tf_op jit(solution)/shard_map/ppermute | solution.py:592
  35.2 0.7 %close.1 = (f32[20,64,128]{2,1,0:T(8,128)S(1)}, f32[20,64,128]{2,1,0:T(8,128)S(1)}, f32[20,64,128]{2,1,0:T(8,128)S(1)}) custom-call(f32[20,64,128]{2,1,0:T(8,128)S(1)} %get-tuple-element.53.head_ref.old_head_ref, f32[14,64,128]{2,1,0:T(8,128)S(1)} %get-tuple-element.54.sink_ref, f32[64,128]{1,0:T(8,128)S(1)} %get-tuple-element.55.infil_ref, ...), custom_call_target="tpu_custom_call" | custom-call | flops 4000000 | bytes 4000000 | tf_op jit(solution)/shard_map/close/pallas_call | solution.py:710
  35.9 0.0 collective-permute-done.4.row_even_ref
  35.9 1.7 %collective-permute-done.5.row_odd_ref = f32[1,20,128]{2,1,0:T(8,128)S(1)} collective-permute-done((f32[1,20,128]{2,1,0:T(8,128)S(1)}, f32[1,20,128]{2,1,0:T(8,128)S(1)}, u32[]{:S(2)}, u32[]{:S(2)}) %collective-permute-start.5) | collective-permute-done | bytes 10272 | tf_op jit(solution)/shard_map/ppermute | solution.py:592
  37.7 0.0 collective-permute-done.7.lane_odd_ref
  37.7 0.0 collective-permute-done.6.lane_even_ref
  37.7 3.1 %last.1 = (f32[20,64,128]{2,1,0:T(8,128)}, f32[32,256]{1,0:T(8,128)S(1)}) custom-call(f32[32,16,256]{2,1,0:T(8,128)S(1)} %all-to-all-done.slots_ref, f32[20,64,128]{2,1,0:T(8,128)S(1)} %get-tuple-element.53.head_ref.old_head_ref, f32[20,64,128]{2,1,0:T(8,128)S(1)} %get-tuple-element.62.cond_ref, f32[20,64,128]{2,1,0:T(8,128)S(1)} %get-tuple-element.63.stor_ref, ...), custom_call_target="tpu_custom_call" | custom-call | tf_op jit(solution)/shard_map/last/pallas_call | solution.py:713
  40.8 11.4 %all_to_all.14 = f32[32,1,256]{2,1,0:T(1,128)S(1)} all-to-all(f32[32,1,256]{2,1,0:T(1,128)S(1)} %copy.10), channel_id=1, replica_groups=mesh['bx'=4,'by'=8] {'bx','by'}, dimensions={0} | all-to-all | bytes 65536 | tf_op jit(solution)/shard_map/all_to_all | solution.py:723
  52.3 0.6 %copy.12 = f32[8192]{0:T(1024)} copy(f32[8192]{0:T(1024)S(1)} %bitcast.6) | data formatting | bytes 65536
  (2 shorter events, 0.0 us)
Async XLA Ops:
  2.7 23.6 %all-to-all-start = ((f32[32,16,256]{2,1,0:T(8,128)}), f32[32,16,256]{2,1,0:T(8,128)S(1)}, u32[]{:S(2)}, u32[]{:S(2)}) async-start(f32[32,16,256]{2,1,0:T(8,128)} %prepare.1), calls=%async_computation | async-start | bytes 1048576 | tf_op jit(solution)/shard_map/all_to_all | solution.py:657
  12.1 4.9 %copy-start = (f32[4,12]{1,0:T(4,128)S(1)}, f32[4,12]{1,0:T(4,128)}, u32[]{:S(2)}) copy-start(f32[4,12]{1,0:T(4,128)} %param.12) | copy-start | bytes 580
  12.1 7.4 %collective-permute-start.3 = (f32[64,128]{1,0:T(8,128)S(1)}, f32[64,128]{1,0:T(8,128)S(1)}, u32[]{:S(2)}, u32[]{:S(2)}) collective-permute-start(f32[64,128]{1,0:T(8,128)S(1)} %get-tuple-element.49.own_ref), channel_id=1, source_target_pairs={{0,8},{1,2},{2,1},{3,4},{4,3},{5,6},{6,5},{7,15},{8,0},{9,10},{10,... | collective-permute-start | bytes 98312 | tf_op jit(solution)/shard_map/ppermute | solution.py:595
  12.4 7.1 %collective-permute-start.2 = (f32[64,128]{1,0:T(8,128)S(1)}, f32[64,128]{1,0:T(8,128)S(1)}, u32[]{:S(2)}, u32[]{:S(2)}) collective-permute-start(f32[64,128]{1,0:T(8,128)S(1)} %get-tuple-element.49.own_ref), channel_id=1, source_target_pairs={{0,1},{1,0},{2,3},{3,2},{4,5},{5,4},{6,7},{7,6},{8,9},{9,8},{10,11... | collective-permute-start | bytes 98312 | tf_op jit(solution)/shard_map/ppermute | solution.py:594
  15.4 4.1 %collective-permute-start = (f32[3,20,128]{2,1,0:T(8,128)S(1)}, f32[3,20,128]{2,1,0:T(8,128)S(1)}, u32[]{:S(2)}, u32[]{:S(2)}) collective-permute-start(f32[3,20,128]{2,1,0:T(8,128)S(1)} %get-tuple-element.47.own_even_ref), channel_id=1, source_target_pairs={{0,8},{1,9},{2,10},{3,11},{4,12},{5,13},{6,14},{7,15},{8,0},{9,1},... | collective-permute-start | bytes 92168 | tf_op jit(solution)/shard_map/ppermute | solution.py:591
  15.4 4.1 %collective-permute-start.1 = (f32[3,20,128]{2,1,0:T(8,128)S(1)}, f32[3,20,128]{2,1,0:T(8,128)S(1)}, u32[]{:S(2)}, u32[]{:S(2)}) collective-permute-start(f32[3,20,128]{2,1,0:T(8,128)S(1)} %get-tuple-element.48.own_odd_ref), channel_id=1, source_target_pairs={{0,24},{1,25},{2,26},{3,27},{4,28},{5,29},{6,30},{7,31},{8,16},{9,... | collective-permute-start | bytes 92168 | tf_op jit(solution)/shard_map/ppermute | solution.py:592
  32.2 5.4 %collective-permute-start.7 = (f32[64,128]{1,0:T(8,128)S(1)}, f32[64,128]{1,0:T(8,128)S(1)}, u32[]{:S(2)}, u32[]{:S(2)}) collective-permute-start(f32[64,128]{1,0:T(8,128)S(1)} %get-tuple-element.69.own_ref), channel_id=1, source_target_pairs={{0,8},{1,2},{2,1},{3,4},{4,3},{5,6},{6,5},{7,15},{8,0},{9,10},{10,... | collective-permute-start | bytes 98312 | tf_op jit(solution)/shard_map/ppermute | solution.py:595
  32.3 5.4 %collective-permute-start.6 = (f32[64,128]{1,0:T(8,128)S(1)}, f32[64,128]{1,0:T(8,128)S(1)}, u32[]{:S(2)}, u32[]{:S(2)}) collective-permute-start(f32[64,128]{1,0:T(8,128)S(1)} %get-tuple-element.69.own_ref), channel_id=1, source_target_pairs={{0,1},{1,0},{2,3},{3,2},{4,5},{5,4},{6,7},{7,6},{8,9},{9,8},{10,11... | collective-permute-start | bytes 98312 | tf_op jit(solution)/shard_map/ppermute | solution.py:594
  34.6 1.4 %collective-permute-start.4 = (f32[1,20,128]{2,1,0:T(8,128)S(1)}, f32[1,20,128]{2,1,0:T(8,128)S(1)}, u32[]{:S(2)}, u32[]{:S(2)}) collective-permute-start(f32[1,20,128]{2,1,0:T(8,128)S(1)} %get-tuple-element.67.own_even_ref), channel_id=1, source_target_pairs={{0,8},{1,9},{2,10},{3,11},{4,12},{5,13},{6,14},{7,15},{8,0},{9,1},... | collective-permute-start | bytes 30728 | tf_op jit(solution)/shard_map/ppermute | solution.py:591
  34.6 3.1 %collective-permute-start.5 = (f32[1,20,128]{2,1,0:T(8,128)S(1)}, f32[1,20,128]{2,1,0:T(8,128)S(1)}, u32[]{:S(2)}, u32[]{:S(2)}) collective-permute-start(f32[1,20,128]{2,1,0:T(8,128)S(1)} %get-tuple-element.68.own_odd_ref), channel_id=1, source_target_pairs={{0,24},{1,25},{2,26},{3,27},{4,28},{5,29},{6,30},{7,31},{8,16},{9,... | collective-permute-start | bytes 30728 | tf_op jit(solution)/shard_map/ppermute | solution.py:592

commit v3 on v2

--- a/solution.py
+++ b/solution.py
@@ -5,7 +5,7 @@
 from jax.experimental.pallas import tpu as pltpu
 from jax.sharding import PartitionSpec as P
 
-ITERS = 2
+
 RESIDUAL_WATER = 0.05
 STORAGE = 0.2
 TIME_STEP = 0.5
@@ -121,15 +121,16 @@
 
 
 def prepare_kernel(
-    root_hbm, transp_hbm, infil_hbm, cell_hbm, out_ref,
-    root_ref, transp_ref, infil_ref, cell_ref, sems,
+    root_hbm, transp_hbm, infil_hbm, cell_hbm, out_hbm,
+    root_ref, transp_ref, infil_ref, cell_ref, out_ref, sems,
 ):
     peers, fields, per_peer = out_ref.shape
     roots = fields - 2
-    steps = 4 if peers % 4 == 0 else 1
-    span = peers // steps * per_peer
+    steps = prepare_steps(peers)
+    count = peers // steps
+    span = count * per_peer
     lines = [
-        pltpu.make_async_copy(a, b, sems.at[steps + i])
+        pltpu.make_async_copy(a, b, sems.at[2 * steps + i])
         for i, (a, b) in enumerate(
             [(transp_hbm, transp_ref), (infil_hbm, infil_ref), (cell_hbm, cell_ref)]
         )
@@ -142,17 +143,32 @@
         )
         for i in range(steps)
     ]
+    leaves = [
+        pltpu.make_async_copy(
+            out_ref.at[pl.ds(i * count, count)],
+            out_hbm.at[pl.ds(i * count, count)],
+            sems.at[steps + i],
+        )
+        for i in range(steps)
+    ]
     for copy in lines + parts:
         copy.start()
     for copy in lines:
         copy.wait()
-    for i, copy in enumerate(parts):
-        copy.wait()
-        for peer in range(i * peers // steps, (i + 1) * peers // steps):
+    for i in range(steps):
+        parts[i].wait()
+        for peer in range(i * count, (i + 1) * count):
             at = slice(peer * per_peer, (peer + 1) * per_peer)
             out_ref[peer, :roots, :] = root_ref[:, at] * transp_ref[:, at]
             out_ref[peer, roots : roots + 1, :] = infil_ref[:, at]
             out_ref[peer, roots + 1 :, :] = cell_ref[:, at].astype(F32)
+        leaves[i].start()
+    for copy in leaves:
+        copy.wait()
+
+
+def prepare_steps(peers):
+    return 4 if peers % 4 == 0 else 1
 
 
 def layer_chunks(layers):
@@ -200,28 +216,25 @@
     width = head_pad.shape[2]
     at = lambda pad, move: pad[k, PAD + top + move : PAD + top + move + size, :]
     head, conduct = at(head_pad, 0), at(cond_pad, 0)
-    halo_head = pltpu.roll(halo_head, (width - 2 * k) % width, 1)
-    halo_cond = pltpu.roll(halo_cond, (width - 2 * k) % width, 1)
-    first = lanes == 0
-    last = lanes == width - 1
-    pairs = [
-        (at(head_pad, -1), at(cond_pad, -1)),
-        (at(head_pad, 1), at(cond_pad, 1)),
-        (
-            jnp.where(first, halo_head, pltpu.roll(head, 1, 1)),
-            jnp.where(first, halo_cond, pltpu.roll(conduct, 1, 1)),
-        ),
-        (
-            jnp.where(last, halo_head, pltpu.roll(head, width - 1, 1)),
-            jnp.where(last, halo_cond, pltpu.roll(conduct, width - 1, 1)),
-        ),
-    ]
     flow = faces = None
-    for other_head, other_cond in pairs:
-        both = conduct + other_cond
-        term = both * (head - other_head)
+    for move in (-1, 1):
+        both = conduct + at(cond_pad, move)
+        term = both * (head - at(head_pad, move))
         flow = term if flow is None else flow + term
         faces = both if faces is None else faces + both
+    if halo_head is not None:
+        halo_head = pltpu.roll(halo_head, (width - 2 * k) % width, 1)
+        halo_cond = pltpu.roll(halo_cond, (width - 2 * k) % width, 1)
+    for shift, edge in ((1, lanes == 0), (width - 1, lanes == width - 1)):
+        other_head = pltpu.roll(head, shift, 1)
+        other_cond = pltpu.roll(conduct, shift, 1)
+        if halo_head is not None:
+            other_head = jnp.where(edge, halo_head, other_head)
+            both = conduct + jnp.where(edge, halo_cond, other_cond)
+        else:
+            both = jnp.where(edge, 0.0, conduct + other_cond)
+        flow = flow + both * (head - other_head)
+        faces = faces + both
     return head, conduct, flow, faces
 
 
@@ -230,14 +243,15 @@
 
 def first_kernel(
     h_ref, soil_ref, ks_ref, table_ref,
-    alpha_hbm, n1_hbm, half_m_hbm, ksat_hbm, room_hbm, sat_ref, cond_ref, stor_ref,
-    alpha_ref, n1_ref, half_m_ref, ksat_ref, room_ref, sems,
+    alpha_hbm, n1_hbm, half_m_hbm, ksat_hbm, room_hbm, sat_hbm, cond_hbm, cond_ref, stor_ref,
+    alpha_ref, n1_ref, half_m_ref, ksat_ref, room_ref, sat_ref, sems,
 ):
     layers, rows, width = h_ref.shape
     outs = copies(
         [
             (alpha_ref, alpha_hbm), (n1_ref, n1_hbm), (half_m_ref, half_m_hbm),
-            (ksat_ref, ksat_hbm), (room_ref, room_hbm),
+            (ksat_ref, ksat_hbm), (room_ref, room_hbm), (sat_ref, sat_hbm),
+            (cond_ref, cond_hbm),
         ],
         sems,
         layers,
@@ -268,54 +282,43 @@
             copy.wait()
 
 
-def factor_kernel(
+def balance_kernel(
     h_ref, cond_ref, stor_ref, table_ref,
-    own_even_ref, own_odd_ref, row_even_ref, row_odd_ref, own_ref, lane_even_ref, lane_odd_ref,
-    res_ref, inv_ref, vert_ref, row_par_ref, lane_par_ref,
-    head_pad, cond_pad, halo_ref,
+    own_even_ref, own_odd_ref, row_even_ref, row_odd_ref,
+    res_ref, diag_ref, vert_ref, row_par_ref,
+    head_pad, cond_pad,
 ):
     layers, rows, width = h_ref.shape
     head_pad[:, PAD : PAD + rows, :] = h_ref[...]
     cond_pad[:, PAD : PAD + rows, :] = cond_ref[...]
-    sign_low, sign_high, sign_lane = edge_signs((rows, width))
-    kinds = lambda x: jnp.clip(x.astype(jnp.int32), 0, width - 1)
+    sign_low, sign_high, _ = edge_signs((8, width))
     for side, sign in ((0, sign_low), (1, sign_high)):
         head, kind, ks = (
             row_halo(own_even_ref[i], own_odd_ref[i], row_even_ref[i], row_odd_ref[i])[side]
             for i in range(3)
         )
-        wide = lane_tables(table_ref[...], head.shape)[:4]
-        pars = [lane_lookup(t, kinds(kind)) for t in wide]
-        pars[3] = sign * (pars[3] * ks)
+        pars = halo_parameters(table_ref, kind, ks, sign)
         for i in range(4):
             row_par_ref[side, i] = pars[i]
         row = PAD - 1 if side == 0 else PAD + rows
         head_pad[:, row, :] = head
         cond_pad[:, row, :] = conductivity(head, *pars)
-    halo = lane_halo(own_ref[...], lane_even_ref[...], lane_odd_ref[...])
-    wide = lane_tables(table_ref[...], halo.shape)[:4]
-    kind = kinds(pltpu.roll(halo, width - 2 * layers, 1))
-    pars = [lane_lookup(t, kind) for t in wide]
-    pars[3] = sign_lane * (pars[3] * pltpu.roll(halo, width - 4 * layers, 1))
-    for i in range(4):
-        lane_par_ref[i] = pars[i]
-    halo_ref[0] = halo
-    halo_ref[1] = conductivity(halo, *pars)
     size = HALF if rows % HALF == 0 else rows
     lanes = lax.broadcasted_iota(jnp.int32, (size, width), 1)
     for top in range(0, rows, size):
         span = slice(top, top + size)
         inner = slice(PAD + top, PAD + top + size)
-        vert_above = flux_above = ratio_above = None
+        vert_above = flux_above = None
         for k in range(layers):
             head, conduct, flow, faces = lateral_terms(
-                k, top, size, head_pad, cond_pad, halo_ref[0, span], halo_ref[1, span], lanes
+                k, top, size, head_pad, cond_pad, None, None, lanes
             )
             diagonal = stor_ref[k, span, :] + faces
             if k < layers - 1:
                 vert = VERTICAL * (conduct + cond_pad[k + 1, inner, :])
                 flux = vert * (head - head_pad[k + 1, inner, :] + 1.0)
                 diagonal = diagonal + vert
+                vert_ref[k, span, :] = vert
             else:
                 vert = None
                 flux = conduct * (2.0 * VERTICAL)
@@ -323,14 +326,17 @@
             if k:
                 residual = residual - flux_above
                 diagonal = diagonal + vert_above
-                diagonal = diagonal - vert_above * ratio_above
-            inverse = 1.0 / diagonal
             res_ref[k, span, :] = residual
-            inv_ref[k, span, :] = inverse
-            if vert is not None:
-                vert_ref[k, span, :] = vert
-                ratio_above = vert * inverse
+            diag_ref[k, span, :] = diagonal
             vert_above, flux_above = vert, flux
+
+
+def halo_parameters(table_ref, kind, ks, sign):
+    pars = [
+        lane_lookup(t, jnp.clip(kind.astype(jnp.int32), 0, kind.shape[1] - 1))
+        for t in lane_tables(table_ref[...], kind.shape)[:4]
+    ]
+    return pars[:3] + [sign * (pars[3] * ks)]
 
 
 def slot_places(ids, width):
@@ -346,11 +352,11 @@
 
 
 def middle_kernel(
-    slots_ref, h_hbm, alpha_hbm, n1_hbm, half_m_hbm, ksat_hbm, room_hbm,
-    res_ref, inv_ref, vert_ref,
+    slots_ref, h_hbm, cond_hbm, alpha_hbm, n1_hbm, half_m_hbm, ksat_hbm, room_hbm, sat_hbm,
+    res_ref, diag_ref, vert_ref, table_ref, own_ref, lane_even_ref, lane_odd_ref,
     head_ref, sink_ref, infil_ref, row_even_ref, row_odd_ref, lane_ref,
-    alpha_ref, n1_ref, half_m_ref, ksat_ref, room_ref,
-    total, left_a, left_b, hot_a, hot_b, h_ref, sems,
+    alpha_ref, n1_ref, half_m_ref, ksat_ref, room_ref, sat_ref, lane_par_ref,
+    total, left_a, left_b, hot_a, hot_b, h_ref, cond_ref, ratio_ref, halo_ref, sems,
 ):
     layers, rows, width = h_ref.shape
     peers, fields, per_peer = slots_ref.shape
@@ -364,7 +370,7 @@
         pltpu.make_async_copy(a, b, sems.at[i])
         for i, (a, b) in enumerate(
             [
-                (h_hbm, h_ref),
+                (h_hbm, h_ref), (cond_hbm, cond_ref), (sat_hbm, sat_ref),
                 (alpha_hbm, alpha_ref), (n1_hbm, n1_ref), (half_m_hbm, half_m_ref),
                 (ksat_hbm, ksat_ref), (room_hbm, room_ref),
             ]
@@ -413,30 +419,51 @@
         cols = slice(b * width, (b + 1) * width)
         return total[at : at + ROW_BLOCK, cols] + total[half + at : half + at + ROW_BLOCK, cols]
 
+    halo = lane_halo(own_ref[...], lane_even_ref[...], lane_odd_ref[...])
+    pars = halo_parameters(
+        table_ref,
+        pltpu.roll(halo, width - 2 * layers, 1),
+        pltpu.roll(halo, width - 4 * layers, 1),
+        edge_signs((rows, width))[2],
+    )
+    for i in range(4):
+        lane_par_ref[i] = pars[i]
+    halo_ref[0] = halo
+    halo_ref[1] = conductivity(halo, *pars)
     lanes = lax.broadcasted_iota(jnp.int32, (ROW_BLOCK, width), 1)
+    edge = (lanes == 0) | (lanes == width - 1)
     for b in range(blocks):
         span = slice(b * ROW_BLOCK, (b + 1) * ROW_BLOCK)
         packed = jnp.zeros((ROW_BLOCK, width), F32)
         infil = grid(roots, b)
         infil_ref[span, :] = infil
-        value = None
+        value = ratio = None
         for k in range(layers):
-            target = -res_ref[k, span, :]
+            halo_head = pltpu.roll(halo_ref[0, span], (width - 2 * k) % width, 1)
+            halo_cond = pltpu.roll(halo_ref[1, span], (width - 2 * k) % width, 1)
+            both = jnp.where(edge, cond_ref[k, span, :] + halo_cond, 0.0)
+            diagonal = diag_ref[k, span, :] + both
+            residual = res_ref[k, span, :] + both * (h_ref[k, span, :] - halo_head)
             if k < roots:
                 sink = grid(k, b)
                 sink_ref[k, span, :] = sink
-                target = target - sink
+                residual = residual + sink
             if k == 0:
-                target = target + infil
+                target = infil - residual
             else:
-                target = target + vert_ref[k - 1, span, :] * value
-            value = target * inv_ref[k, span, :]
+                vert = vert_ref[k - 1, span, :]
+                diagonal = diagonal - vert * ratio
+                target = vert * value - residual
+            inverse = 1.0 / diagonal
+            value = target * inverse
             head_ref[k, span, :] = value
+            if k < layers - 1:
+                ratio = vert_ref[k, span, :] * inverse
+                ratio_ref[k, span, :] = ratio
         change = value
         for k in range(layers - 1, -1, -1):
             if k < layers - 1:
-                ratio = vert_ref[k, span, :] * inv_ref[k, span, :]
-                change = head_ref[k, span, :] + ratio * change
+                change = head_ref[k, span, :] + ratio_ref[k, span, :] * change
             head = h_ref[k, span, :] + change
             head_ref[k, span, :] = head
             packed = edge_lanes((head,), k, layers, lanes, packed)
@@ -449,7 +476,7 @@
     alpha_ref, n1_ref, half_m_ref, ksat_ref, room_ref, sat_ref,
     cond_ref, stor_ref, source_ref,
 ):
-    layers, rows, width = head_ref.shape
+    layers, _, _ = head_ref.shape
     roots = sink_ref.shape[0]
     for k in range(layers):
         room = room_ref[k]
@@ -553,9 +580,7 @@
             found = jnp.dot(both, hot, preferred_element_type=F32)
             found = found[:ROW_BLOCK] + found[ROW_BLOCK:]
             mask = lax.broadcasted_iota(jnp.int32, (ROW_BLOCK, per_peer), 0) == row
-            reply_ref[pl.ds(peer, 1), :] = jnp.sum(
-                jnp.where(mask, found, 0.0), 0, keepdims=True
-            )
+            reply_ref[peer] = jnp.sum(jnp.where(mask, found, 0.0), 0, keepdims=True)
         return carry
 
     lax.fori_loop(0, peers // UNROLL, answer, 0)
@@ -585,25 +610,28 @@
 def exchange(row_even, row_odd, packed):
     even_x, odd_x, even_y, odd_y = swaps()
     axes = ("bx", "by")
+
+    def send(message, pairs):
+        return lax.ppermute(message, axes, pairs)
+
     return (
         row_even,
         row_odd,
-        lax.ppermute(row_even, axes, even_x),
-        lax.ppermute(row_odd, axes, odd_x),
+        send(row_even, even_x),
+        send(row_odd, odd_x),
         packed,
-        lax.ppermute(packed, axes, even_y),
-        lax.ppermute(packed, axes, odd_y),
-    )
-
-
-def call(kernel, ins, outs, scratch, name, limit=20, flops=0):
+        send(packed, even_y),
+        send(packed, odd_y),
+    )
+
+
+def call(kernel, ins, outs, scratch, limit=20, flops=0):
     return pl.pallas_call(
         kernel,
         in_specs=[pl.BlockSpec(memory_space=m) for m in ins],
         out_specs=[pl.BlockSpec(memory_space=m) for _, _, m in outs],
         out_shape=[HBM(s, t) if m is HBM else jax.ShapeDtypeStruct(s, t) for s, t, m in outs],
         scratch_shapes=scratch,
-        name=name,
         cost_estimate=pl.CostEstimate(flops=flops, bytes_accessed=flops, transcendentals=0),
         compiler_params=pltpu.CompilerParams(vmem_limit_bytes=limit * MIB),
     )
@@ -619,11 +647,12 @@
     return pl.pallas_call(
         prepare_kernel,
         in_specs=[pl.BlockSpec(memory_space=HBM)] * 4,
-        out_specs=pl.BlockSpec(memory_space=VMEM),
-        out_shape=VMEM((peers, roots + 2, per_peer), F32),
+        out_specs=pl.BlockSpec(memory_space=HBM),
+        out_shape=HBM((peers, roots + 2, per_peer), F32),
         scratch_shapes=[
             VMEM(root_fraction.shape, F32), VMEM(line, F32), VMEM(line, F32),
-            VMEM(line, jnp.int32), pltpu.SemaphoreType.DMA((8,)),
+            VMEM(line, jnp.int32), VMEM((peers, roots + 2, per_peer), F32),
+            pltpu.SemaphoreType.DMA((2 * prepare_steps(peers) + 3,)),
         ],
         name="prepare",
         compiler_params=pltpu.CompilerParams(vmem_limit_bytes=6 * MIB),
@@ -668,54 +697,54 @@
         [HBM] * 3,
         on_chip(cells) + [(cells, jnp.int32, VMEM)] + on_chip(cells, raw_msg, raw_msg, lane_msg),
         [semaphores((3 * chunks,))],
-        "edges",
     )(*in_hbm(h_old, soil_type, ks_scale))
     pads = [VMEM((layers, rows + 2 * PAD, width), F32)] * 2
     halo = [VMEM((2,) + lane_msg, F32)]
     arrived = exchange(row_even, row_odd, packed)
-    alpha, n1, half_m, ksat, room, old_sat, conduct, storage = call(
+    alpha, n1, half_m, ksat, room, old_sat, stored, conduct, storage = call(
         first_kernel,
         [VMEM] * 4,
-        in_main(*[cells] * 5) + on_chip(*[cells] * 3),
-        buffers(5) + [semaphores((5 * chunks,))],
-        "first",
+        in_main(*[cells] * 7) + on_chip(*[cells] * 2),
+        buffers(6) + [semaphores((7 * chunks,))],
         flops=8_000_000,
     )(head, soil, scale, table)
-    residual, inverse, vert, row_par, lane_par = call(
-        factor_kernel,
-        [VMEM] * 11,
-        on_chip(*[cells] * 3, (2, 4, layers, width), (4,) + lane_msg),
-        pads + halo,
-        "factor",
+    own_even, own_odd, row_even, row_odd, own, lane_even, lane_odd = arrived
+    residual, diagonal, vert, row_par = call(
+        balance_kernel,
+        [VMEM] * 8,
+        on_chip(*[cells] * 3, (2, 4, layers, width)),
+        pads,
         flops=4_000_000,
-    )(head, conduct, storage, table, *arrived)
+    )(head, conduct, storage, table, own_even, own_odd, row_even, row_odd)
     values = roots + 1
     columns = rows // ROW_BLOCK * width
     group = GROUP if peers % (2 * GROUP) == 0 else 1
     lefts = [VMEM((2 * values * ROW_BLOCK, group * per_peer), BF16)] * 2
     hots = [VMEM((columns, group * per_peer), BF16)] * 2
     row_msg = (1, layers, width)
-    head, sink, infil, row_even, row_odd, packed, alpha, n1, half_m, ksat, room = call(
+    (
+        head, sink, infil, row_even, row_odd, packed,
+        alpha, n1, half_m, ksat, room, old_sat, lane_par,
+    ) = call(
         middle_kernel,
-        [VMEM] + [HBM] * 6 + [VMEM] * 3,
+        [VMEM] + [HBM] * 8 + [VMEM] * 7,
         on_chip(cells, (roots, rows, width), lane_msg, row_msg, row_msg, lane_msg)
-        + on_chip(*[cells] * 5),
+        + on_chip(*[cells] * 6, (4,) + lane_msg),
         [VMEM((2 * values * ROW_BLOCK, columns), F32)] + lefts + hots
-        + buffers(1) + [semaphores((6,))],
-        "middle",
+        + buffers(3) + halo + [semaphores((8,))],
     )(
-        slots, *in_hbm(h_old, alpha, n1, half_m, ksat, room), residual, inverse, vert
+        slots, *in_hbm(h_old, stored, alpha, n1, half_m, ksat, room, old_sat),
+        residual, diagonal, vert, table, own, lane_even, lane_odd,
     )
     arrived = exchange(row_even, row_odd, packed)
     conduct, storage, source = call(
-        close_kernel, [VMEM] * 9, on_chip(*[cells] * 3), [], "close", limit=4, flops=4_000_000
+        close_kernel, [VMEM] * 9, on_chip(*[cells] * 3), [], limit=4, flops=4_000_000
     )(head, sink, infil, alpha, n1, half_m, ksat, room, old_sat)
     head, reply = call(
         last_kernel,
         [VMEM] * 18,
-        in_main(cells) + on_chip((peers, per_peer)),
+        in_main(cells) + on_chip((peers, 1, per_peer)),
         pads + buffers(3) + halo + [VMEM(lane_msg, F32), semaphores((1,))],
-        "last",
     )(
         slots, head, conduct, storage, source, sink, alpha, n1, half_m, row_par, lane_par,
         *arrived,

time: 53.2 us -> 52.1 us (0.979)
  blocking collectives: 11.4 us -> 9.98 us
    all_to_all x1, blocking collectives: 11.4 us -> 9.98 us  [on_device(): lax.all_to_all(reply, axes, split_axis=0, concat_axis=0, tiled=True)]
  transfers between devices with their start and end apart: 9 -> 9, of which waited for: 2 -> 2; matrix products, arithmetic and copies ran while one was open for 0% -> 0% of each run, Pallas kernels for 13% -> 12%
where the time goes in v3:
time: 52.1 us; the launch traced here: 51.8 us
  Pallas kernels  18 us (35%)
  starting transfers between devices  15.1 us (29%)
  blocking collectives  9.98 us (19%)
  waiting for transfers between devices  7.35 us (14%)
  between operations  0.75 us (1%)
  local copies, waits for them, and re-layouts  0.63 us (1%)
    all_to_all x1, blocking collectives, on_device(): lax.all_to_all(reply, axes, split_axis=0, concat_axis=0, tiled=True)  9.98 us
    ppermute x8, starting transfers between devices, send(): return lax.ppermute(message, axes, pairs)  7.81 us
    all_to_all x1, starting transfers between devices, on_device(): lax.all_to_all(prepare(root_fraction, transpiration, infiltration, clump_...  7.33 us
    pallas_call x1, Pallas kernels, on_device(): call(middle_kernel, [VMEM] + [HBM] * 8 + [VMEM] * 7, on_chip(cells, (root...  6.65 us
    all_to_all x1, waiting for transfers between devices, on_device(): lax.all_to_all(prepare(root_fraction, transpiration, infiltration, clump_...  5.58 us
    pallas_call x1, Pallas kernels, on_device(): call(last_kernel, [VMEM] * 18, in_main(cells) + on_chip((peers, 1, per_pe...  3.02 us
    pallas_call x1, Pallas kernels, on_device(): call(first_kernel, [VMEM] * 4, in_main(*[cells] * 7) + on_chip(*[cells] *...  2.77 us
    pallas_call x1, Pallas kernels, on_device(): call(edges_kernel, [HBM] * 3, on_chip(cells) + [(cells, jnp.int32, VMEM)]...  2.06 us
  transfers between devices with their start and end apart: 9, of which 2 were waited for; matrix products, arithmetic and copies ran while one was open for 0% of the time, Pallas kernels for 12%

profile of v3, /device:TPU:0, one launch (start us, length us, event | category | flops | bytes accessed | tf_op | source)
XLA Modules:
  0.0 51.8 jit_solution(14987749109378561734)
XLA Ops:
  0.6 1.9 %prepare.1 = f32[32,16,256]{2,1,0:T(8,128)} custom-call(f32[14,8192]{1,0:T(8,128)} %root_hbm.1, f32[1,8192]{1,0:T(1,128)} %bitcast.5, f32[1,8192]{1,0:T(1,128)} %bitcast.6, s32[1,8192]{1,0:T(1,128)} %bitcast.7), custom_call_target="tpu_custom_call" | custom-call | tf_op jit(solution)/shard_map/prepare/pallas_call | solution.py:647
  2.6 7.3 %all-to-all-start = ((f32[32,16,256]{2,1,0:T(8,128)}), f32[32,16,256]{2,1,0:T(8,128)S(1)}, u32[]{:S(2)}, u32[]{:S(2)}) async-start(f32[32,16,256]{2,1,0:T(8,128)} %prepare.1), calls=%async_computation | async-start | bytes 1048576 | tf_op jit(solution)/shard_map/all_to_all | solution.py:686
  9.9 2.1 %shard_map.95 = (f32[20,64,128]{2,1,0:T(8,128)S(1)}, s32[20,64,128]{2,1,0:T(8,128)S(1)}, f32[20,64,128]{2,1,0:T(8,128)S(1)}, f32[3,20,128]{2,1,0:T(8,128)S(1)}, ...) custom-call(f32[20,64,128]{2,1,0:T(8,128)} %h_hbm.3, s32[20,64,128]{2,1,0:T(8,128)} %soil_hbm.1, f32[20,64,128]{2,1,0:T(8,128)} %ks_hbm.1), custom_call_target="tpu_custom_call" | custom-call | tf_op jit(solution)/shard_map/pallas_call | solution.py:695
  12.0 0.0 copy-start
  12.0 0.3 collective-permute-start.3
  12.3 3.0 %collective-permute-start.2 = (f32[64,128]{1,0:T(8,128)S(1)}, f32[64,128]{1,0:T(8,128)S(1)}, u32[]{:S(2)}, u32[]{:S(2)}) collective-permute-start(f32[64,128]{1,0:T(8,128)S(1)} %get-tuple-element.56.own_ref), channel_id=1, source_target_pairs={{0,1},{1,0},{2,3},{3,2},{4,5},{5,4},{6,7},{7,6},{8,9},{9,8},{10,11... | collective-permute-start | bytes 98312 | tf_op jit(solution)/shard_map/ppermute | solution.py:615
  15.3 0.0 collective-permute-start
  15.3 1.6 %collective-permute-start.1 = (f32[3,20,128]{2,1,0:T(8,128)S(1)}, f32[3,20,128]{2,1,0:T(8,128)S(1)}, u32[]{:S(2)}, u32[]{:S(2)}) collective-permute-start(f32[3,20,128]{2,1,0:T(8,128)S(1)} %get-tuple-element.52.own_odd_ref), channel_id=1, source_target_pairs={{0,24},{1,25},{2,26},{3,27},{4,28},{5,29},{6,30},{7,31},{8,16},{9,... | collective-permute-start | bytes 92168 | tf_op jit(solution)/shard_map/ppermute | solution.py:615
  16.9 0.0 copy-done
  16.9 2.8 %shard_map.96 = (f32[20,64,128]{2,1,0:T(8,128)}, f32[20,64,128]{2,1,0:T(8,128)}, f32[20,64,128]{2,1,0:T(8,128)}, f32[20,64,128]{2,1,0:T(8,128)}, f32[20,64,128]{...) custom-call(f32[20,64,128]{2,1,0:T(8,128)S(1)} %get-tuple-element.39, ...), custom_call_target="tpu_custom_call" | custom-call | flops 8000000 | bytes 8000000 | tf_op jit(solution)/shard_map/pallas_call | solution.py:704
  19.6 0.0 collective-permute-done.row_even_ref
  19.7 0.0 collective-permute-done.1.row_odd_ref
  19.7 0.9 %shard_map.97 = (f32[20,64,128]{2,1,0:T(8,128)S(1)}, f32[20,64,128]{2,1,0:T(8,128)S(1)}, f32[20,64,128]{2,1,0:T(8,128)S(1)}, f32[2,4,20,128]{3,2,1,0:T(8,128)S(1)}) custom-call(f32[20,64,128]{2,1,0:T(8,128)S(1)} %get-tuple-element.39.h_ref, f32[20,64,128]{2,1,0:T(8,128)S(1)} %get-tuple-element.49.cond_ref, f32[20,64,128]{2,1,0:T(8,128)S(1)} %get-tuple-element.50.stor_ref, ...), custom_call_target="tpu_custom_call" | custom-call | flops 4000000 | bytes 4000000 | tf_op jit(solution)/shard_map/pallas_call | solution.py:712
  20.5 0.0 collective-permute-done.3.lane_odd_ref
  20.5 0.0 collective-permute-done.2.lane_even_ref
  20.6 5.6 %all-to-all-done.slots_ref = f32[32,16,256]{2,1,0:T(8,128)S(1)} async-done(((f32[32,16,256]{2,1,0:T(8,128)}), f32[32,16,256]{2,1,0:T(8,128)S(1)}, u32[]{:S(2)}, u32[]{:S(2)}) %all-to-all-start) | async-done | bytes 524320 | tf_op jit(solution)/shard_map/all_to_all | solution.py:686
  26.1 6.6 %shard_map.98 = (f32[20,64,128]{2,1,0:T(8,128)S(1)}, f32[14,64,128]{2,1,0:T(8,128)S(1)}, f32[64,128]{1,0:T(8,128)S(1)}, f32[1,20,128]{2,1,0:T(8,128)S(1)}, f32[1...) custom-call(f32[32,16,256]{2,1,0:T(8,128)S(1)} %all-to-all-done.slot, ...), custom_call_target="tpu_custom_call" | custom-call | tf_op jit(solution)/shard_map/pallas_call | solution.py:728
  32.8 0.1 collective-permute-start.7
  32.9 2.2 %collective-permute-start.6 = (f32[64,128]{1,0:T(8,128)S(1)}, f32[64,128]{1,0:T(8,128)S(1)}, u32[]{:S(2)}, u32[]{:S(2)}) collective-permute-start(f32[64,128]{1,0:T(8,128)S(1)} %get-tuple-element.73.own_ref), channel_id=1, source_target_pairs={{0,1},{1,0},{2,3},{3,2},{4,5},{5,4},{6,7},{7,6},{8,9},{9,8},{10,11... | collective-permute-start | bytes 98312 | tf_op jit(solution)/shard_map/ppermute | solution.py:615
  35.1 0.0 collective-permute-start.4
  35.1 0.7 %collective-permute-start.5 = (f32[1,20,128]{2,1,0:T(8,128)S(1)}, f32[1,20,128]{2,1,0:T(8,128)S(1)}, u32[]{:S(2)}, u32[]{:S(2)}) collective-permute-start(f32[1,20,128]{2,1,0:T(8,128)S(1)} %get-tuple-element.72.own_odd_ref), channel_id=1, source_target_pairs={{0,24},{1,25},{2,26},{3,27},{4,28},{5,29},{6,30},{7,31},{8,16},{9,... | collective-permute-start | bytes 30728 | tf_op jit(solution)/shard_map/ppermute | solution.py:615
  35.7 0.7 %shard_map.99 = (f32[20,64,128]{2,1,0:T(8,128)S(1)}, f32[20,64,128]{2,1,0:T(8,128)S(1)}, f32[20,64,128]{2,1,0:T(8,128)S(1)}) custom-call(f32[20,64,128]{2,1,0:T(8,128)S(1)} %get-tuple-element.57.head_ref.old_head_ref, f32[14,64,128]{2,1,0:T(8,128)S(1)} %get-tuple-element.58.sink_ref, f32[64,128]{1,0:T(8,128)S(1)} %get-tuple-element.59.infil_ref, ...), custom_call_target="tpu_custom_call" | custom-call | flops 4000000 | bytes 4000000 | tf_op jit(solution)/shard_map/pallas_call | solution.py:740
  36.4 0.0 collective-permute-done.4.row_even_ref
  36.4 1.8 %collective-permute-done.5.row_odd_ref = f32[1,20,128]{2,1,0:T(8,128)S(1)} collective-permute-done((f32[1,20,128]{2,1,0:T(8,128)S(1)}, f32[1,20,128]{2,1,0:T(8,128)S(1)}, u32[]{:S(2)}, u32[]{:S(2)}) %collective-permute-start.5) | collective-permute-done | bytes 10272 | tf_op jit(solution)/shard_map/ppermute | solution.py:615
  38.2 0.0 collective-permute-done.7.lane_odd_ref
  38.2 0.0 collective-permute-done.6.lane_even_ref
  38.2 3.0 %shard_map.100 = (f32[20,64,128]{2,1,0:T(8,128)}, f32[32,1,256]{2,1,0:T(1,128)S(1)}) custom-call(f32[32,16,256]{2,1,0:T(8,128)S(1)} %all-to-all-done.slots_ref, f32[20,64,128]{2,1,0:T(8,128)S(1)} %get-tuple-element.57.head_ref.old_head_ref, f32[20,64,128]{2,1,0:T(8,128)S(1)} %get-tuple-element.66.cond_ref, f32[20,64,128]{2,1,0:T(8,128)S(1)} %get-tuple-element.67.stor_ref, ...), custom_call_target="tpu_custom_call" | custom-call | tf_op jit(solution)/shard_map/pallas_call | solution.py:743
  41.2 10.0 %all_to_all.10 = f32[32,1,256]{2,1,0:T(1,128)S(1)} all-to-all(f32[32,1,256]{2,1,0:T(1,128)S(1)} %get-tuple-element.75), channel_id=1, replica_groups=mesh['bx'=4,'by'=8] {'bx','by'}, dimensions={0} | all-to-all | bytes 65536 | tf_op jit(solution)/shard_map/all_to_all | solution.py:752
  51.2 0.6 %copy.11 = f32[8192]{0:T(1024)} copy(f32[8192]{0:T(1024)S(1)} %bitcast.4) | data formatting | bytes 65536
  (1 shorter events, 0.0 us)
Async XLA Ops:
  2.6 23.6 %all-to-all-start = ((f32[32,16,256]{2,1,0:T(8,128)}), f32[32,16,256]{2,1,0:T(8,128)S(1)}, u32[]{:S(2)}, u32[]{:S(2)}) async-start(f32[32,16,256]{2,1,0:T(8,128)} %prepare.1), calls=%async_computation | async-start | bytes 1048576 | tf_op jit(solution)/shard_map/all_to_all | solution.py:686
  12.0 4.9 %copy-start = (f32[4,12]{1,0:T(4,128)S(1)}, f32[4,12]{1,0:T(4,128)}, u32[]{:S(2)}) copy-start(f32[4,12]{1,0:T(4,128)} %param.12) | copy-start | bytes 580
  12.0 8.6 %collective-permute-start.3 = (f32[64,128]{1,0:T(8,128)S(1)}, f32[64,128]{1,0:T(8,128)S(1)}, u32[]{:S(2)}, u32[]{:S(2)}) collective-permute-start(f32[64,128]{1,0:T(8,128)S(1)} %get-tuple-element.56.own_ref), channel_id=1, source_target_pairs={{0,8},{1,2},{2,1},{3,4},{4,3},{5,6},{6,5},{7,15},{8,0},{9,10},{10,... | collective-permute-start | bytes 98312 | tf_op jit(solution)/shard_map/ppermute | solution.py:615
  12.3 8.3 %collective-permute-start.2 = (f32[64,128]{1,0:T(8,128)S(1)}, f32[64,128]{1,0:T(8,128)S(1)}, u32[]{:S(2)}, u32[]{:S(2)}) collective-permute-start(f32[64,128]{1,0:T(8,128)S(1)} %get-tuple-element.56.own_ref), channel_id=1, source_target_pairs={{0,1},{1,0},{2,3},{3,2},{4,5},{5,4},{6,7},{7,6},{8,9},{9,8},{10,11... | collective-permute-start | bytes 98312 | tf_op jit(solution)/shard_map/ppermute | solution.py:615
  15.3 4.4 %collective-permute-start = (f32[3,20,128]{2,1,0:T(8,128)S(1)}, f32[3,20,128]{2,1,0:T(8,128)S(1)}, u32[]{:S(2)}, u32[]{:S(2)}) collective-permute-start(f32[3,20,128]{2,1,0:T(8,128)S(1)} %get-tuple-element.51.own_even_ref), channel_id=1, source_target_pairs={{0,8},{1,9},{2,10},{3,11},{4,12},{5,13},{6,14},{7,15},{8,0},{9,1},... | collective-permute-start | bytes 92168 | tf_op jit(solution)/shard_map/ppermute | solution.py:615
  15.3 4.4 %collective-permute-start.1 = (f32[3,20,128]{2,1,0:T(8,128)S(1)}, f32[3,20,128]{2,1,0:T(8,128)S(1)}, u32[]{:S(2)}, u32[]{:S(2)}) collective-permute-start(f32[3,20,128]{2,1,0:T(8,128)S(1)} %get-tuple-element.52.own_odd_ref), channel_id=1, source_target_pairs={{0,24},{1,25},{2,26},{3,27},{4,28},{5,29},{6,30},{7,31},{8,16},{9,... | collective-permute-start | bytes 92168 | tf_op jit(solution)/shard_map/ppermute | solution.py:615
  32.8 5.4 %collective-permute-start.7 = (f32[64,128]{1,0:T(8,128)S(1)}, f32[64,128]{1,0:T(8,128)S(1)}, u32[]{:S(2)}, u32[]{:S(2)}) collective-permute-start(f32[64,128]{1,0:T(8,128)S(1)} %get-tuple-element.73.own_ref), channel_id=1, source_target_pairs={{0,8},{1,2},{2,1},{3,4},{4,3},{5,6},{6,5},{7,15},{8,0},{9,10},{10,... | collective-permute-start | bytes 98312 | tf_op jit(solution)/shard_map/ppermute | solution.py:615
  32.9 5.3 %collective-permute-start.6 = (f32[64,128]{1,0:T(8,128)S(1)}, f32[64,128]{1,0:T(8,128)S(1)}, u32[]{:S(2)}, u32[]{:S(2)}) collective-permute-start(f32[64,128]{1,0:T(8,128)S(1)} %get-tuple-element.73.own_ref), channel_id=1, source_target_pairs={{0,1},{1,0},{2,3},{3,2},{4,5},{5,4},{6,7},{7,6},{8,9},{9,8},{10,11... | collective-permute-start | bytes 98312 | tf_op jit(solution)/shard_map/ppermute | solution.py:615
  35.1 1.4 %collective-permute-start.4 = (f32[1,20,128]{2,1,0:T(8,128)S(1)}, f32[1,20,128]{2,1,0:T(8,128)S(1)}, u32[]{:S(2)}, u32[]{:S(2)}) collective-permute-start(f32[1,20,128]{2,1,0:T(8,128)S(1)} %get-tuple-element.71.own_even_ref), channel_id=1, source_target_pairs={{0,8},{1,9},{2,10},{3,11},{4,12},{5,13},{6,14},{7,15},{8,0},{9,1},... | collective-permute-start | bytes 30728 | tf_op jit(solution)/shard_map/ppermute | solution.py:615
  35.1 3.1 %collective-permute-start.5 = (f32[1,20,128]{2,1,0:T(8,128)S(1)}, f32[1,20,128]{2,1,0:T(8,128)S(1)}, u32[]{:S(2)}, u32[]{:S(2)}) collective-permute-start(f32[1,20,128]{2,1,0:T(8,128)S(1)} %get-tuple-element.72.own_odd_ref), channel_id=1, source_target_pairs={{0,24},{1,25},{2,26},{3,27},{4,28},{5,29},{6,30},{7,31},{8,16},{9,... | collective-permute-start | bytes 30728 | tf_op jit(solution)/shard_map/ppermute | solution.py:615

commit v4 on v3

--- a/solution.py
+++ b/solution.py
@@ -13,6 +13,7 @@
 TINY = 1e-30
 ROW_BLOCK = 32
 HALF = 32
+LAST = 64
 UNROLL = 8
 GROUP = 4
 LOG2E = 1.4426950408889634
@@ -212,7 +213,7 @@
     edge_rows((h_ref, soil_ref, ks_ref), row_even_ref, row_odd_ref)
 
 
-def lateral_terms(k, top, size, head_pad, cond_pad, halo_head, halo_cond, lanes):
+def lateral_terms(k, top, size, head_pad, cond_pad, lanes):
     width = head_pad.shape[2]
     at = lambda pad, move: pad[k, PAD + top + move : PAD + top + move + size, :]
     head, conduct = at(head_pad, 0), at(cond_pad, 0)
@@ -222,18 +223,9 @@
         term = both * (head - at(head_pad, move))
         flow = term if flow is None else flow + term
         faces = both if faces is None else faces + both
-    if halo_head is not None:
-        halo_head = pltpu.roll(halo_head, (width - 2 * k) % width, 1)
-        halo_cond = pltpu.roll(halo_cond, (width - 2 * k) % width, 1)
     for shift, edge in ((1, lanes == 0), (width - 1, lanes == width - 1)):
-        other_head = pltpu.roll(head, shift, 1)
-        other_cond = pltpu.roll(conduct, shift, 1)
-        if halo_head is not None:
-            other_head = jnp.where(edge, halo_head, other_head)
-            both = conduct + jnp.where(edge, halo_cond, other_cond)
-        else:
-            both = jnp.where(edge, 0.0, conduct + other_cond)
-        flow = flow + both * (head - other_head)
+        both = jnp.where(edge, 0.0, conduct + pltpu.roll(conduct, shift, 1))
+        flow = flow + both * (head - pltpu.roll(head, shift, 1))
         faces = faces + both
     return head, conduct, flow, faces
 
@@ -288,7 +280,7 @@
     res_ref, diag_ref, vert_ref, row_par_ref,
     head_pad, cond_pad,
 ):
-    layers, rows, width = h_ref.shape
+    _, rows, width = h_ref.shape
     head_pad[:, PAD : PAD + rows, :] = h_ref[...]
     cond_pad[:, PAD : PAD + rows, :] = cond_ref[...]
     sign_low, sign_high, _ = edge_signs((8, width))
@@ -303,6 +295,11 @@
         row = PAD - 1 if side == 0 else PAD + rows
         head_pad[:, row, :] = head
         cond_pad[:, row, :] = conductivity(head, *pars)
+    interior(head_pad, cond_pad, stor_ref, None, res_ref, diag_ref, vert_ref)
+
+
+def interior(head_pad, cond_pad, stor_ref, source_ref, res_ref, diag_ref, vert_ref):
+    layers, rows, width = res_ref.shape
     size = HALF if rows % HALF == 0 else rows
     lanes = lax.broadcasted_iota(jnp.int32, (size, width), 1)
     for top in range(0, rows, size):
@@ -310,9 +307,7 @@
         inner = slice(PAD + top, PAD + top + size)
         vert_above = flux_above = None
         for k in range(layers):
-            head, conduct, flow, faces = lateral_terms(
-                k, top, size, head_pad, cond_pad, None, None, lanes
-            )
+            head, conduct, flow, faces = lateral_terms(k, top, size, head_pad, cond_pad, lanes)
             diagonal = stor_ref[k, span, :] + faces
             if k < layers - 1:
                 vert = VERTICAL * (conduct + cond_pad[k + 1, inner, :])
@@ -323,6 +318,8 @@
                 vert = None
                 flux = conduct * (2.0 * VERTICAL)
             residual = flux + flow
+            if source_ref is not None:
+                residual = residual + source_ref[k, span, :]
             if k:
                 residual = residual - flux_above
                 diagonal = diagonal + vert_above
@@ -337,6 +334,11 @@
         for t in lane_tables(table_ref[...], kind.shape)[:4]
     ]
     return pars[:3] + [sign * (pars[3] * ks)]
+
+
+def add_rows(array, part, row):
+    pieces = [array[:row], array[row : row + 8] + part, array[row + 8 :]]
+    return jnp.concatenate([p for p in pieces if p.shape[0]], 0)
 
 
 def slot_places(ids, width):
@@ -430,125 +432,142 @@
         lane_par_ref[i] = pars[i]
     halo_ref[0] = halo
     halo_ref[1] = conductivity(halo, *pars)
-    lanes = lax.broadcasted_iota(jnp.int32, (ROW_BLOCK, width), 1)
+    lanes = lax.broadcasted_iota(jnp.int32, (rows, width), 1)
     edge = (lanes == 0) | (lanes == width - 1)
-    for b in range(blocks):
-        span = slice(b * ROW_BLOCK, (b + 1) * ROW_BLOCK)
-        packed = jnp.zeros((ROW_BLOCK, width), F32)
-        infil = grid(roots, b)
-        infil_ref[span, :] = infil
-        value = ratio = None
-        for k in range(layers):
-            halo_head = pltpu.roll(halo_ref[0, span], (width - 2 * k) % width, 1)
-            halo_cond = pltpu.roll(halo_ref[1, span], (width - 2 * k) % width, 1)
-            both = jnp.where(edge, cond_ref[k, span, :] + halo_cond, 0.0)
-            diagonal = diag_ref[k, span, :] + both
-            residual = res_ref[k, span, :] + both * (h_ref[k, span, :] - halo_head)
-            if k < roots:
-                sink = grid(k, b)
-                sink_ref[k, span, :] = sink
-                residual = residual + sink
-            if k == 0:
-                target = infil - residual
-            else:
-                vert = vert_ref[k - 1, span, :]
-                diagonal = diagonal - vert * ratio
-                target = vert * value - residual
-            inverse = 1.0 / diagonal
-            value = target * inverse
-            head_ref[k, span, :] = value
-            if k < layers - 1:
-                ratio = vert_ref[k, span, :] * inverse
-                ratio_ref[k, span, :] = ratio
-        change = value
-        for k in range(layers - 1, -1, -1):
-            if k < layers - 1:
-                change = head_ref[k, span, :] + ratio_ref[k, span, :] * change
-            head = h_ref[k, span, :] + change
-            head_ref[k, span, :] = head
-            packed = edge_lanes((head,), k, layers, lanes, packed)
-        lane_ref[span, :] = packed
+    whole = lambda f: jnp.concatenate([grid(f, b) for b in range(blocks)], 0)
+    infil = whole(roots)
+    infil_ref[...] = infil
+    value = ratio = None
+    for k in range(layers):
+        halo_head = pltpu.roll(halo_ref[0], (width - 2 * k) % width, 1)
+        halo_cond = pltpu.roll(halo_ref[1], (width - 2 * k) % width, 1)
+        both = jnp.where(edge, cond_ref[k] + halo_cond, 0.0)
+        diagonal = diag_ref[k] + both
+        residual = res_ref[k] + both * (h_ref[k] - halo_head)
+        if k < roots:
+            sink = whole(k)
+            sink_ref[k] = sink
+            residual = residual + sink
+        if k == 0:
+            target = infil - residual
+        else:
+            vert = vert_ref[k - 1]
+            diagonal = diagonal - vert * ratio
+            target = vert * value - residual
+        inverse = 1.0 / diagonal
+        value = target * inverse
+        head_ref[k] = value
+        if k < layers - 1:
+            ratio = vert_ref[k] * inverse
+            ratio_ref[k] = ratio
+    change = value
+    packed = jnp.zeros((rows, width), F32)
+    for k in range(layers - 1, -1, -1):
+        if k < layers - 1:
+            change = head_ref[k] + ratio_ref[k] * change
+        head = h_ref[k] + change
+        head_ref[k] = head
+        packed = edge_lanes((head,), k, layers, lanes, packed)
+    lane_ref[...] = packed
     edge_rows((head_ref,), row_even_ref, row_odd_ref)
 
 
 def close_kernel(
     head_ref, sink_ref, infil_ref,
     alpha_ref, n1_ref, half_m_ref, ksat_ref, room_ref, sat_ref,
-    cond_ref, stor_ref, source_ref,
+    cond_ref, res_ref, diag_ref, vert_ref, denom_ref,
+    head_pad, cond_pad, stor_ref, source_ref,
 ):
-    layers, _, _ = head_ref.shape
+    layers, rows, _ = head_ref.shape
     roots = sink_ref.shape[0]
+    denom = None
     for k in range(layers):
         room = room_ref[k]
+        head = head_ref[k]
         saturation, conduct, storage = closure(
-            head_ref[k], alpha_ref[k], n1_ref[k], half_m_ref[k], ksat_ref[k], room
+            head, alpha_ref[k], n1_ref[k], half_m_ref[k], ksat_ref[k], room
         )
         cond_ref[k] = conduct
+        head_pad[k, PAD : PAD + rows, :] = head
+        cond_pad[k, PAD : PAD + rows, :] = conduct
+        for row, beyond in ((0, PAD - 1), (rows - 1, PAD + rows)):
+            head_pad[k, beyond : beyond + 1, :] = head[row : row + 1]
+            cond_pad[k, beyond : beyond + 1, :] = -conduct[row : row + 1]
         stor_ref[k] = storage
         source = room * (saturation - sat_ref[k])
         if k < roots:
-            source = source + sink_ref[k]
+            sink = sink_ref[k]
+            source = source + sink
+            denom = sink if denom is None else denom + sink
         if k == 0:
             source = source - infil_ref[...]
         source_ref[k] = source
+    denom_ref[...] = denom
+    interior(head_pad, cond_pad, stor_ref, source_ref, res_ref, diag_ref, vert_ref)
 
 
 def last_kernel(
-    slots_ref, old_head_ref, cond_ref, stor_ref, source_ref, sink_ref,
+    slots_ref, old_head_ref, cond_ref, old_res_ref, old_diag_ref, vert_ref, denom_ref, sink_ref,
     alpha_ref, n1_ref, half_m_ref, row_par_ref, lane_par_ref,
     own_even_ref, own_odd_ref, row_even_ref, row_odd_ref, own_ref, lane_even_ref, lane_odd_ref,
     head_hbm, reply_ref,
-    head_pad, cond_pad, head_ref, ratio_ref, value_ref, halo_ref, stress_ref, sems,
+    head_ref, ratio_ref, value_ref, halo_ref, side_ref, stress_ref, sems,
 ):
     layers, rows, width = head_ref.shape
     peers, fields, per_peer = slots_ref.shape
     roots = fields - 2
     blocks = rows // ROW_BLOCK
-    head_pad[:, PAD : PAD + rows, :] = old_head_ref[...]
-    cond_pad[:, PAD : PAD + rows, :] = cond_ref[...]
     sides = row_halo(own_even_ref[0], own_odd_ref[0], row_even_ref[0], row_odd_ref[0])
-    for side, row in ((0, PAD - 1), (1, PAD + rows)):
-        head_pad[:, row, :] = sides[side]
-        pars = [row_par_ref[side, i] for i in range(4)]
-        cond_pad[:, row, :] = conductivity(sides[side], *pars)
+    for side in range(2):
+        side_ref[side, 0] = sides[side]
+        side_ref[side, 1] = conductivity(sides[side], *(row_par_ref[side, i] for i in range(4)))
     halo = lane_halo(own_ref[...], lane_even_ref[...], lane_odd_ref[...])
     halo_ref[0] = halo
     halo_ref[1] = conductivity(halo, *(lane_par_ref[i] for i in range(4)))
-    size = HALF if rows % HALF == 0 else rows
+    size = LAST if rows % LAST == 0 else rows
     lanes = lax.broadcasted_iota(jnp.int32, (size, width), 1)
+    edge = (lanes == 0) | (lanes == width - 1)
+    places = lax.broadcasted_iota(jnp.int32, (8, width), 0)
     for top in range(0, rows, size):
         span = slice(top, top + size)
-        vert_above = flux_above = ratio_above = value = None
+        value = ratio = None
         for k in range(layers):
-            head, conduct, flow, faces = lateral_terms(
-                k, top, size, head_pad, cond_pad, halo_ref[0, span], halo_ref[1, span], lanes
-            )
-            diagonal = stor_ref[k, span, :] + faces
+            head, conduct = old_head_ref[k, span, :], cond_ref[k, span, :]
+            halo_head = pltpu.roll(halo_ref[0, span], (width - 2 * k) % width, 1)
+            halo_cond = pltpu.roll(halo_ref[1, span], (width - 2 * k) % width, 1)
+            both = jnp.where(edge, conduct + halo_cond, 0.0)
+            faces = both
+            flow = both * (head - halo_head)
+            for side, row, holds in (
+                (0, 0, top == 0), (1, size - 8, top + size == rows)
+            ):
+                if holds:
+                    part = slice(row, row + 8)
+                    both = jnp.where(
+                        places == (0 if side == 0 else 7),
+                        conduct[part] + side_ref[side, 1, k : k + 1, :],
+                        0.0,
+                    )
+                    more = both * (head[part] - side_ref[side, 0, k : k + 1, :])
+                    faces = add_rows(faces, both, row)
+                    flow = add_rows(flow, more, row)
+            diagonal = old_diag_ref[k, span, :] + faces
+            residual = old_res_ref[k, span, :] + flow
+            if k:
+                vert = vert_ref[k - 1, span, :]
+                diagonal = diagonal - vert * ratio
+                target = vert * value - residual
+            else:
+                target = -residual
+            inverse = 1.0 / diagonal
+            value = target * inverse
+            value_ref[k, span, :] = value
             if k < layers - 1:
-                vert = VERTICAL * (conduct + cond_ref[k + 1, span, :])
-                flux = vert * (head - old_head_ref[k + 1, span, :] + 1.0)
-                diagonal = diagonal + vert
-            else:
-                vert = None
-                flux = conduct * (2.0 * VERTICAL)
-            residual = flux + flow + source_ref[k, span, :]
-            if k:
-                residual = residual - flux_above
-                diagonal = diagonal + vert_above
-                diagonal = diagonal - vert_above * ratio_above
-                inverse = 1.0 / diagonal
-                value = (vert_above * value - residual) * inverse
-            else:
-                inverse = 1.0 / diagonal
-                value = -residual * inverse
-            value_ref[k, span, :] = value
-            if vert is not None:
-                ratio_above = vert * inverse
-                ratio_ref[k, span, :] = ratio_above
-            vert_above, flux_above = vert, flux
+                ratio = vert_ref[k, span, :] * inverse
+                ratio_ref[k, span, :] = ratio
         change = value
         head_ref[layers - 1, span, :] = old_head_ref[layers - 1, span, :] + change
-        numer = denom = None
+        numer = None
         for k in range(layers - 2, -1, -1):
             change = value_ref[k, span, :] + ratio_ref[k, span, :] * change
             head = old_head_ref[k, span, :] + change
@@ -557,10 +576,9 @@
                 half = powers(
                     head, alpha_ref[k, span, :], n1_ref[k, span, :], half_m_ref[k, span, :]
                 )[2]
-                sink = sink_ref[k, span, :]
-                term = sink * jnp.exp2(half + half)
+                term = sink_ref[k, span, :] * jnp.exp2(half + half)
                 numer = term if numer is None else numer + term
-                denom = sink if denom is None else denom + sink
+        denom = denom_ref[span, :]
         held = denom > 0.0
         stress_ref[span, :] = jnp.where(held, numer / jnp.where(held, denom, 1.0), 0.0)
     leave = pltpu.make_async_copy(head_ref, head_hbm, sems.at[0])
@@ -737,17 +755,23 @@
         residual, diagonal, vert, table, own, lane_even, lane_odd,
     )
     arrived = exchange(row_even, row_odd, packed)
-    conduct, storage, source = call(
-        close_kernel, [VMEM] * 9, on_chip(*[cells] * 3), [], limit=4, flops=4_000_000
+    conduct, residual, diagonal, vert, denom = call(
+        close_kernel,
+        [VMEM] * 9,
+        on_chip(*[cells] * 4, lane_msg),
+        pads + buffers(2),
+        limit=8,
+        flops=8_000_000,
     )(head, sink, infil, alpha, n1, half_m, ksat, room, old_sat)
     head, reply = call(
         last_kernel,
-        [VMEM] * 18,
+        [VMEM] * 20,
         in_main(cells) + on_chip((peers, 1, per_peer)),
-        pads + buffers(3) + halo + [VMEM(lane_msg, F32), semaphores((1,))],
+        buffers(3) + halo
+        + [VMEM((2, 2, layers, width), F32), VMEM(lane_msg, F32), semaphores((1,))],
     )(
-        slots, head, conduct, storage, source, sink, alpha, n1, half_m, row_par, lane_par,
-        *arrived,
+        slots, head, conduct, residual, diagonal, vert, denom, sink, alpha, n1, half_m,
+        row_par, lane_par, *arrived,
     )
     stress = lax.all_to_all(reply, axes, split_axis=0, concat_axis=0, tiled=True)
     return head, stress.reshape(slot_count)

time: 52.1 us -> 51.3 us (0.985)
  waiting for transfers between devices: 7.35 us -> 6.51 us
    ppermute x8, waiting for transfers between devices: 1.78 us -> 0.93 us  [send(): return lax.ppermute(message, axes, pairs)]
  transfers between devices with their start and end apart: 9 -> 9, of which waited for: 2 -> 2; matrix products, arithmetic and copies ran while one was open for 0% -> 0% of each run, Pallas kernels for 12% -> 14%
where the time goes in v4:
time: 51.3 us; the launch traced here: 51.1 us
  Pallas kernels  18 us (35%)
  starting transfers between devices  15.1 us (29%)
  blocking collectives  9.99 us (19%)
  waiting for transfers between devices  6.51 us (13%)
  between operations  0.75 us (1%)
  local copies, waits for them, and re-layouts  0.63 us (1%)
    all_to_all x1, blocking collectives, on_device(): lax.all_to_all(reply, axes, split_axis=0, concat_axis=0, tiled=True)  9.99 us
    ppermute x8, starting transfers between devices, send(): return lax.ppermute(message, axes, pairs)  7.82 us
    all_to_all x1, starting transfers between devices, on_device(): lax.all_to_all(prepare(root_fraction, transpiration, infiltration, clump_...  7.33 us
    pallas_call x1, Pallas kernels, on_device(): call(middle_kernel, [VMEM] + [HBM] * 8 + [VMEM] * 7, on_chip(cells, (root...  6.62 us
    all_to_all x1, waiting for transfers between devices, on_device(): lax.all_to_all(prepare(root_fraction, transpiration, infiltration, clump_...  5.58 us
    pallas_call x1, Pallas kernels, on_device(): call(first_kernel, [VMEM] * 4, in_main(*[cells] * 7) + on_chip(*[cells] *...  2.77 us
    pallas_call x1, Pallas kernels, on_device(): call(last_kernel, [VMEM] * 20, in_main(cells) + on_chip((peers, 1, per_pe...  2.25 us
    pallas_call x1, Pallas kernels, on_device(): call(edges_kernel, [HBM] * 3, on_chip(cells) + [(cells, jnp.int32, VMEM)]...  2.06 us
  transfers between devices with their start and end apart: 9, of which 2 were waited for; matrix products, arithmetic and copies ran while one was open for 0% of the time, Pallas kernels for 14%

profile of v4, /device:TPU:0, one launch (start us, length us, event | category | flops | bytes accessed | tf_op | source)
XLA Modules:
  0.0 51.1 jit_solution(5157162311213150816)
XLA Ops:
  0.6 1.9 %prepare.1 = f32[32,16,256]{2,1,0:T(8,128)} custom-call(f32[14,8192]{1,0:T(8,128)} %root_hbm.1, f32[1,8192]{1,0:T(1,128)} %bitcast.5, f32[1,8192]{1,0:T(1,128)} %bitcast.6, s32[1,8192]{1,0:T(1,128)} %bitcast.7), custom_call_target="tpu_custom_call" | custom-call | tf_op jit(solution)/shard_map/prepare/pallas_call | solution.py:665
  2.6 7.3 %all-to-all-start = ((f32[32,16,256]{2,1,0:T(8,128)}), f32[32,16,256]{2,1,0:T(8,128)S(1)}, u32[]{:S(2)}, u32[]{:S(2)}) async-start(f32[32,16,256]{2,1,0:T(8,128)} %prepare.1), calls=%async_computation | async-start | bytes 1048576 | tf_op jit(solution)/shard_map/all_to_all | solution.py:704
  9.9 2.1 %shard_map.95 = (f32[20,64,128]{2,1,0:T(8,128)S(1)}, s32[20,64,128]{2,1,0:T(8,128)S(1)}, f32[20,64,128]{2,1,0:T(8,128)S(1)}, f32[3,20,128]{2,1,0:T(8,128)S(1)}, ...) custom-call(f32[20,64,128]{2,1,0:T(8,128)} %h_hbm.3, s32[20,64,128]{2,1,0:T(8,128)} %soil_hbm.1, f32[20,64,128]{2,1,0:T(8,128)} %ks_hbm.1), custom_call_target="tpu_custom_call" | custom-call | tf_op jit(solution)/shard_map/pallas_call | solution.py:713
  12.0 0.0 copy-start
  12.0 0.3 collective-permute-start.3
  12.3 3.0 %collective-permute-start.2 = (f32[64,128]{1,0:T(8,128)S(1)}, f32[64,128]{1,0:T(8,128)S(1)}, u32[]{:S(2)}, u32[]{:S(2)}) collective-permute-start(f32[64,128]{1,0:T(8,128)S(1)} %get-tuple-element.58.own_ref), channel_id=1, source_target_pairs={{0,1},{1,0},{2,3},{3,2},{4,5},{5,4},{6,7},{7,6},{8,9},{9,8},{10,11... | collective-permute-start | bytes 98312 | tf_op jit(solution)/shard_map/ppermute | solution.py:633
  15.3 0.0 collective-permute-start
  15.3 1.6 %collective-permute-start.1 = (f32[3,20,128]{2,1,0:T(8,128)S(1)}, f32[3,20,128]{2,1,0:T(8,128)S(1)}, u32[]{:S(2)}, u32[]{:S(2)}) collective-permute-start(f32[3,20,128]{2,1,0:T(8,128)S(1)} %get-tuple-element.54.own_odd_ref), channel_id=1, source_target_pairs={{0,24},{1,25},{2,26},{3,27},{4,28},{5,29},{6,30},{7,31},{8,16},{9,... | collective-permute-start | bytes 92168 | tf_op jit(solution)/shard_map/ppermute | solution.py:633
  16.9 0.0 copy-done
  16.9 2.8 %shard_map.96 = (f32[20,64,128]{2,1,0:T(8,128)}, f32[20,64,128]{2,1,0:T(8,128)}, f32[20,64,128]{2,1,0:T(8,128)}, f32[20,64,128]{2,1,0:T(8,128)}, f32[20,64,128]{...) custom-call(f32[20,64,128]{2,1,0:T(8,128)S(1)} %get-tuple-element.41, ...), custom_call_target="tpu_custom_call" | custom-call | flops 8000000 | bytes 8000000 | tf_op jit(solution)/shard_map/pallas_call | solution.py:722
  19.6 0.0 collective-permute-done.row_even_ref
  19.7 0.0 collective-permute-done.1.row_odd_ref
  19.7 0.9 %shard_map.97 = (f32[20,64,128]{2,1,0:T(8,128)S(1)}, f32[20,64,128]{2,1,0:T(8,128)S(1)}, f32[20,64,128]{2,1,0:T(8,128)S(1)}, f32[2,4,20,128]{3,2,1,0:T(8,128)S(1)}) custom-call(f32[20,64,128]{2,1,0:T(8,128)S(1)} %get-tuple-element.41.h_ref, f32[20,64,128]{2,1,0:T(8,128)S(1)} %get-tuple-element.51.cond_ref, f32[20,64,128]{2,1,0:T(8,128)S(1)} %get-tuple-element.52.stor_ref, ...), custom_call_target="tpu_custom_call" | custom-call | flops 4000000 | bytes 4000000 | tf_op jit(solution)/shard_map/pallas_call | solution.py:730
  20.5 0.0 collective-permute-done.3.lane_odd_ref
  20.5 0.0 collective-permute-done.2.lane_even_ref
  20.6 5.6 %all-to-all-done.slots_ref = f32[32,16,256]{2,1,0:T(8,128)S(1)} async-done(((f32[32,16,256]{2,1,0:T(8,128)}), f32[32,16,256]{2,1,0:T(8,128)S(1)}, u32[]{:S(2)}, u32[]{:S(2)}) %all-to-all-start) | async-done | bytes 524320 | tf_op jit(solution)/shard_map/all_to_all | solution.py:704
  26.1 6.6 %shard_map.98 = (f32[20,64,128]{2,1,0:T(8,128)S(1)}, f32[14,64,128]{2,1,0:T(8,128)S(1)}, f32[64,128]{1,0:T(8,128)S(1)}, f32[1,20,128]{2,1,0:T(8,128)S(1)}, f32[1...) custom-call(f32[32,16,256]{2,1,0:T(8,128)S(1)} %all-to-all-done.slot, ...), custom_call_target="tpu_custom_call" | custom-call | tf_op jit(solution)/shard_map/pallas_call | solution.py:746
  32.8 0.1 collective-permute-start.7
  32.8 2.2 %collective-permute-start.6 = (f32[64,128]{1,0:T(8,128)S(1)}, f32[64,128]{1,0:T(8,128)S(1)}, u32[]{:S(2)}, u32[]{:S(2)}) collective-permute-start(f32[64,128]{1,0:T(8,128)S(1)} %get-tuple-element.77.own_ref), channel_id=1, source_target_pairs={{0,1},{1,0},{2,3},{3,2},{4,5},{5,4},{6,7},{7,6},{8,9},{9,8},{10,11... | collective-permute-start | bytes 98312 | tf_op jit(solution)/shard_map/ppermute | solution.py:633
  35.1 0.0 collective-permute-start.4
  35.1 0.7 %collective-permute-start.5 = (f32[1,20,128]{2,1,0:T(8,128)S(1)}, f32[1,20,128]{2,1,0:T(8,128)S(1)}, u32[]{:S(2)}, u32[]{:S(2)}) collective-permute-start(f32[1,20,128]{2,1,0:T(8,128)S(1)} %get-tuple-element.76.own_odd_ref), channel_id=1, source_target_pairs={{0,24},{1,25},{2,26},{3,27},{4,28},{5,29},{6,30},{7,31},{8,16},{9,... | collective-permute-start | bytes 30728 | tf_op jit(solution)/shard_map/ppermute | solution.py:633
  35.7 1.5 %shard_map.99 = (f32[20,64,128]{2,1,0:T(8,128)S(1)}, f32[20,64,128]{2,1,0:T(8,128)S(1)}, f32[20,64,128]{2,1,0:T(8,128)S(1)}, f32[20,64,128]{2,1,0:T(8,128)S(1)}, f32[64,128]{1,0:T(8,128)S(1)}) custom-call(f32[20,64,128]{2,1,0:T(8,128)S(1)} %get-tuple-element.59.head_ref.old_head_ref, f32[14,64,128]{2,1,0:T(8,128)S(1)} %get-tuple-element.60.sink_ref, ...), custom_call_target="tpu_custom_call" | custom-call | flops 8000000 | bytes 8000000 | tf_op jit(solution)/shard_map/pallas_call | solution.py:758
  37.3 0.0 collective-permute-done.4.row_even_ref
  37.3 0.9 %collective-permute-done.5.row_odd_ref = f32[1,20,128]{2,1,0:T(8,128)S(1)} collective-permute-done((f32[1,20,128]{2,1,0:T(8,128)S(1)}, f32[1,20,128]{2,1,0:T(8,128)S(1)}, u32[]{:S(2)}, u32[]{:S(2)}) %collective-permute-start.5) | collective-permute-done | bytes 10272 | tf_op jit(solution)/shard_map/ppermute | solution.py:633
  38.2 0.0 collective-permute-done.7.lane_odd_ref
  38.2 0.0 collective-permute-done.6.lane_even_ref
  38.2 2.2 %shard_map.100 = (f32[20,64,128]{2,1,0:T(8,128)}, f32[32,1,256]{2,1,0:T(1,128)S(1)}) custom-call(f32[32,16,256]{2,1,0:T(8,128)S(1)} %all-to-all-done.slots_ref, f32[20,64,128]{2,1,0:T(8,128)S(1)} %get-tuple-element.59.head_ref.old_head_ref, f32[20,64,128]{2,1,0:T(8,128)S(1)} %get-tuple-element.68.cond_ref, f32[20,64,128]{2,1,0:T(8,128)S(1)} %get-tuple-element.69.old_res_ref, ...), custom_call_target="tpu_custom_call" | custom-call | tf_op jit(solution)/shard_map/pallas_call | solution.py:766
  40.4 10.0 %all_to_all.10 = f32[32,1,256]{2,1,0:T(1,128)S(1)} all-to-all(f32[32,1,256]{2,1,0:T(1,128)S(1)} %get-tuple-element.79), channel_id=1, replica_groups=mesh['bx'=4,'by'=8] {'bx','by'}, dimensions={0} | all-to-all | bytes 65536 | tf_op jit(solution)/shard_map/all_to_all | solution.py:776
  50.4 0.6 %copy.11 = f32[8192]{0:T(1024)} copy(f32[8192]{0:T(1024)S(1)} %bitcast.4) | data formatting | bytes 65536
  (1 shorter events, 0.0 us)
Async XLA Ops:
  2.6 23.6 %all-to-all-start = ((f32[32,16,256]{2,1,0:T(8,128)}), f32[32,16,256]{2,1,0:T(8,128)S(1)}, u32[]{:S(2)}, u32[]{:S(2)}) async-start(f32[32,16,256]{2,1,0:T(8,128)} %prepare.1), calls=%async_computation | async-start | bytes 1048576 | tf_op jit(solution)/shard_map/all_to_all | solution.py:704
  12.0 4.9 %copy-start = (f32[4,12]{1,0:T(4,128)S(1)}, f32[4,12]{1,0:T(4,128)}, u32[]{:S(2)}) copy-start(f32[4,12]{1,0:T(4,128)} %param.12) | copy-start | bytes 580
  12.0 8.6 %collective-permute-start.3 = (f32[64,128]{1,0:T(8,128)S(1)}, f32[64,128]{1,0:T(8,128)S(1)}, u32[]{:S(2)}, u32[]{:S(2)}) collective-permute-start(f32[64,128]{1,0:T(8,128)S(1)} %get-tuple-element.58.own_ref), channel_id=1, source_target_pairs={{0,8},{1,2},{2,1},{3,4},{4,3},{5,6},{6,5},{7,15},{8,0},{9,10},{10,... | collective-permute-start | bytes 98312 | tf_op jit(solution)/shard_map/ppermute | solution.py:633
  12.3 8.3 %collective-permute-start.2 = (f32[64,128]{1,0:T(8,128)S(1)}, f32[64,128]{1,0:T(8,128)S(1)}, u32[]{:S(2)}, u32[]{:S(2)}) collective-permute-start(f32[64,128]{1,0:T(8,128)S(1)} %get-tuple-element.58.own_ref), channel_id=1, source_target_pairs={{0,1},{1,0},{2,3},{3,2},{4,5},{5,4},{6,7},{7,6},{8,9},{9,8},{10,11... | collective-permute-start | bytes 98312 | tf_op jit(solution)/shard_map/ppermute | solution.py:633
  15.3 4.4 %collective-permute-start = (f32[3,20,128]{2,1,0:T(8,128)S(1)}, f32[3,20,128]{2,1,0:T(8,128)S(1)}, u32[]{:S(2)}, u32[]{:S(2)}) collective-permute-start(f32[3,20,128]{2,1,0:T(8,128)S(1)} %get-tuple-element.53.own_even_ref), channel_id=1, source_target_pairs={{0,8},{1,9},{2,10},{3,11},{4,12},{5,13},{6,14},{7,15},{8,0},{9,1},... | collective-permute-start | bytes 92168 | tf_op jit(solution)/shard_map/ppermute | solution.py:633
  15.3 4.4 %collective-permute-start.1 = (f32[3,20,128]{2,1,0:T(8,128)S(1)}, f32[3,20,128]{2,1,0:T(8,128)S(1)}, u32[]{:S(2)}, u32[]{:S(2)}) collective-permute-start(f32[3,20,128]{2,1,0:T(8,128)S(1)} %get-tuple-element.54.own_odd_ref), channel_id=1, source_target_pairs={{0,24},{1,25},{2,26},{3,27},{4,28},{5,29},{6,30},{7,31},{8,16},{9,... | collective-permute-start | bytes 92168 | tf_op jit(solution)/shard_map/ppermute | solution.py:633
  32.8 5.4 %collective-permute-start.7 = (f32[64,128]{1,0:T(8,128)S(1)}, f32[64,128]{1,0:T(8,128)S(1)}, u32[]{:S(2)}, u32[]{:S(2)}) collective-permute-start(f32[64,128]{1,0:T(8,128)S(1)} %get-tuple-element.77.own_ref), channel_id=1, source_target_pairs={{0,8},{1,2},{2,1},{3,4},{4,3},{5,6},{6,5},{7,15},{8,0},{9,10},{10,... | collective-permute-start | bytes 98312 | tf_op jit(solution)/shard_map/ppermute | solution.py:633
  32.8 5.3 %collective-permute-start.6 = (f32[64,128]{1,0:T(8,128)S(1)}, f32[64,128]{1,0:T(8,128)S(1)}, u32[]{:S(2)}, u32[]{:S(2)}) collective-permute-start(f32[64,128]{1,0:T(8,128)S(1)} %get-tuple-element.77.own_ref), channel_id=1, source_target_pairs={{0,1},{1,0},{2,3},{3,2},{4,5},{5,4},{6,7},{7,6},{8,9},{9,8},{10,11... | collective-permute-start | bytes 98312 | tf_op jit(solution)/shard_map/ppermute | solution.py:633
  35.1 2.2 %collective-permute-start.4 = (f32[1,20,128]{2,1,0:T(8,128)S(1)}, f32[1,20,128]{2,1,0:T(8,128)S(1)}, u32[]{:S(2)}, u32[]{:S(2)}) collective-permute-start(f32[1,20,128]{2,1,0:T(8,128)S(1)} %get-tuple-element.75.own_even_ref), channel_id=1, source_target_pairs={{0,8},{1,9},{2,10},{3,11},{4,12},{5,13},{6,14},{7,15},{8,0},{9,1},... | collective-permute-start | bytes 30728 | tf_op jit(solution)/shard_map/ppermute | solution.py:633
  35.1 3.1 %collective-permute-start.5 = (f32[1,20,128]{2,1,0:T(8,128)S(1)}, f32[1,20,128]{2,1,0:T(8,128)S(1)}, u32[]{:S(2)}, u32[]{:S(2)}) collective-permute-start(f32[1,20,128]{2,1,0:T(8,128)S(1)} %get-tuple-element.76.own_odd_ref), channel_id=1, source_target_pairs={{0,24},{1,25},{2,26},{3,27},{4,28},{5,29},{6,30},{7,31},{8,16},{9,... | collective-permute-start | bytes 30728 | tf_op jit(solution)/shard_map/ppermute | solution.py:633

commit v5 on v4

--- a/solution.py
+++ b/solution.py
@@ -14,7 +14,7 @@
 ROW_BLOCK = 32
 HALF = 32
 LAST = 64
-UNROLL = 8
+UNROLL = 16
 GROUP = 4
 LOG2E = 1.4426950408889634
 PAD = 8
@@ -516,7 +516,6 @@
     layers, rows, width = head_ref.shape
     peers, fields, per_peer = slots_ref.shape
     roots = fields - 2
-    blocks = rows // ROW_BLOCK
     sides = row_halo(own_even_ref[0], own_odd_ref[0], row_even_ref[0], row_odd_ref[0])
     for side in range(2):
         side_ref[side, 0] = sides[side]
@@ -583,21 +582,19 @@
         stress_ref[span, :] = jnp.where(held, numer / jnp.where(held, denom, 1.0), 0.0)
     leave = pltpu.make_async_copy(head_ref, head_hbm, sems.at[0])
     leave.start()
-    wide = jnp.concatenate(
-        [stress_ref[b * ROW_BLOCK : (b + 1) * ROW_BLOCK, :] for b in range(blocks)], 1
-    )
-    high = wide.astype(BF16)
-    both = jnp.concatenate([high, (wide - high.astype(F32)).astype(BF16)], 0)
+    stress = stress_ref[...]
+    high = stress.astype(BF16)
+    both = jnp.concatenate([high, (stress - high.astype(F32)).astype(BF16)], 0)
 
     def answer(block, carry):
         for g in range(UNROLL):
             peer = block * UNROLL + g
             ids = slots_ref[peer, fields - 1 : fields, :].astype(jnp.int32)
-            row, column = slot_places(ids, width)
-            hot = one_hot(column, blocks * width)
+            hot = one_hot(ids & (width - 1), width)
             found = jnp.dot(both, hot, preferred_element_type=F32)
-            found = found[:ROW_BLOCK] + found[ROW_BLOCK:]
-            mask = lax.broadcasted_iota(jnp.int32, (ROW_BLOCK, per_peer), 0) == row
+            found = found[:rows] + found[rows:]
+            place = lax.broadcasted_iota(jnp.int32, (rows, per_peer), 0)
+            mask = place == (ids >> (width.bit_length() - 1))
             reply_ref[peer] = jnp.sum(jnp.where(mask, found, 0.0), 0, keepdims=True)
         return carry
 

time: 51.3 us -> 51.1 us (level)
  no operation moved by 1% of the time
where the time goes in v5:
time: 51.1 us; the launch traced here: 50.8 us
  Pallas kernels  17.8 us (35%)
  starting transfers between devices  15.1 us (30%)
  blocking collectives  9.99 us (20%)
  waiting for transfers between devices  6.51 us (13%)
  between operations  0.75 us (1%)
  local copies, waits for them, and re-layouts  0.63 us (1%)
    all_to_all x1, blocking collectives, on_device(): lax.all_to_all(reply, axes, split_axis=0, concat_axis=0, tiled=True)  9.99 us
    ppermute x8, starting transfers between devices, send(): return lax.ppermute(message, axes, pairs)  7.82 us
    all_to_all x1, starting transfers between devices, on_device(): lax.all_to_all(prepare(root_fraction, transpiration, infiltration, clump_...  7.33 us
    pallas_call x1, Pallas kernels, on_device(): call(middle_kernel, [VMEM] + [HBM] * 8 + [VMEM] * 7, on_chip(cells, (root...  6.62 us
    all_to_all x1, waiting for transfers between devices, on_device(): lax.all_to_all(prepare(root_fraction, transpiration, infiltration, clump_...  5.58 us
    pallas_call x1, Pallas kernels, on_device(): call(first_kernel, [VMEM] * 4, in_main(*[cells] * 7) + on_chip(*[cells] *...  2.77 us
    pallas_call x1, Pallas kernels, on_device(): call(edges_kernel, [HBM] * 3, on_chip(cells) + [(cells, jnp.int32, VMEM)]...  2.06 us
    pallas_call x1, Pallas kernels, on_device(): call(last_kernel, [VMEM] * 20, in_main(cells) + on_chip((peers, 1, per_pe...  2.03 us
  transfers between devices with their start and end apart: 9, of which 2 were waited for; matrix products, arithmetic and copies ran while one was open for 0% of the time, Pallas kernels for 14%

profile of v5, /device:TPU:0, one launch (start us, length us, event | category | flops | bytes accessed | tf_op | source)
XLA Modules:
  0.0 50.8 jit_solution(15124500724451655450)
XLA Ops:
  0.6 1.9 %prepare.1 = f32[32,16,256]{2,1,0:T(8,128)} custom-call(f32[14,8192]{1,0:T(8,128)} %root_hbm.1, f32[1,8192]{1,0:T(1,128)} %bitcast.5, f32[1,8192]{1,0:T(1,128)} %bitcast.6, s32[1,8192]{1,0:T(1,128)} %bitcast.7), custom_call_target="tpu_custom_call" | custom-call | tf_op jit(solution)/shard_map/prepare/pallas_call | solution.py:662
  2.6 7.3 %all-to-all-start = ((f32[32,16,256]{2,1,0:T(8,128)}), f32[32,16,256]{2,1,0:T(8,128)S(1)}, u32[]{:S(2)}, u32[]{:S(2)}) async-start(f32[32,16,256]{2,1,0:T(8,128)} %prepare.1), calls=%async_computation | async-start | bytes 1048576 | tf_op jit(solution)/shard_map/all_to_all | solution.py:701
  9.9 2.1 %shard_map.95 = (f32[20,64,128]{2,1,0:T(8,128)S(1)}, s32[20,64,128]{2,1,0:T(8,128)S(1)}, f32[20,64,128]{2,1,0:T(8,128)S(1)}, f32[3,20,128]{2,1,0:T(8,128)S(1)}, ...) custom-call(f32[20,64,128]{2,1,0:T(8,128)} %h_hbm.3, s32[20,64,128]{2,1,0:T(8,128)} %soil_hbm.1, f32[20,64,128]{2,1,0:T(8,128)} %ks_hbm.1), custom_call_target="tpu_custom_call" | custom-call | tf_op jit(solution)/shard_map/pallas_call | solution.py:710
  12.0 0.0 copy-start
  12.0 0.3 collective-permute-start.3
  12.3 3.0 %collective-permute-start.2 = (f32[64,128]{1,0:T(8,128)S(1)}, f32[64,128]{1,0:T(8,128)S(1)}, u32[]{:S(2)}, u32[]{:S(2)}) collective-permute-start(f32[64,128]{1,0:T(8,128)S(1)} %get-tuple-element.58.own_ref), channel_id=1, source_target_pairs={{0,1},{1,0},{2,3},{3,2},{4,5},{5,4},{6,7},{7,6},{8,9},{9,8},{10,11... | collective-permute-start | bytes 98312 | tf_op jit(solution)/shard_map/ppermute | solution.py:630
  15.3 0.0 collective-permute-start
  15.3 1.6 %collective-permute-start.1 = (f32[3,20,128]{2,1,0:T(8,128)S(1)}, f32[3,20,128]{2,1,0:T(8,128)S(1)}, u32[]{:S(2)}, u32[]{:S(2)}) collective-permute-start(f32[3,20,128]{2,1,0:T(8,128)S(1)} %get-tuple-element.54.own_odd_ref), channel_id=1, source_target_pairs={{0,24},{1,25},{2,26},{3,27},{4,28},{5,29},{6,30},{7,31},{8,16},{9,... | collective-permute-start | bytes 92168 | tf_op jit(solution)/shard_map/ppermute | solution.py:630
  16.9 0.0 copy-done
  16.9 2.8 %shard_map.96 = (f32[20,64,128]{2,1,0:T(8,128)}, f32[20,64,128]{2,1,0:T(8,128)}, f32[20,64,128]{2,1,0:T(8,128)}, f32[20,64,128]{2,1,0:T(8,128)}, f32[20,64,128]{...) custom-call(f32[20,64,128]{2,1,0:T(8,128)S(1)} %get-tuple-element.41, ...), custom_call_target="tpu_custom_call" | custom-call | flops 8000000 | bytes 8000000 | tf_op jit(solution)/shard_map/pallas_call | solution.py:719
  19.6 0.0 collective-permute-done.row_even_ref
  19.7 0.0 collective-permute-done.1.row_odd_ref
  19.7 0.9 %shard_map.97 = (f32[20,64,128]{2,1,0:T(8,128)S(1)}, f32[20,64,128]{2,1,0:T(8,128)S(1)}, f32[20,64,128]{2,1,0:T(8,128)S(1)}, f32[2,4,20,128]{3,2,1,0:T(8,128)S(1)}) custom-call(f32[20,64,128]{2,1,0:T(8,128)S(1)} %get-tuple-element.41.h_ref, f32[20,64,128]{2,1,0:T(8,128)S(1)} %get-tuple-element.51.cond_ref, f32[20,64,128]{2,1,0:T(8,128)S(1)} %get-tuple-element.52.stor_ref, ...), custom_call_target="tpu_custom_call" | custom-call | flops 4000000 | bytes 4000000 | tf_op jit(solution)/shard_map/pallas_call | solution.py:727
  20.5 0.0 collective-permute-done.3.lane_odd_ref
  20.5 0.0 collective-permute-done.2.lane_even_ref
  20.6 5.6 %all-to-all-done.slots_ref = f32[32,16,256]{2,1,0:T(8,128)S(1)} async-done(((f32[32,16,256]{2,1,0:T(8,128)}), f32[32,16,256]{2,1,0:T(8,128)S(1)}, u32[]{:S(2)}, u32[]{:S(2)}) %all-to-all-start) | async-done | bytes 524320 | tf_op jit(solution)/shard_map/all_to_all | solution.py:701
  26.1 6.6 %shard_map.98 = (f32[20,64,128]{2,1,0:T(8,128)S(1)}, f32[14,64,128]{2,1,0:T(8,128)S(1)}, f32[64,128]{1,0:T(8,128)S(1)}, f32[1,20,128]{2,1,0:T(8,128)S(1)}, f32[1...) custom-call(f32[32,16,256]{2,1,0:T(8,128)S(1)} %all-to-all-done.slot, ...), custom_call_target="tpu_custom_call" | custom-call | tf_op jit(solution)/shard_map/pallas_call | solution.py:743
  32.8 0.1 collective-permute-start.7
  32.8 2.2 %collective-permute-start.6 = (f32[64,128]{1,0:T(8,128)S(1)}, f32[64,128]{1,0:T(8,128)S(1)}, u32[]{:S(2)}, u32[]{:S(2)}) collective-permute-start(f32[64,128]{1,0:T(8,128)S(1)} %get-tuple-element.77.own_ref), channel_id=1, source_target_pairs={{0,1},{1,0},{2,3},{3,2},{4,5},{5,4},{6,7},{7,6},{8,9},{9,8},{10,11... | collective-permute-start | bytes 98312 | tf_op jit(solution)/shard_map/ppermute | solution.py:630
  35.1 0.0 collective-permute-start.4
  35.1 0.7 %collective-permute-start.5 = (f32[1,20,128]{2,1,0:T(8,128)S(1)}, f32[1,20,128]{2,1,0:T(8,128)S(1)}, u32[]{:S(2)}, u32[]{:S(2)}) collective-permute-start(f32[1,20,128]{2,1,0:T(8,128)S(1)} %get-tuple-element.76.own_odd_ref), channel_id=1, source_target_pairs={{0,24},{1,25},{2,26},{3,27},{4,28},{5,29},{6,30},{7,31},{8,16},{9,... | collective-permute-start | bytes 30728 | tf_op jit(solution)/shard_map/ppermute | solution.py:630
  35.7 1.5 %shard_map.99 = (f32[20,64,128]{2,1,0:T(8,128)S(1)}, f32[20,64,128]{2,1,0:T(8,128)S(1)}, f32[20,64,128]{2,1,0:T(8,128)S(1)}, f32[20,64,128]{2,1,0:T(8,128)S(1)}, f32[64,128]{1,0:T(8,128)S(1)}) custom-call(f32[20,64,128]{2,1,0:T(8,128)S(1)} %get-tuple-element.59.head_ref.old_head_ref, f32[14,64,128]{2,1,0:T(8,128)S(1)} %get-tuple-element.60.sink_ref, ...), custom_call_target="tpu_custom_call" | custom-call | flops 8000000 | bytes 8000000 | tf_op jit(solution)/shard_map/pallas_call | solution.py:755
  37.3 0.0 collective-permute-done.4.row_even_ref
  37.3 0.9 %collective-permute-done.5.row_odd_ref = f32[1,20,128]{2,1,0:T(8,128)S(1)} collective-permute-done((f32[1,20,128]{2,1,0:T(8,128)S(1)}, f32[1,20,128]{2,1,0:T(8,128)S(1)}, u32[]{:S(2)}, u32[]{:S(2)}) %collective-permute-start.5) | collective-permute-done | bytes 10272 | tf_op jit(solution)/shard_map/ppermute | solution.py:630
  38.2 0.0 collective-permute-done.7.lane_odd_ref
  38.2 0.0 collective-permute-done.6.lane_even_ref
  38.2 2.0 %shard_map.100 = (f32[20,64,128]{2,1,0:T(8,128)}, f32[32,1,256]{2,1,0:T(1,128)S(1)}) custom-call(f32[32,16,256]{2,1,0:T(8,128)S(1)} %all-to-all-done.slots_ref, f32[20,64,128]{2,1,0:T(8,128)S(1)} %get-tuple-element.59.head_ref.old_head_ref, f32[20,64,128]{2,1,0:T(8,128)S(1)} %get-tuple-element.68.cond_ref, f32[20,64,128]{2,1,0:T(8,128)S(1)} %get-tuple-element.69.old_res_ref, ...), custom_call_target="tpu_custom_call" | custom-call | tf_op jit(solution)/shard_map/pallas_call | solution.py:763
  40.2 10.0 %all_to_all.10 = f32[32,1,256]{2,1,0:T(1,128)S(1)} all-to-all(f32[32,1,256]{2,1,0:T(1,128)S(1)} %get-tuple-element.79), channel_id=1, replica_groups=mesh['bx'=4,'by'=8] {'bx','by'}, dimensions={0} | all-to-all | bytes 65536 | tf_op jit(solution)/shard_map/all_to_all | solution.py:773
  50.2 0.6 %copy.11 = f32[8192]{0:T(1024)} copy(f32[8192]{0:T(1024)S(1)} %bitcast.4) | data formatting | bytes 65536
  (1 shorter events, 0.0 us)
Async XLA Ops:
  2.6 23.6 %all-to-all-start = ((f32[32,16,256]{2,1,0:T(8,128)}), f32[32,16,256]{2,1,0:T(8,128)S(1)}, u32[]{:S(2)}, u32[]{:S(2)}) async-start(f32[32,16,256]{2,1,0:T(8,128)} %prepare.1), calls=%async_computation | async-start | bytes 1048576 | tf_op jit(solution)/shard_map/all_to_all | solution.py:701
  12.0 4.9 %copy-start = (f32[4,12]{1,0:T(4,128)S(1)}, f32[4,12]{1,0:T(4,128)}, u32[]{:S(2)}) copy-start(f32[4,12]{1,0:T(4,128)} %param.12) | copy-start | bytes 580
  12.0 8.6 %collective-permute-start.3 = (f32[64,128]{1,0:T(8,128)S(1)}, f32[64,128]{1,0:T(8,128)S(1)}, u32[]{:S(2)}, u32[]{:S(2)}) collective-permute-start(f32[64,128]{1,0:T(8,128)S(1)} %get-tuple-element.58.own_ref), channel_id=1, source_target_pairs={{0,8},{1,2},{2,1},{3,4},{4,3},{5,6},{6,5},{7,15},{8,0},{9,10},{10,... | collective-permute-start | bytes 98312 | tf_op jit(solution)/shard_map/ppermute | solution.py:630
  12.3 8.3 %collective-permute-start.2 = (f32[64,128]{1,0:T(8,128)S(1)}, f32[64,128]{1,0:T(8,128)S(1)}, u32[]{:S(2)}, u32[]{:S(2)}) collective-permute-start(f32[64,128]{1,0:T(8,128)S(1)} %get-tuple-element.58.own_ref), channel_id=1, source_target_pairs={{0,1},{1,0},{2,3},{3,2},{4,5},{5,4},{6,7},{7,6},{8,9},{9,8},{10,11... | collective-permute-start | bytes 98312 | tf_op jit(solution)/shard_map/ppermute | solution.py:630
  15.3 4.4 %collective-permute-start = (f32[3,20,128]{2,1,0:T(8,128)S(1)}, f32[3,20,128]{2,1,0:T(8,128)S(1)}, u32[]{:S(2)}, u32[]{:S(2)}) collective-permute-start(f32[3,20,128]{2,1,0:T(8,128)S(1)} %get-tuple-element.53.own_even_ref), channel_id=1, source_target_pairs={{0,8},{1,9},{2,10},{3,11},{4,12},{5,13},{6,14},{7,15},{8,0},{9,1},... | collective-permute-start | bytes 92168 | tf_op jit(solution)/shard_map/ppermute | solution.py:630
  15.3 4.4 %collective-permute-start.1 = (f32[3,20,128]{2,1,0:T(8,128)S(1)}, f32[3,20,128]{2,1,0:T(8,128)S(1)}, u32[]{:S(2)}, u32[]{:S(2)}) collective-permute-start(f32[3,20,128]{2,1,0:T(8,128)S(1)} %get-tuple-element.54.own_odd_ref), channel_id=1, source_target_pairs={{0,24},{1,25},{2,26},{3,27},{4,28},{5,29},{6,30},{7,31},{8,16},{9,... | collective-permute-start | bytes 92168 | tf_op jit(solution)/shard_map/ppermute | solution.py:630
  32.8 5.4 %collective-permute-start.7 = (f32[64,128]{1,0:T(8,128)S(1)}, f32[64,128]{1,0:T(8,128)S(1)}, u32[]{:S(2)}, u32[]{:S(2)}) collective-permute-start(f32[64,128]{1,0:T(8,128)S(1)} %get-tuple-element.77.own_ref), channel_id=1, source_target_pairs={{0,8},{1,2},{2,1},{3,4},{4,3},{5,6},{6,5},{7,15},{8,0},{9,10},{10,... | collective-permute-start | bytes 98312 | tf_op jit(solution)/shard_map/ppermute | solution.py:630
  32.8 5.3 %collective-permute-start.6 = (f32[64,128]{1,0:T(8,128)S(1)}, f32[64,128]{1,0:T(8,128)S(1)}, u32[]{:S(2)}, u32[]{:S(2)}) collective-permute-start(f32[64,128]{1,0:T(8,128)S(1)} %get-tuple-element.77.own_ref), channel_id=1, source_target_pairs={{0,1},{1,0},{2,3},{3,2},{4,5},{5,4},{6,7},{7,6},{8,9},{9,8},{10,11... | collective-permute-start | bytes 98312 | tf_op jit(solution)/shard_map/ppermute | solution.py:630
  35.1 2.2 %collective-permute-start.4 = (f32[1,20,128]{2,1,0:T(8,128)S(1)}, f32[1,20,128]{2,1,0:T(8,128)S(1)}, u32[]{:S(2)}, u32[]{:S(2)}) collective-permute-start(f32[1,20,128]{2,1,0:T(8,128)S(1)} %get-tuple-element.75.own_even_ref), channel_id=1, source_target_pairs={{0,8},{1,9},{2,10},{3,11},{4,12},{5,13},{6,14},{7,15},{8,0},{9,1},... | collective-permute-start | bytes 30728 | tf_op jit(solution)/shard_map/ppermute | solution.py:630
  35.1 3.1 %collective-permute-start.5 = (f32[1,20,128]{2,1,0:T(8,128)S(1)}, f32[1,20,128]{2,1,0:T(8,128)S(1)}, u32[]{:S(2)}, u32[]{:S(2)}) collective-permute-start(f32[1,20,128]{2,1,0:T(8,128)S(1)} %get-tuple-element.76.own_odd_ref), channel_id=1, source_target_pairs={{0,24},{1,25},{2,26},{3,27},{4,28},{5,29},{6,30},{7,31},{8,16},{9,... | collective-permute-start | bytes 30728 | tf_op jit(solution)/shard_map/ppermute | solution.py:630
